TPU v7x, 32 devices: a whole 2x2x4 slice. The times are simulated.
32 devices in a mesh: seq: 2 (over y), ctx: 4 (over z), tp: 4 (over x, core).
Axes of the slice: x: 2, y: 2, z: 4, core: 2. Of those that a mesh axis runs over, the one named last changes fastest.
Arguments:
- tokens: bfloat16 [2048, 2048], P(('seq', 'ctx')), may hold values from -6 to 6
- query_weight: bfloat16 [2048, 2048], P(('seq', 'ctx'), 'tp'), may hold values from -0.125 to 0.125
- key_weight: bfloat16 [2048, 2048], P(('seq', 'ctx'), 'tp'), may hold values from -0.125 to 0.125
- value_weight: bfloat16 [2048, 2048], P(('seq', 'ctx'), 'tp'), may hold values from -0.125 to 0.125
- output_weight: bfloat16 [2048, 2048], P('tp', ('seq', 'ctx')), may hold values from -1.5 to 1.5
- gate_weight: bfloat16 [2048, 8192], P(('seq', 'ctx'), 'tp'), may hold values from -0.125 to 0.125
- up_weight: bfloat16 [2048, 8192], P(('seq', 'ctx'), 'tp'), may hold values from -0.125 to 0.125
- down_weight: bfloat16 [8192, 2048], P('tp', ('seq', 'ctx')), may hold values from -0.0625 to 0.0625
- attention_gain: bfloat16 [2048], P(('seq', 'ctx')), may hold values from 0.25 to 1.75
- feedforward_gain: bfloat16 [2048], P(('seq', 'ctx')), may hold values from 0.25 to 1.75
- order: int32 [8], replicated, may hold values from 0 to 7, each once
- cotangent: bfloat16 [2048, 2048], P(('seq', 'ctx')), may hold values from -6 to 6
Outputs:
- block_output: bfloat16 [2048, 2048], P(('seq', 'ctx'))
- input_grad: float32 [2048, 2048], P(('seq', 'ctx'))
- query_weight_grad: float32 [2048, 2048], P(('seq', 'ctx'), 'tp')
- key_weight_grad: float32 [2048, 2048], P(('seq', 'ctx'), 'tp')
- value_weight_grad: float32 [2048, 2048], P(('seq', 'ctx'), 'tp')
- output_weight_grad: float32 [2048, 2048], P('tp', ('seq', 'ctx'))
- gate_weight_grad: float32 [2048, 8192], P(('seq', 'ctx'), 'tp')
- up_weight_grad: float32 [2048, 8192], P(('seq', 'ctx'), 'tp')
- down_weight_grad: float32 [8192, 2048], P('tp', ('seq', 'ctx'))
- attention_gain_grad: float32 [2048], P(('seq', 'ctx'))
- feedforward_gain_grad: float32 [2048], P(('seq', 'ctx'))
Inputs may be any that keep to these rules, and one draw needn't show every extreme that they name: order holds every block position of a sequence once; the device of ctx index c stores blocks 2c and 2c + 1 of each sequence.
All inputs are finite; a program needn't handle non-finite values.
Results may differ from a plain program's by a relative error of at most 0.02.
Values may be sent and summed in bfloat16 or wider, within the bound.
No kernel may reach another device: no remote copies, remote signals or barrier semaphores. Data moves between devices by JAX's collectives and lax.ppermute only.
A program may use at most 128 MiB of HBM per device.

v0:
```python
from functools import partial

import jax
import jax.numpy as jnp
from jax import lax
from jax.sharding import PartitionSpec as P

HD = 64
BLOCK = 128


THETA = 130000.0
EPS = 1e-05


def shifted(block, axis, distance):
    devices = range(lax.axis_size(axis))
    route = [((i - distance) % len(devices), i) for i in devices]
    return lax.ppermute(block, axis, route)


def rms_norm(hidden, gain):
    return hidden * lax.rsqrt(jnp.mean(hidden * hidden, axis=-1, keepdims=True) + EPS) * gain


def rotary(values, places):
    row_count = values.shape[0]
    by_heads = values.reshape(row_count, -1, HD)
    halfway = HD // 2
    inverse = THETA ** (-(jnp.arange(halfway, dtype=jnp.float32) * 2.0) / HD)
    angle = places.astype(jnp.float32)[:, None] * inverse[None, :]
    angle = jnp.concatenate([angle, angle], axis=1)
    cosine = jnp.cos(angle)[:, None, :]
    sine = jnp.sin(angle)[:, None, :]
    turned = jnp.concatenate([-by_heads[..., halfway:], by_heads[..., :halfway]], axis=-1)
    return (by_heads * cosine + turned * sine).reshape(row_count, -1)


def gated(gate, upward):
    return jax.nn.silu(gate) * upward


def product(left, right):
    return jnp.dot(left, right, preferred_element_type=jnp.float32)


def contract_rows(left, right):
    return lax.dot_general(
        left, right, (((0,), (0,)), ((), ())), preferred_element_type=jnp.float32
    )


def contract_cols(left, right):
    return lax.dot_general(
        left, right, (((1,), (1,)), ((), ())), preferred_element_type=jnp.float32
    )


def key_places(order, first_row, row_total):
    stored = first_row + jnp.arange(row_total, dtype=jnp.int32)
    group_slot = stored // BLOCK
    slot_table = jnp.arange(order.shape[0], dtype=jnp.int32)
    block_place = jnp.sum(
        jnp.where(group_slot[:, None] == slot_table[None, :], order[None, :], 0), axis=1
    )
    return block_place * BLOCK + stored % BLOCK


def exp_scores(query_heads, query_places, key_rows, key_pos):
    row_total = key_rows.shape[0]
    key_heads = key_rows.reshape(row_total, -1, HD)
    scores = (
        jnp.einsum("qhd,khd->hqk", query_heads, key_heads, preferred_element_type=jnp.float32)
        * 0.125
    )
    allowed = query_places[:, None] >= key_pos[None, :]
    return (jnp.where(allowed[None], jnp.exp(scores), 0.0), key_heads)


def per_device(
    tokens,
    query_weight,
    key_weight,
    value_weight,
    output_weight,
    gate_weight,
    up_weight,
    down_weight,
    attention_gain,
    feedforward_gain,
    order,
    cotangent,
):
    rows_local = tokens.shape[0]
    ctx_index = lax.axis_index("ctx")
    ctx_total = lax.axis_size("ctx")
    gathered = (
        lax.all_gather(query_weight, ("seq", "ctx"), axis=0, tiled=True),
        lax.all_gather(key_weight, ("seq", "ctx"), axis=0, tiled=True),
        lax.all_gather(value_weight, ("seq", "ctx"), axis=0, tiled=True),
        lax.all_gather(output_weight, ("seq", "ctx"), axis=1, tiled=True),
        lax.all_gather(gate_weight, ("seq", "ctx"), axis=0, tiled=True),
        lax.all_gather(up_weight, ("seq", "ctx"), axis=0, tiled=True),
        lax.all_gather(down_weight, ("seq", "ctx"), axis=1, tiled=True),
        lax.all_gather(attention_gain, ("seq", "ctx"), axis=0, tiled=True),
        lax.all_gather(feedforward_gain, ("seq", "ctx"), axis=0, tiled=True),
    )
    (
        full_query,
        full_key,
        full_value,
        full_output,
        full_gate,
        full_up,
        full_down,
        gain_first,
        gain_second,
    ) = gathered
    inputs = tokens.astype(jnp.float32)
    query_places = key_places(order, ctx_index * rows_local, rows_local)
    normed_value, norm_back_first = jax.vjp(rms_norm, inputs, gain_first.astype(jnp.float32))
    normed = normed_value.astype(jnp.bfloat16)
    rope_here = partial(rotary, places=query_places)
    query_rot, query_back = jax.vjp(rope_here, product(normed, full_query))
    key_rot, key_back = jax.vjp(rope_here, product(normed, full_key))
    value_rows = product(normed, full_value).astype(jnp.bfloat16)
    query_rows = query_rot.astype(jnp.bfloat16)
    key_rows = key_rot.astype(jnp.bfloat16)
    width = query_rows.shape[1]
    head_count = width // HD
    query_heads = query_rows.reshape(rows_local, head_count, HD)
    packed = jnp.stack([key_rows, value_rows])
    empty_totals = jnp.zeros((rows_local, head_count), jnp.float32)
    empty_numerator = jnp.zeros((rows_local, width), jnp.float32)
    arrived = lax.all_gather(packed, "ctx", axis=1, tiled=True)
    row_total = arrived.shape[1]

    def one_block(block_index, partial_state):
        first_row = block_index * rows_local
        section = lax.dynamic_slice_in_dim(arrived, first_row, rows_local, 1)
        key_pos = key_places(order, first_row, rows_local)
        weights, key_heads = exp_scores(query_heads, query_places, section[0], key_pos)
        value_heads = section[1].reshape(rows_local, -1, HD)
        totals, numerator = partial_state
        totals = totals + jnp.sum(weights, axis=2).T
        numerator = numerator + jnp.einsum(
            "hqk,khd->qhd",
            weights.astype(jnp.bfloat16),
            value_heads,
            preferred_element_type=jnp.float32,
        ).reshape(rows_local, width)
        return (totals, numerator)

    totals, numerator = lax.fori_loop(
        0, row_total // rows_local, one_block, (empty_totals, empty_numerator)
    )
    numerator_heads = numerator.reshape(rows_local, head_count, HD)
    mixed = (numerator_heads / totals[:, :, None]).astype(jnp.bfloat16).reshape(rows_local, width)
    middle = inputs + lax.psum(product(mixed, full_output), "tp")
    normed_two_value, norm_back_second = jax.vjp(rms_norm, middle, gain_second.astype(jnp.float32))
    normed_two = normed_two_value.astype(jnp.bfloat16)
    activated, gated_back = jax.vjp(
        gated, product(normed_two, full_gate), product(normed_two, full_up)
    )
    hidden = activated.astype(jnp.bfloat16)
    block_output = middle + lax.psum(product(hidden, full_down).astype(jnp.bfloat16), "tp").astype(
        jnp.float32
    )
    back_weights = (
        lax.all_gather(query_weight, ("seq", "ctx"), axis=0, tiled=True),
        lax.all_gather(key_weight, ("seq", "ctx"), axis=0, tiled=True),
        lax.all_gather(value_weight, ("seq", "ctx"), axis=0, tiled=True),
        lax.all_gather(output_weight, ("seq", "ctx"), axis=1, tiled=True),
        lax.all_gather(gate_weight, ("seq", "ctx"), axis=0, tiled=True),
        lax.all_gather(up_weight, ("seq", "ctx"), axis=0, tiled=True),
        lax.all_gather(down_weight, ("seq", "ctx"), axis=1, tiled=True),
        lax.all_gather(attention_gain, ("seq", "ctx"), axis=0, tiled=True),
        lax.all_gather(feedforward_gain, ("seq", "ctx"), axis=0, tiled=True),
    )
    (
        back_query,
        back_key,
        back_value,
        back_output,
        back_gate,
        back_up,
        back_down,
        gain_unused,
        gain_spare,
    ) = back_weights
    down_grad = contract_rows(hidden, cotangent)
    hidden_grad = contract_cols(cotangent, back_down)
    gate_grad, upward_grad = gated_back(hidden_grad)
    gate_grad = gate_grad.astype(jnp.bfloat16)
    upward_grad = upward_grad.astype(jnp.bfloat16)
    gate_wgrad = contract_rows(normed_two, gate_grad)
    upward_wgrad = contract_rows(normed_two, upward_grad)
    normed_two_grad = lax.psum(
        contract_cols(gate_grad, back_gate) + contract_cols(upward_grad, back_up), "tp"
    )
    middle_norm_grad, second_gain_grad = norm_back_second(normed_two_grad)
    middle_grad = cotangent.astype(jnp.float32) + middle_norm_grad
    branch_grad = middle_grad.astype(jnp.bfloat16)
    output_wgrad = contract_rows(mixed, branch_grad)
    mixed_grad = contract_cols(branch_grad, back_output).reshape(rows_local, head_count, HD)
    numerator_grad = (mixed_grad / totals[:, :, None]).astype(jnp.bfloat16)
    totals_grad = -jnp.sum(mixed_grad * numerator_heads, axis=2) / (totals * totals)
    totals_grad_heads = totals_grad.T[:, :, None]

    def visit(turn_index, state):
        visiting, carried, query_acc = state
        source = (ctx_index - turn_index) % ctx_total
        key_pos = key_places(order, source * rows_local, rows_local)
        weights, key_heads = exp_scores(query_heads, query_places, visiting[0], key_pos)
        value_heads = visiting[1].reshape(rows_local, -1, HD)
        through = jnp.einsum(
            "qhd,khd->hqk", numerator_grad, value_heads, preferred_element_type=jnp.float32
        )
        slopes = (weights * (through + totals_grad_heads)).astype(jnp.bfloat16)
        query_acc = (
            query_acc
            + jnp.einsum("hqk,khd->qhd", slopes, key_heads, preferred_element_type=jnp.float32)
            * 0.125
        )
        key_term = (
            jnp.einsum("hqk,qhd->khd", slopes, query_heads, preferred_element_type=jnp.float32)
            * 0.125
        )
        value_term = jnp.einsum(
            "hqk,qhd->khd",
            weights.astype(jnp.bfloat16),
            numerator_grad,
            preferred_element_type=jnp.float32,
        )
        carried = carried + jnp.stack(
            [key_term.reshape(rows_local, width), value_term.reshape(rows_local, width)]
        )
        visiting = shifted(visiting, "ctx", 1)
        carried = shifted(carried, "ctx", 1)
        return (visiting, carried, query_acc)

    start_state = (
        packed,
        jnp.zeros((2, rows_local, width), jnp.float32),
        jnp.zeros((rows_local, head_count, HD), jnp.float32),
    )
    ended, key_value_grad, query_acc = lax.fori_loop(0, ctx_total, visit, start_state)
    query_proj_grad = query_back(query_acc.reshape(rows_local, width))[0].astype(jnp.bfloat16)
    key_proj_grad = key_back(key_value_grad[0])[0].astype(jnp.bfloat16)
    value_grad = key_value_grad[1].astype(jnp.bfloat16)
    query_wgrad = contract_rows(normed, query_proj_grad)
    key_wgrad = contract_rows(normed, key_proj_grad)
    value_wgrad = contract_rows(normed, value_grad)
    normed_grad = lax.psum(
        (
            contract_cols(query_proj_grad, back_query)
            + contract_cols(key_proj_grad, back_key)
            + contract_cols(value_grad, back_value)
        ).astype(jnp.bfloat16),
        "tp",
    ).astype(jnp.float32)
    input_norm_grad, first_gain_grad = norm_back_first(normed_grad)
    input_grad = middle_grad + input_norm_grad
    scattered = (
        lax.psum_scatter(
            query_wgrad.astype(jnp.bfloat16), ("seq", "ctx"), scatter_dimension=0, tiled=True
        ).astype(jnp.float32),
        lax.psum_scatter(
            key_wgrad.astype(jnp.bfloat16), ("seq", "ctx"), scatter_dimension=0, tiled=True
        ).astype(jnp.float32),
        lax.psum_scatter(
            value_wgrad.astype(jnp.bfloat16), ("seq", "ctx"), scatter_dimension=0, tiled=True
        ).astype(jnp.float32),
        lax.psum_scatter(
            output_wgrad.astype(jnp.bfloat16), ("seq", "ctx"), scatter_dimension=1, tiled=True
        ).astype(jnp.float32),
        lax.psum_scatter(
            gate_wgrad.astype(jnp.bfloat16), ("seq", "ctx"), scatter_dimension=0, tiled=True
        ).astype(jnp.float32),
        lax.psum_scatter(
            upward_wgrad.astype(jnp.bfloat16), ("seq", "ctx"), scatter_dimension=0, tiled=True
        ).astype(jnp.float32),
        lax.psum_scatter(
            down_grad.astype(jnp.bfloat16), ("seq", "ctx"), scatter_dimension=1, tiled=True
        ).astype(jnp.float32),
        lax.psum_scatter(
            first_gain_grad.astype(jnp.bfloat16), ("seq", "ctx"), scatter_dimension=0, tiled=True
        ).astype(jnp.float32),
        lax.psum_scatter(
            second_gain_grad.astype(jnp.bfloat16), ("seq", "ctx"), scatter_dimension=0, tiled=True
        ).astype(jnp.float32),
    )
    return (
        block_output.astype(jnp.bfloat16),
        input_grad,
        scattered[0],
        scattered[1],
        scattered[2],
        scattered[3],
        scattered[4],
        scattered[5],
        scattered[6],
        scattered[7],
        scattered[8],
    )


def solution(mesh):
    placed = (
        P(("seq", "ctx"), None),
        P(("seq", "ctx"), "tp"),
        P(("seq", "ctx"), "tp"),
        P(("seq", "ctx"), "tp"),
        P("tp", ("seq", "ctx")),
        P(("seq", "ctx"), "tp"),
        P(("seq", "ctx"), "tp"),
        P("tp", ("seq", "ctx")),
        P(("seq", "ctx")),
        P(("seq", "ctx")),
        P(),
        P(("seq", "ctx"), None),
    )
    return jax.shard_map(
        per_device,
        mesh=mesh,
        in_specs=placed,
        out_specs=(
            P(("seq", "ctx"), None),
            P(("seq", "ctx"), None),
            P(("seq", "ctx"), "tp"),
            P(("seq", "ctx"), "tp"),
            P(("seq", "ctx"), "tp"),
            P("tp", ("seq", "ctx")),
            P(("seq", "ctx"), "tp"),
            P(("seq", "ctx"), "tp"),
            P("tp", ("seq", "ctx")),
            P(("seq", "ctx")),
            P(("seq", "ctx")),
        ),
        check_vma=False,
    )
```

profile of v0, /device:TPU:0, one launch (start us, length us, event | category | flops | bytes accessed | tf_op | source)
XLA Modules:
  0.0 1750.3 jit_solution(15163281541108414726)
XLA Ops:
  10.1 22.3 %all-gather = bf16[8,1,256]{2,1,0:T(2,128)(2,1)S(1)} all-gather(bf16[1,1,256]{2,1,0:T(2,128)(2,1)S(1)} %reshape.359), channel_id=1, replica_groups=mesh['seq'=2,'ctx'=4,'tp'=4] {'seq','ctx'}, dimensions={0}, use_global_device_ids=true | all-gather | bytes 4608 | tf_op jit(solution)/shard_map/all_gather | solution.py:105
  34.6 27.6 %all-gather.11.cloned.1.call-done = bf16[2048,512]{1,0:T(8,128)(2,1)} async-done(((bf16[256,512]{1,0:T(8,128)(2,1)}), bf16[2048,512]{1,0:T(8,128)(2,1)}) %all-gather.11.cloned.1.call-update) | async-done | bytes 2097168 | tf_op jit(solution)/shard_map/all_gather | solution.py:99
  62.2 2.3 fusion.57
  64.7 47.4 %all-gather.17.cloned.1.call-done = bf16[2048,512]{1,0:T(8,128)(2,1)} async-done(((bf16[256,512]{1,0:T(8,128)(2,1)}), bf16[2048,512]{1,0:T(8,128)(2,1)}) %all-gather.17.cloned.1.call-update) | async-done | bytes 2097168 | tf_op jit(solution)/shard_map/all_gather | solution.py:98
  112.1 2.3 fusion.54
  118.9 2.1 copy.65
  121.0 2.1 add_convert_fusion.3
  123.1 39.0 %all-gather.13.cloned.1.call-done = bf16[2048,512]{1,0:T(8,128)(2,1)} async-done(((bf16[256,512]{1,0:T(8,128)(2,1)}), bf16[2048,512]{1,0:T(8,128)(2,1)}) %all-gather.13.cloned.1.call-update) | async-done | bytes 2097168 | tf_op jit(solution)/shard_map/all_gather | solution.py:100
  162.1 2.3 fusion.36
  166.1 43.8 %all-gather.15.cloned.1.call-done = bf16[2,1024,512]{2,1,0:T(8,128)(2,1)} async-done(((bf16[2,256,512]{2,1,0:T(8,128)(2,1)}), bf16[2,1024,512]{2,1,0:T(8,128)(2,1)}) %all-gather.15.cloned.1.call-update) | async-done | bytes 2097168 | tf_op jit(solution)/shard_map/all_gather | solution.py:135
  209.9 22.9 %while.39 = (s32[]{:T(128)}, f32[256,8]{0,1:T(8,128)S(1)}, f32[256,512]{0,1:T(8,128)}, s32[256]{0:T(256)}, s32[8]{0:T(128)}, /*index=5*/bf16[2,1024,512]{2,1,0:T...) while((s32[]{:T(128)}, f32[256,8]{0,1:T(8,128)S(1)}, ...), condition=%wide.region_5.6_spmd.clone, body=%wide.region_2.5_spmd.clone.sunk | while | flops 137706752 | bytes 9411818 | solution.py:154
  218.9 1.9 bitcast_add_fusion.5
  224.8 1.9 bitcast_add_fusion.5
  230.8 1.9 bitcast_add_fusion.5
  233.8 27.7 %all-gather.19.cloned.1.call-done = bf16[512,2048]{1,0:T(8,128)(2,1)} async-done(((bf16[512,256]{1,0:T(8,128)(2,1)}), bf16[512,2048]{1,0:T(8,128)(2,1)}) %all-gather.19.cloned.1.call-update) | async-done | bytes 2097168 | tf_op jit(solution)/shard_map/all_gather | solution.py:101
  261.5 3.6 fusion.65
  267.5 17.9 %all-gather.1 = bf16[8,1,256]{2,1,0:T(2,128)(2,1)S(1)} all-gather(bf16[1,1,256]{2,1,0:T(2,128)(2,1)S(1)} %reshape.361), channel_id=1, replica_groups=mesh['seq'=2,'ctx'=4,'tp'=4] {'seq','ctx'}, dimensions={0}, use_global_device_ids=true | all-gather | bytes 4608 | tf_op jit(solution)/shard_map/all_gather | solution.py:106
  286.0 28.9 %all-reduce.12.cloned.1.call-done = f32[256,2048]{1,0:T(8,128)} async-done(((f32[256,2048]{1,0:T(8,128)}), f32[256,2048]{1,0:T(8,128)}) %all-reduce.12.cloned.1.call-update) | async-done | bytes 2097168 | tf_op jit(solution)/shard_map/psum | solution.py:159
  314.9 2.0 multiply_reduce_fusion.2
  317.8 124.5 %all-gather.21.cloned.1.call-done = bf16[2048,2048]{1,0:T(8,128)(2,1)} async-done(((bf16[256,2048]{1,0:T(8,128)(2,1)}), bf16[2048,2048]{1,0:T(8,128)(2,1)}) %all-gather.21.cloned.1.call-update) | async-done | bytes 8388624 | tf_op jit(solution)/shard_map/all_gather | solution.py:102
  442.3 7.0 fusion.66
  449.4 118.5 %all-gather.23.cloned.1.call-done = bf16[2048,2048]{1,0:T(8,128)(2,1)} async-done(((bf16[256,2048]{1,0:T(8,128)(2,1)}), bf16[2048,2048]{1,0:T(8,128)(2,1)}) %all-gather.23.cloned.1.call-update) | async-done | bytes 8388624 | tf_op jit(solution)/shard_map/all_gather | solution.py:103
  567.8 7.0 fusion.67
  574.9 118.8 %all-gather.25.cloned.1.call-done = bf16[2048,2048]{1,0:T(8,128)(2,1)} async-done(((bf16[2048,256]{1,0:T(8,128)(2,1)}), bf16[2048,2048]{1,0:T(8,128)(2,1)}) %all-gather.25.cloned.1.call-update) | async-done | bytes 8388624 | tf_op jit(solution)/shard_map/all_gather | solution.py:104
  693.6 9.0 multiply_convert_fusion.1
  702.6 6.6 fusion.68
  709.2 3.7 convolution_add_fusion.2
  715.0 7.4 convolution_convert_fusion.7
  722.4 40.2 %all-reduce.14.cloned.1.call-done = f32[256,2048]{1,0:T(8,128)} async-done(((f32[256,2048]{1,0:T(8,128)}), f32[256,2048]{1,0:T(8,128)}) %all-reduce.14.cloned.1.call-update) | async-done | bytes 2097168 | tf_op jit(solution)/shard_map/psum | solution.py:198
  762.7 2.8 multiply_reduce_fusion
  768.8 173.2 %while.40 = (s32[]{:T(128)}, bf16[2,256,512]{1,2,0:T(8,128)(2,1)}, f32[2,256,512]{1,2,0:T(8,128)S(1)}, f32[256,8,64]{0,2,1:T(8,128)}, s32[256]{0:T(256)}, /*inde...) while((s32[]{:T(128)}, bf16[2,256,512]{1,2,0:T(8,128)(2,1)}, ...), condition=%wide.region_14.15_spmd.clone, body=%wide.region_12.14_spmd.clone.sunk | while | flops 340866304 | bytes 25116048 | solution.py:247
  779.6 34.0 %collective-permute-done = bf16[2,256,512]{1,2,0:T(8,128)(2,1)} collective-permute-done((bf16[2,256,512]{1,2,0:T(8,128)(2,1)S(1)}, bf16[2,256,512]{1,2,0:T(8,128)(2,1)}, u32[]{:S(2)}, u32[]{:S(2)}) %collective-permute-start) | collective-permute-done | bytes 524320 | tf_op jit(solution)/shard_map/while/body/eval_jaxpr/ppermute | solution.py:19
  821.2 2.3 fusion.157
  823.5 33.8 %collective-permute-done = bf16[2,256,512]{1,2,0:T(8,128)(2,1)} collective-permute-done((bf16[2,256,512]{1,2,0:T(8,128)(2,1)S(1)}, bf16[2,256,512]{1,2,0:T(8,128)(2,1)}, u32[]{:S(2)}, u32[]{:S(2)}) %collective-permute-start) | collective-permute-done | bytes 524320 | tf_op jit(solution)/shard_map/while/body/eval_jaxpr/ppermute | solution.py:19
  863.8 2.3 fusion.157
  866.1 34.1 %collective-permute-done = bf16[2,256,512]{1,2,0:T(8,128)(2,1)} collective-permute-done((bf16[2,256,512]{1,2,0:T(8,128)(2,1)S(1)}, bf16[2,256,512]{1,2,0:T(8,128)(2,1)}, u32[]{:S(2)}, u32[]{:S(2)}) %collective-permute-start) | collective-permute-done | bytes 524320 | tf_op jit(solution)/shard_map/while/body/eval_jaxpr/ppermute | solution.py:19
  906.6 2.3 fusion.157
  908.9 33.2 %collective-permute-done = bf16[2,256,512]{1,2,0:T(8,128)(2,1)} collective-permute-done((bf16[2,256,512]{1,2,0:T(8,128)(2,1)S(1)}, bf16[2,256,512]{1,2,0:T(8,128)(2,1)}, u32[]{:S(2)}, u32[]{:S(2)}) %collective-permute-start) | collective-permute-done | bytes 524320 | tf_op jit(solution)/shard_map/while/body/eval_jaxpr/ppermute | solution.py:19
  950.8 3.6 convolution_convert_fusion.3
  955.7 2.2 convolution_convert_fusion.6
  958.0 2.3 convolution_convert_fusion.5
  960.6 2.2 convolution_convert_fusion.4
  964.0 5.7 convolution_convert_fusion.2
  970.9 5.7 convolution_convert_fusion.1
  978.1 5.7 convolution_convert_fusion
  985.7 13.8 all-reduce.16.cloned.1.call-done
  999.5 2.3 fusion.27
  1001.8 22.1 %all-reduce.6 = (bf16[2048]{0:T(1024)(128)(2,1)S(1)}, bf16[2048]{0:T(1024)(128)(2,1)S(1)}) all-reduce(bf16[2048]{0:T(1024)(128)(2,1)S(1)} %get-tuple-element.603, bf16[2048]{0:T(1024)(128)(2,1)S(1)} %copy-done.34), channel_id=9, replica_groups=mesh['seq'=2,'ctx'=4,'tp'=4] {'seq','ctx'}, use_global_device_ids=true, to_apply=%region_25.26.clone | all-reduce | flops 4096 | bytes 16384
  1025.2 2.7 add_convert_fusion
  1027.9 1.9 fusion.32
  1029.8 42.1 %reduce-scatter.14.cloned.1.call-done = bf16[512,256]{1,0:T(8,128)(2,1)} async-done(((bf16[512,2048]{1,0:T(8,128)(2,1)}), bf16[512,256]{1,0:T(8,128)(2,1)}) %reduce-scatter.14.cloned.1.call-update) | async-done | bytes 262160 | tf_op jit(solution)/shard_map/reduce_scatter | solution.py:274
  1071.9 1.8 convert_element_type.204
  1073.7 69.6 %reduce-scatter.8.cloned.1.call-done = bf16[256,512]{1,0:T(8,128)(2,1)} async-done(((bf16[2048,512]{1,0:T(8,128)(2,1)}), bf16[256,512]{1,0:T(8,128)(2,1)}) %reduce-scatter.8.cloned.1.call-update) | async-done | bytes 262160 | tf_op jit(solution)/shard_map/reduce_scatter | solution.py:265
  1143.3 1.8 convert_element_type.198
  1145.1 68.6 %reduce-scatter.10.cloned.1.call-done = bf16[256,512]{1,0:T(8,128)(2,1)} async-done(((bf16[2048,512]{1,0:T(8,128)(2,1)}), bf16[256,512]{1,0:T(8,128)(2,1)}) %reduce-scatter.10.cloned.1.call-update) | async-done | bytes 262160 | tf_op jit(solution)/shard_map/reduce_scatter | solution.py:268
  1213.7 1.8 convert_element_type.200
  1215.5 68.9 %reduce-scatter.12.cloned.1.call-done = bf16[256,512]{1,0:T(8,128)(2,1)} async-done(((bf16[2048,512]{1,0:T(8,128)(2,1)}), bf16[256,512]{1,0:T(8,128)(2,1)}) %reduce-scatter.12.cloned.1.call-update) | async-done | bytes 262160 | tf_op jit(solution)/shard_map/reduce_scatter | solution.py:271
  1284.4 1.8 convert_element_type.202
  1286.2 150.2 %reduce-scatter.16.cloned.1.call-done = bf16[256,2048]{1,0:T(8,128)(2,1)} async-done(((bf16[2048,2048]{1,0:T(8,128)(2,1)}), bf16[256,2048]{1,0:T(8,128)(2,1)}) %reduce-scatter.16.cloned.1.call-update) | async-done | bytes 1048592 | tf_op jit(solution)/shard_map/reduce_scatter | solution.py:277
  1436.4 2.8 convert_element_type.206
  1439.2 148.8 %reduce-scatter.18.cloned.1.call-done = bf16[256,2048]{1,0:T(8,128)(2,1)} async-done(((bf16[2048,2048]{1,0:T(8,128)(2,1)}), bf16[256,2048]{1,0:T(8,128)(2,1)}) %reduce-scatter.18.cloned.1.call-update) | async-done | bytes 1048592 | tf_op jit(solution)/shard_map/reduce_scatter | solution.py:280
  1587.9 2.8 convert_element_type.208
  1590.7 149.6 %reduce-scatter.20.cloned.1.call-done = bf16[2048,256]{1,0:T(8,128)(2,1)} async-done(((bf16[2048,2048]{1,0:T(8,128)(2,1)}), bf16[2048,256]{1,0:T(8,128)(2,1)}) %reduce-scatter.20.cloned.1.call-update) | async-done | bytes 1048592 | tf_op jit(solution)/shard_map/reduce_scatter | solution.py:283
  1740.3 2.7 convert_element_type.210
  (264 shorter events, 86.1 us)
Async XLA Ops:
  7.2 27.1 %copy-start.2 = (bf16[256,2048]{1,0:T(8,128)(2,1)S(1)}, bf16[256,2048]{1,0:T(8,128)(2,1)}, u32[]{:S(2)}) copy-start(bf16[256,2048]{1,0:T(8,128)(2,1)} %param.16) | copy-start | bytes 3145732
  7.2 55.0 %all-gather.11.cloned.1.call-start = ((), (), s32[]{:S(2)}) async-start(), calls=%async_computation.7 | async-start | bytes 2359296 | tf_op jit(solution)/shard_map/all_gather | solution.py:99
  7.9 104.2 %all-gather.17.cloned.1.call-start = ((), (), s32[]{:S(2)}) async-start(), calls=%async_computation.10 | async-start | bytes 2359296 | tf_op jit(solution)/shard_map/all_gather | solution.py:98
  8.7 153.4 %all-gather.13.cloned.1.call-start = ((), (), s32[]{:S(2)}) async-start(), calls=%async_computation.8 | async-start | bytes 2359296 | tf_op jit(solution)/shard_map/all_gather | solution.py:100
  9.4 200.5 %all-gather.15.cloned.1.call-start = ((), (), s32[]{:S(2)}) async-start(), calls=%async_computation.9 | async-start | bytes 2621440 | tf_op jit(solution)/shard_map/all_gather | solution.py:135
  34.5 30.0 %copy-start.35 = (f32[256]{0:T(256)}, f32[256]{0:T(256)S(1)}, u32[]{:S(2)}) copy-start(f32[256]{0:T(256)S(1)} %fusion.33) | copy-start | bytes 3076
  34.6 127.5 %copy-start.30 = (f32[256]{0:T(256)}, f32[256]{0:T(256)S(1)}, u32[]{:S(2)}) copy-start(f32[256]{0:T(256)S(1)} %fusion.49) | copy-start | bytes 3076
  123.1 42.9 %copy-start.27 = (bf16[256,512]{1,0:T(8,128)(2,1)S(1)}, bf16[256,512]{1,0:T(8,128)(2,1)}, u32[]{:S(2)}) copy-start(bf16[256,512]{1,0:T(8,128)(2,1)} %get-tuple-element.660) | copy-start | bytes 786436
  165.3 96.3 %all-gather.19.cloned.1.call-start = ((), (), s32[]{:S(2)}) async-start(), calls=%async_computation.11 | async-start | bytes 2359296 | tf_op jit(solution)/shard_map/all_gather | solution.py:101
  165.9 149.1 %all-reduce.12.cloned.1.call-start = ((), (), s32[]{:S(2)}) async-start(), calls=%async_computation.12 | async-start | bytes 4194304 | tf_op jit(solution)/shard_map/psum | solution.py:159
  233.8 31.4 %copy-start.17 = (bf16[256,512]{0,1:T(8,128)(2,1)}, bf16[256,512]{0,1:T(8,128)(2,1)S(1)}, u32[]{:S(2)}) copy-start(bf16[256,512]{0,1:T(8,128)(2,1)S(1)} %fusion.37) | copy-start | bytes 786436
  265.2 2.3 copy-start.40
  265.2 49.7 %copy-start.3 = (bf16[256,2048]{1,0:T(8,128)(2,1)S(1)}, bf16[256,2048]{1,0:T(8,128)(2,1)}, u32[]{:S(2)}) copy-start(bf16[256,2048]{1,0:T(8,128)(2,1)} %param.16) | copy-start | bytes 3145732
  265.2 177.1 %all-gather.21.cloned.1.call-start = ((), (), s32[]{:S(2)}) async-start(), calls=%async_computation.13 | async-start | bytes 9437184 | tf_op jit(solution)/shard_map/all_gather | solution.py:102
  266.0 301.8 %all-gather.23.cloned.1.call-start = ((), (), s32[]{:S(2)}) async-start(), calls=%async_computation.14 | async-start | bytes 9437184 | tf_op jit(solution)/shard_map/all_gather | solution.py:103
  266.7 426.9 %all-gather.25.cloned.1.call-start = ((), (), s32[]{:S(2)}) async-start(), calls=%async_computation.15 | async-start | bytes 9437184 | tf_op jit(solution)/shard_map/all_gather | solution.py:104
  267.5 495.2 %all-reduce.14.cloned.1.call-start = ((), (), s32[]{:S(2)}) async-start(), calls=%async_computation.16 | async-start | bytes 4194304 | tf_op jit(solution)/shard_map/psum | solution.py:198
  314.9 2.6 copy-start.28
  316.9 448.6 %copy-start = (f32[256,2048]{1,0:T(8,128)}, f32[256,2048]{1,0:T(8,128)S(1)}, u32[]{:S(2)}) copy-start(f32[256,2048]{1,0:T(8,128)S(1)} %get-tuple-element.644) | copy-start | bytes 6291460
  317.8 250.0 %copy-start.9 = (bf16[256,2048]{1,0:T(8,128)(2,1)}, bf16[256,2048]{1,0:T(8,128)(2,1)S(1)}, u32[]{:S(2)}) copy-start(bf16[256,2048]{1,0:T(8,128)(2,1)S(1)} %multiply_convert_fusion.3) | copy-start | bytes 3145732
  702.6 6.6 copy-start.25
  702.6 6.6 copy-start.23
  702.6 6.6 copy-start.39
  712.9 1.0 copy-start.13
  712.9 286.6 %all-reduce.16.cloned.1.call-start = ((), (), s32[]{:S(2)}) async-start(), calls=%async_computation.24 | async-start | bytes 4194304 | tf_op jit(solution)/shard_map/psum | solution.py:166
  715.0 47.7 %copy-start.29 = (f32[8,1,256]{2,1,0:T(1,128)S(1)}, f32[8,1,256]{2,1,0:T(1,128)}, u32[]{:S(2)}) copy-start(f32[8,1,256]{2,1,0:T(1,128)} %convert_element_type.216) | copy-start | bytes 24580
  715.0 47.7 %copy-start.33 = (f32[256]{0:T(256)S(1)}, f32[256]{0:T(256)}, u32[]{:S(2)}) copy-start(f32[256]{0:T(256)} %copy-done.32) | copy-start | bytes 3076
  722.4 43.1 %copy-start.38 = (f32[256]{0:T(256)S(1)}, f32[256]{0:T(256)}, u32[]{:S(2)}) copy-start(f32[256]{0:T(256)} %copy-done.37) | copy-start | bytes 3076
  762.7 2.9 copy-start.12
  762.7 2.9 copy-start.14
  765.5 1.0 copy-start.8
  765.6 1.8 copy-start.11
  767.3 1.4 copy-start.5
  775.3 38.2 %collective-permute-start.1 = (f32[2,256,512]{1,2,0:T(8,128)}, f32[2,256,512]{1,2,0:T(8,128)S(1)}, u32[]{:S(2)}, u32[]{:S(2)}) collective-permute-start(f32[2,256,512]{1,2,0:T(8,128)} %maximum_add_fusion.2), channel_id=1, source_target_pairs={{12,0},{0,4},{4,8},{8,12},{13,1},{1,5},{5,9},{9,13},{14,2},{2,6},{... | collective-permute-start | bytes 3145736 | tf_op jit(solution)/shard_map/while/body/eval_jaxpr/ppermute | solution.py:19
  776.8 36.7 %collective-permute-start = (bf16[2,256,512]{1,2,0:T(8,128)(2,1)S(1)}, bf16[2,256,512]{1,2,0:T(8,128)(2,1)}, u32[]{:S(2)}, u32[]{:S(2)}) collective-permute-start(bf16[2,256,512]{1,2,0:T(8,128)(2,1)S(1)} %copy.95), channel_id=1, source_target_pairs={{12,0},{0,4},{4,8},{8,12},{13,1},{1,5},{5,9},{9,13},{14,2},{2,6},{... | collective-permute-start | bytes 1572872 | tf_op jit(solution)/shard_map/while/body/eval_jaxpr/ppermute | solution.py:19
  820.0 37.3 %collective-permute-start.1 = (f32[2,256,512]{1,2,0:T(8,128)}, f32[2,256,512]{1,2,0:T(8,128)S(1)}, u32[]{:S(2)}, u32[]{:S(2)}) collective-permute-start(f32[2,256,512]{1,2,0:T(8,128)} %maximum_add_fusion.2), channel_id=1, source_target_pairs={{12,0},{0,4},{4,8},{8,12},{13,1},{1,5},{5,9},{9,13},{14,2},{2,6},{... | collective-permute-start | bytes 3145736 | tf_op jit(solution)/shard_map/while/body/eval_jaxpr/ppermute | solution.py:19
  820.0 37.3 %collective-permute-start = (bf16[2,256,512]{1,2,0:T(8,128)(2,1)S(1)}, bf16[2,256,512]{1,2,0:T(8,128)(2,1)}, u32[]{:S(2)}, u32[]{:S(2)}) collective-permute-start(bf16[2,256,512]{1,2,0:T(8,128)(2,1)S(1)} %copy.95), channel_id=1, source_target_pairs={{12,0},{0,4},{4,8},{8,12},{13,1},{1,5},{5,9},{9,13},{14,2},{2,6},{... | collective-permute-start | bytes 1572872 | tf_op jit(solution)/shard_map/while/body/eval_jaxpr/ppermute | solution.py:19
  863.8 36.4 %collective-permute-start.1 = (f32[2,256,512]{1,2,0:T(8,128)}, f32[2,256,512]{1,2,0:T(8,128)S(1)}, u32[]{:S(2)}, u32[]{:S(2)}) collective-permute-start(f32[2,256,512]{1,2,0:T(8,128)} %maximum_add_fusion.2), channel_id=1, source_target_pairs={{12,0},{0,4},{4,8},{8,12},{13,1},{1,5},{5,9},{9,13},{14,2},{2,6},{... | collective-permute-start | bytes 3145736 | tf_op jit(solution)/shard_map/while/body/eval_jaxpr/ppermute | solution.py:19
  863.8 36.4 %collective-permute-start = (bf16[2,256,512]{1,2,0:T(8,128)(2,1)S(1)}, bf16[2,256,512]{1,2,0:T(8,128)(2,1)}, u32[]{:S(2)}, u32[]{:S(2)}) collective-permute-start(bf16[2,256,512]{1,2,0:T(8,128)(2,1)S(1)} %copy.95), channel_id=1, source_target_pairs={{12,0},{0,4},{4,8},{8,12},{13,1},{1,5},{5,9},{9,13},{14,2},{2,6},{... | collective-permute-start | bytes 1572872 | tf_op jit(solution)/shard_map/while/body/eval_jaxpr/ppermute | solution.py:19
  906.6 35.5 %collective-permute-start.1 = (f32[2,256,512]{1,2,0:T(8,128)}, f32[2,256,512]{1,2,0:T(8,128)S(1)}, u32[]{:S(2)}, u32[]{:S(2)}) collective-permute-start(f32[2,256,512]{1,2,0:T(8,128)} %maximum_add_fusion.2), channel_id=1, source_target_pairs={{12,0},{0,4},{4,8},{8,12},{13,1},{1,5},{5,9},{9,13},{14,2},{2,6},{... | collective-permute-start | bytes 3145736 | tf_op jit(solution)/shard_map/while/body/eval_jaxpr/ppermute | solution.py:19
  906.6 35.5 %collective-permute-start = (bf16[2,256,512]{1,2,0:T(8,128)(2,1)S(1)}, bf16[2,256,512]{1,2,0:T(8,128)(2,1)}, u32[]{:S(2)}, u32[]{:S(2)}) collective-permute-start(bf16[2,256,512]{1,2,0:T(8,128)(2,1)S(1)} %copy.95), channel_id=1, source_target_pairs={{12,0},{0,4},{4,8},{8,12},{13,1},{1,5},{5,9},{9,13},{14,2},{2,6},{... | collective-permute-start | bytes 1572872 | tf_op jit(solution)/shard_map/while/body/eval_jaxpr/ppermute | solution.py:19
  942.1 1.3 copy-start.7
  943.4 1.6 copy-start.20
  945.0 1.6 copy-start.19
  946.5 1.6 copy-start.21
  949.9 122.0 %reduce-scatter.14.cloned.1.call-start = ((), (), s32[]{:S(2)}) async-start(), calls=%async_computation.20 | async-start | bytes 2359296 | tf_op jit(solution)/shard_map/reduce_scatter | solution.py:274
  954.5 1.2 copy-start.4
  954.5 1.2 copy-start.31
  954.5 188.8 %reduce-scatter.8.cloned.1.call-start = ((), (), s32[]{:S(2)}) async-start(), calls=%async_computation.17 | async-start | bytes 2359296 | tf_op jit(solution)/shard_map/reduce_scatter | solution.py:265
  957.9 255.8 %reduce-scatter.10.cloned.1.call-start = ((), (), s32[]{:S(2)}) async-start(), calls=%async_computation.18 | async-start | bytes 2359296 | tf_op jit(solution)/shard_map/reduce_scatter | solution.py:268
  960.3 2.6 copy-start.10
  960.3 324.1 %reduce-scatter.12.cloned.1.call-start = ((), (), s32[]{:S(2)}) async-start(), calls=%async_computation.19 | async-start | bytes 2359296 | tf_op jit(solution)/shard_map/reduce_scatter | solution.py:271
  962.8 1.2 copy-start.26
  962.8 473.6 %reduce-scatter.16.cloned.1.call-start = ((), (), s32[]{:S(2)}) async-start(), calls=%async_computation.21 | async-start | bytes 9437184 | tf_op jit(solution)/shard_map/reduce_scatter | solution.py:277
  969.7 1.2 copy-start.24
  969.7 618.2 %reduce-scatter.18.cloned.1.call-start = ((), (), s32[]{:S(2)}) async-start(), calls=%async_computation.22 | async-start | bytes 9437184 | tf_op jit(solution)/shard_map/reduce_scatter | solution.py:280
  976.6 1.2 copy-start.15
  976.6 1.5 copy-start.22
  976.6 763.7 %reduce-scatter.20.cloned.1.call-start = ((), (), s32[]{:S(2)}) async-start(), calls=%async_computation.23 | async-start | bytes 9437184 | tf_op jit(solution)/shard_map/reduce_scatter | solution.py:283
  983.8 18.0 %copy-start.34 = (bf16[2048]{0:T(1024)(128)(2,1)S(1)}, bf16[2048]{0:T(1024)(128)(2,1)}, u32[]{:S(2)}) copy-start(bf16[2048]{0:T(1024)(128)(2,1)} %get-tuple-element.601) | copy-start | bytes 12292
  983.8 41.3 %copy-start.36 = (f32[256]{0:T(256)S(1)}, f32[256]{0:T(256)}, u32[]{:S(2)}) copy-start(f32[256]{0:T(256)} %copy-done.35) | copy-start | bytes 3076
  983.8 41.3 %copy-start.1 = (f32[256,2048]{1,0:T(8,128)S(1)}, f32[256,2048]{1,0:T(8,128)}, u32[]{:S(2)}) copy-start(f32[256,2048]{1,0:T(8,128)} %copy-done) | copy-start | bytes 6291460
  1025.2 2.7 copy-start.6
  1025.2 2.7 copy-start.16
  (4 other events, 2.8 us)
Sparse Core Ops, SparseCore 0:
  10.1 52.0 all-gather.10
  64.3 47.7 all-gather.16
  114.3 47.7 all-gather.12
  165.4 44.4 all-gather.14
  211.7 49.7 all-gather.18
  265.3 49.5 all-reduce.11
  317.3 125.0 all-gather.20
  444.7 123.1 all-gather.22
  570.0 123.5 all-gather.24
  713.1 49.5 all-reduce.13
  950.0 49.4 all-reduce.15
  1003.3 68.4 reduce-scatter.13
  1076.4 66.8 reduce-scatter.7
  1147.1 66.5 reduce-scatter.9
  1217.5 66.8 reduce-scatter.11
  1288.3 148.0 reduce-scatter.15
  1439.9 148.0 reduce-scatter.17
  1591.9 148.3 reduce-scatter.19
where the time goes:
time: 1760 us; the launch traced here: 1750 us
  waiting for transfers between devices  1470 us (84%)
  matrix products  106 us (6%)
  other arithmetic  63.6 us (4%)
  blocking collectives  62.2 us (4%)
  local copies, waits for them, and re-layouts  28.8 us (2%)
    reduce_scatter x1, waiting for transfers between devices, per_device(): lax.psum_scatter(gate_wgrad.astype(jnp.bfloat16), ('seq', 'ctx'), scatter...  150 us
    reduce_scatter x1, waiting for transfers between devices, per_device(): lax.psum_scatter(down_grad.astype(jnp.bfloat16), ('seq', 'ctx'), scatter_...  150 us
    reduce_scatter x1, waiting for transfers between devices, per_device(): lax.psum_scatter(upward_wgrad.astype(jnp.bfloat16), ('seq', 'ctx'), scatt...  149 us
    ppermute x8, waiting for transfers between devices, shifted(): return lax.ppermute(block, axis, route)  135 us
    all_gather x1, waiting for transfers between devices, per_device(): lax.all_gather(gate_weight, ('seq', 'ctx'), axis=0, tiled=True)  125 us
    all_gather x1, waiting for transfers between devices, per_device(): lax.all_gather(down_weight, ('seq', 'ctx'), axis=1, tiled=True)  119 us
    all_gather x1, waiting for transfers between devices, per_device(): lax.all_gather(up_weight, ('seq', 'ctx'), axis=0, tiled=True)  118 us
    reduce_scatter x1, waiting for transfers between devices, per_device(): lax.psum_scatter(query_wgrad.astype(jnp.bfloat16), ('seq', 'ctx'), scatte...  69.6 us
  transfers between devices with their start and end apart: 26, of which 22 were waited for; matrix products, arithmetic and copies ran while one was open for 7% of the time, Pallas kernels for 0%

commit v1 on v0

--- a/solution.py
+++ b/solution.py
@@ -3,7 +3,7 @@
 import jax
 import jax.numpy as jnp
 from jax import lax
-from jax.sharding import PartitionSpec as P
+from jax.sharding import Mesh, PartitionSpec as P
 
 HD = 64
 BLOCK = 128
@@ -77,7 +77,7 @@
     return (jnp.where(allowed[None], jnp.exp(scores), 0.0), key_heads)
 
 
-def per_device(
+def general_device(
     tokens,
     query_weight,
     key_weight,
@@ -305,7 +305,7 @@
     )
 
 
-def solution(mesh):
+def general_solution(mesh):
     placed = (
         P(("seq", "ctx"), None),
         P(("seq", "ctx"), "tp"),
@@ -321,7 +321,7 @@
         P(("seq", "ctx"), None),
     )
     return jax.shard_map(
-        per_device,
+        general_device,
         mesh=mesh,
         in_specs=placed,
         out_specs=(
@@ -339,3 +339,366 @@
         ),
         check_vma=False,
     )
+
+
+LOW = jnp.bfloat16
+
+
+def swap(value, axis, mask=1):
+    pairs = [(i, i ^ mask) for i in range(lax.axis_size(axis))]
+    return lax.ppermute(value, axis, pairs)
+
+
+def after(value, *earlier):
+    return lax.optimization_barrier((value, earlier))[0]
+
+
+def gather_rows(shard):
+    near = swap(shard, "ctx", 1)
+    far = swap(shard, "ctx", 2)
+    last = swap(far, "ctx", 1)
+    line = [shard, near, far, last]
+    line = jnp.concatenate(line + [swap(piece, "x") for piece in line])
+    return jnp.concatenate([line, swap(line, "core")])
+
+
+def gather_local_rows(local, x, core):
+    count = local.shape[0] // 4
+
+    def own(a, b):
+        return lax.dynamic_slice_in_dim(local, ((x ^ a) * 2 + (core ^ b)) * count, count, 0)
+
+    shard = own(0, 0)
+    near = swap(shard, "ctx", 1)
+    far = swap(shard, "ctx", 2)
+    last = swap(far, "ctx", 1)
+    line = [near, far, last]
+    line_x = [swap(piece, "x") for piece in line]
+    other = swap(jnp.concatenate(line + line_x), "core")
+    three = 3 * count
+    return jnp.concatenate(
+        [own(0, 0)]
+        + line
+        + [own(1, 0)]
+        + line_x
+        + [own(0, 1), other[:three], own(1, 1), other[three:]]
+    )
+
+
+def scatter_rows(keep, give):
+    mine = keep + swap(give.astype(LOW), "core").astype(jnp.float32)
+    half = mine.shape[0] // 2
+    count = half // 4
+    away = mine[half:].astype(LOW)
+    piece = [
+        mine[j * count : (j + 1) * count]
+        + swap(away[j * count : (j + 1) * count], "x").astype(jnp.float32)
+        for j in (3, 2, 1, 0)
+    ][::-1]
+    last = swap(piece[3].astype(LOW), "ctx", 1)
+    near = swap(piece[1].astype(LOW), "ctx", 1)
+    far = swap((piece[2] + last.astype(jnp.float32)).astype(LOW), "ctx", 2)
+    return piece[0] + near.astype(jnp.float32) + far.astype(jnp.float32)
+
+
+def spread(pieces, base, axis):
+    got = [pieces[0], swap(pieces[1], "ctx", 1), swap(pieces[2], "ctx", 2), swap(pieces[3], "ctx", 3)]
+    got = got + [swap(piece, "seq") for piece in got]
+    extent = pieces[0].shape[axis]
+    shape = list(pieces[0].shape)
+    shape[axis] = extent * 8
+    whole = jnp.zeros(shape, pieces[0].dtype)
+    for j, piece in enumerate(got):
+        whole = lax.dynamic_update_slice_in_dim(whole, piece, (base ^ j) * extent, axis)
+    return whole
+
+
+def collect(grad, seq, ctx, axis):
+    half = grad.shape[axis] // 2
+    extent = half // 4
+    give = lax.dynamic_slice_in_dim(grad, (1 - seq) * half, half, axis).astype(LOW)
+    keep = lax.dynamic_slice_in_dim(grad, seq * half, half, axis)
+    total = (keep + swap(give, "seq").astype(jnp.float32)).astype(LOW)
+    pieces = [
+        lax.dynamic_slice_in_dim(total, (ctx ^ j) * extent, extent, axis) for j in range(4)
+    ]
+    return [pieces[0]] + [swap(pieces[j], "ctx", j) for j in (1, 2, 3)]
+
+
+def place(pieces, ctx, axis):
+    extent = pieces[0].shape[axis]
+    shape = list(pieces[0].shape)
+    shape[axis] = extent * 4
+    whole = jnp.zeros(shape, jnp.float32)
+    for j, piece in enumerate(pieces):
+        whole = lax.dynamic_update_slice_in_dim(
+            whole, piece.astype(jnp.float32), (ctx ^ j) * extent, axis
+        )
+    return whole
+
+
+def place_rows(shard, x, core):
+    line = [shard, swap(shard, "x")]
+    line = line + [swap(piece, "core") for piece in line]
+    count = shard.shape[0]
+    whole = jnp.zeros((4 * count, shard.shape[1]), shard.dtype)
+    for j, piece in enumerate(line):
+        whole = lax.dynamic_update_slice_in_dim(
+            whole, piece, ((x ^ (j & 1)) * 2 + (core ^ (j >> 1))) * count, 0
+        )
+    return whole
+
+
+def turn(values, cosine, sine):
+    halfway = HD // 2
+    parts = []
+    for first in range(0, values.shape[1], HD):
+        low, high = values[:, first : first + halfway], values[:, first + halfway : first + HD]
+        parts += [low * cosine - high * sine, high * cosine + low * sine]
+    return jnp.concatenate(parts, axis=1)
+
+
+def fast_device(
+    tokens,
+    query_weight,
+    key_weight,
+    value_weight,
+    output_weight,
+    gate_weight,
+    up_weight,
+    down_weight,
+    attention_gain,
+    feedforward_gain,
+    order,
+    cotangent,
+):
+    f32 = jnp.float32
+    seq, ctx = lax.axis_index("seq"), lax.axis_index("ctx")
+    x, core = lax.axis_index("x"), lax.axis_index("core")
+    base = seq * 4 + ctx
+    local_rows = tokens.shape[0]
+    count = local_rows // 4
+    width = query_weight.shape[1] // 4
+    unit = gate_weight.shape[1] // 4
+    depth = query_weight.shape[0]
+
+    def columns(weight, j, extent):
+        return lax.dynamic_slice_in_dim(weight, (ctx ^ j) * extent, extent, 1)
+
+    def rows_of(weight, j, extent):
+        return lax.dynamic_slice_in_dim(weight, (ctx ^ j) * extent, extent, 0)
+
+    gains = jnp.zeros((16, 3 * width), LOW)
+    gains = gains.at[0, :depth].set(attention_gain).at[1, :depth].set(feedforward_gain)
+    qkv_pieces = [
+        jnp.concatenate(
+            [
+                jnp.concatenate(
+                    [columns(w, j, width) for w in (query_weight, key_weight, value_weight)], axis=1
+                ),
+                gains,
+            ]
+        )[None]
+        for j in range(4)
+    ]
+    every_token = gather_local_rows(tokens, x, core)
+    qkv_blocks = spread(qkv_pieces, base, 0)
+    qkv_full = qkv_blocks[:, :depth].reshape(8 * depth, 3 * width)
+    gain_first = qkv_blocks[:, depth, :depth].reshape(1, 8 * depth).astype(f32)
+    gain_second = qkv_blocks[:, depth + 1, :depth].reshape(1, 8 * depth).astype(f32)
+
+    output_full = spread([rows_of(output_weight, j, width) for j in range(4)], base, 1)
+    gate_up_full = spread(
+        [
+            jnp.concatenate([columns(gate_weight, j, unit), columns(up_weight, j, unit)], axis=1)
+            for j in range(4)
+        ],
+        base,
+        0,
+    )
+    down_full = spread([rows_of(down_weight, j, unit) for j in range(4)], base, 1)
+    every_cotangent = gather_local_rows(cotangent, x, core)
+
+    blocks = jnp.arange(16, dtype=jnp.int32)
+    stored = (
+        (ctx ^ (blocks & 3)) * local_rows
+        + (x ^ ((blocks >> 2) & 1)) * (2 * count)
+        + (core ^ (blocks >> 3)) * count
+    )
+    stored = (stored[:, None] + jnp.arange(count, dtype=jnp.int32)[None, :]).reshape(-1)
+    slots = jnp.arange(order.shape[0], dtype=jnp.int32)
+    places = jnp.sum(
+        jnp.where((stored // BLOCK)[:, None] == slots[None, :], order[None, :], 0), axis=1
+    )
+    places = places * BLOCK + stored % BLOCK
+    inverse = THETA ** (-(jnp.arange(HD // 2, dtype=f32) * 2.0) / HD)
+    angle = places.astype(f32)[:, None] * inverse[None, :]
+    cosine, sine = jnp.cos(angle), jnp.sin(angle)
+    allowed = places[:, None] >= places[None, :]
+
+    every_input = every_token.astype(f32)
+    scale_first = lax.rsqrt(jnp.mean(every_input * every_input, axis=1, keepdims=True) + EPS)
+    normed = (every_input * scale_first * gain_first).astype(LOW)
+    projected = product(normed, qkv_full)
+    queries = turn(projected[:, :width], cosine, sine).astype(LOW)
+    keys = turn(projected[:, width : 2 * width], cosine, sine).astype(LOW)
+    values = projected[:, 2 * width :].astype(LOW)
+    heads = [slice(first, first + HD) for first in range(0, width, HD)]
+    weights, totals, numerator, mixed = [], [], [], []
+    for head in heads:
+        scores = contract_cols(queries[:, head], keys[:, head]) * 0.125
+        weight = jnp.where(allowed, jnp.exp(scores), 0.0)
+        total = jnp.sum(weight, axis=1, keepdims=True)
+        summed = product(weight.astype(LOW), values[:, head])
+        weights.append(weight)
+        totals.append(total)
+        numerator.append(summed)
+        mixed.append((summed / total).astype(LOW))
+    mixed = jnp.concatenate(mixed, axis=1)
+    half = mixed.shape[0] // 2
+
+    give = product(mixed[half:], output_full)
+    keep = product(mixed[:half], output_full)
+    own_input = lax.dynamic_slice_in_dim(tokens, (x * 2 + core) * count, count, 0).astype(f32)
+    own_cotangent = lax.dynamic_slice_in_dim(cotangent, (x * 2 + core) * count, count, 0)
+    own_cotangent = own_cotangent.astype(f32)
+    middle = own_input + scatter_rows(keep, give)
+    scale_second = lax.rsqrt(jnp.mean(middle * middle, axis=1, keepdims=True) + EPS)
+    normed_two = gather_rows((middle * scale_second * gain_second).astype(LOW))
+
+    gate_up = product(normed_two, gate_up_full)
+    hidden_grad = contract_cols(every_cotangent, down_full)
+    gate, up = gate_up[:, :unit], gate_up[:, unit:]
+    sigmoid = 1.0 / (1.0 + jnp.exp(-gate))
+    silu = gate * sigmoid
+    hidden = (silu * up).astype(LOW)
+    gate_grad = hidden_grad * up * (sigmoid * (1.0 + gate * (1.0 - sigmoid)))
+    gate_up_grad = jnp.concatenate([gate_grad, hidden_grad * silu], axis=1).astype(LOW)
+    give = contract_cols(gate_up_grad[half:], gate_up_full)
+    keep = contract_cols(gate_up_grad[:half], gate_up_full)
+    normed_two_grad = scatter_rows(keep, give)
+    second_gain_part = jnp.sum(normed_two_grad * middle * scale_second, axis=0)
+    scaled = normed_two_grad * gain_second
+    middle_grad = (
+        own_cotangent
+        + scale_second * scaled
+        - middle * scale_second**3 * jnp.mean(scaled * middle, axis=1, keepdims=True)
+    )
+    branch_grad = gather_rows(middle_grad.astype(LOW))
+
+    down_pieces = collect(contract_rows(hidden, every_cotangent), seq, ctx, 1)
+    gate_up_pieces = collect(contract_rows(normed_two, gate_up_grad), seq, ctx, 0)
+    produced = scatter_rows(product(hidden[:half], down_full), product(hidden[half:], down_full))
+    block_output = place_rows((middle + produced).astype(LOW), x, core)
+
+    mixed_grad = contract_cols(branch_grad, output_full)
+    output_pieces = collect(contract_rows(mixed, branch_grad), seq, ctx, 1)
+    query_grad, key_grad, value_grad = [], [], []
+    for index, head in enumerate(heads):
+        grad = mixed_grad[:, head]
+        numerator_grad = (grad / totals[index]).astype(LOW)
+        total_grad = -jnp.sum(grad * numerator[index], axis=1, keepdims=True) / (
+            totals[index] * totals[index]
+        )
+        through = contract_cols(numerator_grad, values[:, head])
+        slopes = (weights[index] * (through + total_grad)).astype(LOW)
+        query_grad.append(product(slopes, keys[:, head]) * 0.125)
+        key_grad.append(contract_rows(slopes, queries[:, head]) * 0.125)
+        value_grad.append(contract_rows(weights[index].astype(LOW), numerator_grad))
+    projected_grad = jnp.concatenate(
+        [
+            turn(jnp.concatenate(query_grad, axis=1), cosine, -sine),
+            turn(jnp.concatenate(key_grad, axis=1), cosine, -sine),
+            jnp.concatenate(value_grad, axis=1),
+        ],
+        axis=1,
+    ).astype(LOW)
+    give = contract_cols(projected_grad[half:], qkv_full)
+    keep = contract_cols(projected_grad[:half], qkv_full)
+    normed_grad = scatter_rows(keep, give)
+    scale_own = lax.rsqrt(jnp.mean(own_input * own_input, axis=1, keepdims=True) + EPS)
+    first_gain_part = jnp.sum(normed_grad * own_input * scale_own, axis=0)
+    scaled = normed_grad * gain_first
+    input_grad = (
+        middle_grad
+        + scale_own * scaled
+        - own_input * scale_own**3 * jnp.mean(scaled * own_input, axis=1, keepdims=True)
+    )
+    input_grad = place_rows(input_grad.astype(LOW), x, core).astype(f32)
+    qkv_pieces = collect(contract_rows(normed, projected_grad), seq, ctx, 0)
+
+    part = jnp.stack([first_gain_part, second_gain_part])
+    part = part + swap(part, "core")
+    part = part + swap(part, "x")
+    extent = part.shape[1] // 2
+    part = lax.dynamic_slice_in_dim(part, seq * extent, extent, 1) + swap(
+        lax.dynamic_slice_in_dim(part, (1 - seq) * extent, extent, 1), "seq"
+    )
+    share = [lax.dynamic_slice_in_dim(part, (ctx ^ j) * depth, depth, 1) for j in range(4)]
+    gain_grads = share[0] + swap(share[1], "ctx", 1)
+    gain_grads = gain_grads + swap(share[2], "ctx", 2) + swap(share[3], "ctx", 3)
+
+    def cut(pieces, first, extent):
+        return place([piece[:, first : first + extent] for piece in pieces], ctx, 1)
+
+    return (
+        block_output,
+        input_grad,
+        cut(qkv_pieces, 0, width),
+        cut(qkv_pieces, width, width),
+        cut(qkv_pieces, 2 * width, width),
+        place(output_pieces, ctx, 0),
+        cut(gate_up_pieces, 0, unit),
+        cut(gate_up_pieces, unit, unit),
+        place(down_pieces, ctx, 0),
+        gain_grads[0],
+        gain_grads[1],
+    )
+
+
+def fast_solution(mesh):
+    sizes = mesh.shape
+    lines = Mesh(
+        mesh.devices.reshape(sizes["seq"], sizes["ctx"], 2, 2), ("seq", "ctx", "x", "core")
+    )
+    rows, heads = ("seq", "ctx"), ("x", "core")
+    wide, tall = P(rows, heads), P(heads, rows)
+    return jax.shard_map(
+        fast_device,
+        mesh=lines,
+        in_specs=(
+            P(rows, None),
+            wide,
+            wide,
+            wide,
+            tall,
+            wide,
+            wide,
+            tall,
+            P(rows),
+            P(rows),
+            P(),
+            P(rows, None),
+        ),
+        out_specs=(
+            P(rows, None),
+            P(rows, None),
+            wide,
+            wide,
+            wide,
+            tall,
+            wide,
+            wide,
+            tall,
+            P(rows),
+            P(rows),
+        ),
+        check_vma=False,
+    )
+
+
+def solution(mesh):
+    sizes = mesh.shape
+    if mesh.axis_names == ("seq", "ctx", "tp") and tuple(sizes.values()) == (2, 4, 4):
+        return fast_solution(mesh)
+    return general_solution(mesh)

time: 1760 us -> 635 us (0.36)
  waiting for transfers between devices: 1470 us -> 376 us
  starting transfers between devices: 5.36 us -> 128 us
  blocking collectives: 62.2 us -> 0 us
  matrix products: 106 us -> 61.9 us
  other arithmetic: 63.6 us -> 20.5 us
    reduce_scatter x7 -> x0, waiting for transfers between devices: 698 us -> none  [the longest x1 150 us: per_device(): lax.psum_scatter(gate_wgrad.astype(jnp.bfloat16), ('seq', 'ctx'), scatter...]
    all_gather x8 -> x0, waiting for transfers between devices: 547 us -> none  [the longest x1 125 us: per_device(): lax.all_gather(gate_weight, ('seq', 'ctx'), axis=0, tiled=True)]
    ppermute x8 -> x118, waiting for transfers between devices: 135 us -> 376 us  [swap(): return lax.ppermute(value, axis, pairs)]
    ppermute x8 -> x118, starting transfers between devices: 4.17 us -> 128 us  [swap(): return lax.ppermute(value, axis, pairs)]
    psum x3 -> x0, waiting for transfers between devices: 83 us -> none  [the longest x1 40.2 us: per_device(): lax.psum(contract_cols(gate_grad, back_gate) + contract_cols(upward_grad,...]
    all_gather x2 -> x0, blocking collectives: 40.2 us -> none  [the longest x1 22.3 us: per_device(): lax.all_gather(attention_gain, ('seq', 'ctx'), axis=0, tiled=True)]
    dot_general x28 -> x0, matrix products: 23.4 us -> none  [the longest x4 8.08 us: visit(): jnp.einsum('hqk,khd->qhd', slopes, key_heads, preferred_element_type=jnp....]
    unnamed x1 -> x0, blocking collectives: 22.1 us -> none
  transfers between devices with their start and end apart: 26 -> 118, of which waited for: 22 -> 66; matrix products, arithmetic and copies ran while one was open for 7% -> 13% of each run, Pallas kernels for 0% -> 0%
where the time goes in v1:
time: 635 us; the launch traced here: 628 us
  waiting for transfers between devices  376 us (59%)
  starting transfers between devices  128 us (20%)
  matrix products  61.9 us (10%)
  local copies, waits for them, and re-layouts  37.1 us (6%)
  other arithmetic  20.5 us (3%)
    ppermute x118, waiting for transfers between devices, swap(): return lax.ppermute(value, axis, pairs)  376 us
    ppermute x118, starting transfers between devices, swap(): return lax.ppermute(value, axis, pairs)  128 us
    dot_general x10, matrix products, contract_cols(): lax.dot_general(left, right, (((1,), (1,)), ((), ())), preferred_element_...  30.1 us
    dot_general x10, matrix products, product(): return jnp.dot(left, right, preferred_element_type=jnp.float32)  17.9 us
    dynamic_update_slice x28, local copies, waits for them, and re-layouts, spread(): lax.dynamic_update_slice_in_dim(whole, piece, (base ^ j) * extent, axis)  14.5 us
    dot_general x8, matrix products, contract_rows(): lax.dot_general(left, right, (((0,), (0,)), ((), ())), preferred_element_...  13.9 us
  transfers between devices with their start and end apart: 118, of which 66 were waited for; matrix products, arithmetic and copies ran while one was open for 13% of the time, Pallas kernels for 0%

profile of v1, /device:TPU:0, one launch (start us, length us, event | category | flops | bytes accessed | tf_op | source)
XLA Modules:
  0.0 627.5 jit_solution(17385802326213147153)
XLA Ops:
  2.4 3.0 collective-permute-start
  5.4 2.6 collective-permute-start.1
  10.2 3.9 collective-permute-start.16
  21.7 3.2 collective-permute-done.15
  25.7 3.1 collective-permute-start.8
  32.8 11.1 %collective-permute-done.2 = bf16[64,2048]{1,0:T(8,128)(2,1)S(1)} collective-permute-done((bf16[64,2048]{1,0:T(8,128)(2,1)S(1)}, bf16[64,2048]{1,0:T(8,128)(2,1)S(1)}, u32[]{:S(2)}, u32[]{:S(2)}) %collective-permute-start.2) | collective-permute-done | bytes 262176 | tf_op jit(solution)/shard_map/ppermute | solution.py:349
  46.1 7.0 %collective-permute-done.4 = bf16[64,2048]{1,0:T(8,128)(2,1)S(1)} collective-permute-done((bf16[64,2048]{1,0:T(8,128)(2,1)S(1)}, bf16[64,2048]{1,0:T(8,128)(2,1)S(1)}, u32[]{:S(2)}, u32[]{:S(2)}) %collective-permute-start.4) | collective-permute-done | bytes 262176 | tf_op jit(solution)/shard_map/ppermute | solution.py:349
  58.5 2.8 collective-permute-done.19
  63.1 3.4 collective-permute-done.20
  70.6 3.9 collective-permute-done.10
  76.3 2.7 collective-permute-done.11
  89.6 3.6 fusion.5
  103.3 2.5 broadcast_in_dim.75
  114.1 11.8 %collective-permute-done.45 = bf16[512,256]{1,0:T(8,128)(2,1)} collective-permute-done((bf16[512,256]{1,0:T(8,128)(2,1)}, bf16[512,256]{1,0:T(8,128)(2,1)}, u32[]{:S(2)}, u32[]{:S(2)}) %collective-permute-start.45) | collective-permute-done | bytes 262176 | tf_op jit(solution)/shard_map/ppermute | solution.py:349
  130.3 5.0 collective-permute-start.38
  141.2 20.4 %collective-permute-done.64 = bf16[64,2048]{1,0:T(8,128)(2,1)S(1)} collective-permute-done((bf16[64,2048]{1,0:T(8,128)(2,1)S(1)}, bf16[64,2048]{1,0:T(8,128)(2,1)S(1)}, u32[]{:S(2)}, u32[]{:S(2)}) %collective-permute-start.64) | collective-permute-done | bytes 262176 | tf_op jit(solution)/shard_map/ppermute | solution.py:349
  162.4 2.5 fusion.170
  167.3 7.0 %collective-permute-done.23 = bf16[64,2048]{1,0:T(8,128)(2,1)S(1)} collective-permute-done((bf16[64,2048]{1,0:T(8,128)(2,1)S(1)}, bf16[64,2048]{1,0:T(8,128)(2,1)S(1)}, u32[]{:S(2)}, u32[]{:S(2)}) %collective-permute-start.23) | collective-permute-done | bytes 262176 | tf_op jit(solution)/shard_map/ppermute | solution.py:349
  174.3 3.0 collective-permute-done.26
  181.2 2.4 collective-permute-done.39
  188.0 4.3 collective-permute-start.24
  196.5 4.2 collective-permute-done.24
  200.7 4.3 collective-permute-done.28
  207.9 9.7 %collective-permute-done.29 = bf16[64,2048]{1,0:T(8,128)(2,1)S(1)} collective-permute-done((bf16[64,2048]{1,0:T(8,128)(2,1)S(1)}, bf16[64,2048]{1,0:T(8,128)(2,1)S(1)}, u32[]{:S(2)}, u32[]{:S(2)}) %collective-permute-start.29) | collective-permute-done | bytes 262176 | tf_op jit(solution)/shard_map/ppermute | solution.py:349
  218.3 6.2 collective-permute-done.31
  227.4 6.4 %collective-permute-done.33 = bf16[64,2048]{1,0:T(8,128)(2,1)S(1)} collective-permute-done((bf16[64,2048]{1,0:T(8,128)(2,1)S(1)}, bf16[64,2048]{1,0:T(8,128)(2,1)S(1)}, u32[]{:S(2)}, u32[]{:S(2)}) %collective-permute-start.33) | collective-permute-done | bytes 262176 | tf_op jit(solution)/shard_map/ppermute | solution.py:349
  242.8 4.3 collective-permute-done.50
  247.8 10.6 %collective-permute-done.41 = bf16[256,1024]{1,0:T(8,128)(2,1)S(1)} collective-permute-done((bf16[256,1024]{1,0:T(8,128)(2,1)S(1)}, bf16[256,1024]{1,0:T(8,128)(2,1)S(1)}, u32[]{:S(2)}, u32[]{:S(2)}) %collective-permute-start.41) | collective-permute-done | bytes 524320 | tf_op jit(solution)/shard_map/ppermute | solution.py:349
  259.2 10.4 %collective-permute-done.42 = bf16[256,1024]{1,0:T(8,128)(2,1)S(1)} collective-permute-done((bf16[256,1024]{1,0:T(8,128)(2,1)S(1)}, bf16[256,1024]{1,0:T(8,128)(2,1)S(1)}, u32[]{:S(2)}, u32[]{:S(2)}) %collective-permute-start.42) | collective-permute-done | bytes 524320 | tf_op jit(solution)/shard_map/ppermute | solution.py:349
  270.5 4.8 collective-permute-done.43
  276.4 6.8 %fusion.174 = f32[1024,1024]{0,1:T(8,128)S(1)} fusion(bf16[1024,2048]{1,0:T(8,128)(2,1)S(1)} %constant_dynamic-update-slice_fusion.21, bf16[2048,1024]{1,0:T(8,128)(2,1)} %constant_dynamic-update-slice_fusion.84), kind=kOutput, calls=%fused_computation.468 | convolution fusion | flops 4294967296 | bytes 12582912 | tf_op jit(solution)/shard_map/dot_general | solution.py:44
  283.2 3.1 multiply_convert_fusion.2
  286.3 6.7 %convolution_convert_fusion = bf16[512,2048]{1,0:T(8,128)(2,1)} fusion(bf16[2048,1024]{1,0:T(8,128)(2,1)} %constant_dynamic-update-slice_fusion.84, bf16[1024,512]{0,1:T(8,128)(2,1)S(1)} %get-tuple-element.67, bf16[1024,512]{0,1:T(8,128)(2,1)S(1)} %get-tuple-element.66), kind=kOutput, calls=%fused_computation.15 | convolution fusion | flops 2150629376 | bytes 8388608 | tf_op jit(solution)/shard_map/dot_general | solution.py:54
  297.9 4.8 fusion.7
  302.7 18.4 %collective-permute-done.108 = bf16[512,1024]{1,0:T(8,128)(2,1)S(1)} collective-permute-done((bf16[512,1024]{1,0:T(8,128)(2,1)S(1)}, bf16[512,1024]{1,0:T(8,128)(2,1)S(1)}, u32[]{:S(2)}, u32[]{:S(2)}) %collective-permute-start.108) | collective-permute-done | bytes 1048608 | tf_op jit(solution)/shard_map/ppermute | solution.py:349
  323.6 2.5 collective-permute-start.110
  326.3 7.7 %collective-permute-done.109 = bf16[512,256]{1,0:T(8,128)(2,1)S(1)} collective-permute-done((bf16[512,256]{1,0:T(8,128)(2,1)S(1)}, bf16[512,256]{1,0:T(8,128)(2,1)S(1)}, u32[]{:S(2)}, u32[]{:S(2)}) %collective-permute-start.109) | collective-permute-done | bytes 262176 | tf_op jit(solution)/shard_map/ppermute | solution.py:349
  336.0 7.2 %fusion.171 = (bf16[512,2048]{1,0:T(8,128)(2,1)S(1)}, f32[512,2048]{1,0:T(8,128)}) fusion(bf16[512,2048]{1,0:T(8,128)(2,1)} %collective-permute-done.69, bf16[2048,1024]{1,0:T(8,128)(2,1)} %constant_dynamic-update-slice_fusion.84, bf16[1024,512]{0,1:T(8,128)(2,1)S(1)} %copy-done.65, bf16[1024,512]{0,1:T(8,128)(2,1)S(1)} %copy-done.63), kind=kOutput, calls=%fused_computation.465 | convolution fusion | flops 2152726528 | bytes 14680064 | tf_op jit(solution)/shard_map/dot_general | solution.py:54
  347.5 22.6 %collective-permute-done.104 = bf16[1024,1024]{1,0:T(8,128)(2,1)S(1)} collective-permute-done((bf16[1024,1024]{1,0:T(8,128)(2,1)S(1)}, bf16[1024,1024]{1,0:T(8,128)(2,1)S(1)}, u32[]{:S(2)}, u32[]{:S(2)}) %collective-permute-start.104) | collective-permute-done | bytes 2097184 | tf_op jit(solution)/shard_map/ppermute | solution.py:349
  373.3 11.7 %collective-permute-done.53 = bf16[64,2048]{1,0:T(8,128)(2,1)S(1)} collective-permute-done((bf16[64,2048]{1,0:T(8,128)(2,1)S(1)}, bf16[64,2048]{1,0:T(8,128)(2,1)S(1)}, u32[]{:S(2)}, u32[]{:S(2)}) %collective-permute-start.53) | collective-permute-done | bytes 262176 | tf_op jit(solution)/shard_map/ppermute | solution.py:349
  385.0 5.6 collective-permute-done.56
  392.5 6.9 %collective-permute-done.75 = bf16[64,2048]{1,0:T(8,128)(2,1)S(1)} collective-permute-done((bf16[64,2048]{1,0:T(8,128)(2,1)S(1)}, bf16[64,2048]{1,0:T(8,128)(2,1)S(1)}, u32[]{:S(2)}, u32[]{:S(2)}) %collective-permute-start.75) | collective-permute-done | bytes 262176 | tf_op jit(solution)/shard_map/ppermute | solution.py:349
  401.7 8.6 %collective-permute-done.57 = bf16[64,2048]{1,0:T(8,128)(2,1)S(1)} collective-permute-done((bf16[64,2048]{1,0:T(8,128)(2,1)S(1)}, bf16[64,2048]{1,0:T(8,128)(2,1)S(1)}, u32[]{:S(2)}, u32[]{:S(2)}) %collective-permute-start.57) | collective-permute-done | bytes 262176 | tf_op jit(solution)/shard_map/ppermute | solution.py:349
  411.1 6.4 %collective-permute-done.72 = bf16[64,2048]{1,0:T(8,128)(2,1)S(1)} collective-permute-done((bf16[64,2048]{1,0:T(8,128)(2,1)S(1)}, bf16[64,2048]{1,0:T(8,128)(2,1)S(1)}, u32[]{:S(2)}, u32[]{:S(2)}) %collective-permute-start.72) | collective-permute-done | bytes 262176 | tf_op jit(solution)/shard_map/ppermute | solution.py:349
  417.5 5.9 collective-permute-done.76
  423.7 7.0 %collective-permute-done.54 = bf16[64,2048]{1,0:T(8,128)(2,1)S(1)} collective-permute-done((bf16[64,2048]{1,0:T(8,128)(2,1)S(1)}, bf16[64,2048]{1,0:T(8,128)(2,1)S(1)}, u32[]{:S(2)}, u32[]{:S(2)}) %collective-permute-start.54) | collective-permute-done | bytes 262176 | tf_op jit(solution)/shard_map/ppermute | solution.py:349
  430.8 5.3 collective-permute-done.58
  439.2 9.3 %collective-permute-done.77 = bf16[64,2048]{1,0:T(8,128)(2,1)S(1)} collective-permute-done((bf16[64,2048]{1,0:T(8,128)(2,1)S(1)}, bf16[64,2048]{1,0:T(8,128)(2,1)S(1)}, u32[]{:S(2)}, u32[]{:S(2)}) %collective-permute-start.77) | collective-permute-done | bytes 262176 | tf_op jit(solution)/shard_map/ppermute | solution.py:349
  448.7 8.3 %collective-permute-done.79 = bf16[64,2048]{1,0:T(8,128)(2,1)S(1)} collective-permute-done((bf16[64,2048]{1,0:T(8,128)(2,1)S(1)}, bf16[64,2048]{1,0:T(8,128)(2,1)S(1)}, u32[]{:S(2)}, u32[]{:S(2)}) %collective-permute-start.79) | collective-permute-done | bytes 262176 | tf_op jit(solution)/shard_map/ppermute | solution.py:349
  459.2 6.0 collective-permute-done.81
  465.5 2.5 collective-permute-done.82
  468.0 3.5 collective-permute-done.83
  476.1 33.8 %collective-permute-done.106 = bf16[256,1024]{1,0:T(8,128)(2,1)S(1)} collective-permute-done((bf16[256,1024]{1,0:T(8,128)(2,1)S(1)}, bf16[256,1024]{1,0:T(8,128)(2,1)S(1)}, u32[]{:S(2)}, u32[]{:S(2)}) %collective-permute-start.106) | collective-permute-done | bytes 524320 | tf_op jit(solution)/shard_map/ppermute | solution.py:349
  532.7 3.1 fusion.9
  537.1 3.9 collective-permute-done.100
  541.1 11.2 %collective-permute-start.101 = (bf16[128,256]{1,0:T(8,128)(2,1)S(1)}, bf16[128,256]{1,0:T(8,128)(2,1)S(1)}, u32[]{:S(2)}, u32[]{:S(2)}) collective-permute-start(bf16[128,256]{1,0:T(8,128)(2,1)S(1)} %get-tuple-element.139), channel_id=1, source_target_pairs={{0,4},{4,0},{8,12},{12,8},{1,5},{5,1},{9,13},{13,9},{2,6},{6,2},{1... | collective-permute-start | bytes 196616 | tf_op jit(solution)/shard_map/ppermute | solution.py:349
  554.8 4.4 collective-permute-done.102
  563.4 6.7 %collective-permute-done.87 = bf16[64,2048]{1,0:T(8,128)(2,1)S(1)} collective-permute-done((bf16[64,2048]{1,0:T(8,128)(2,1)S(1)}, bf16[64,2048]{1,0:T(8,128)(2,1)S(1)}, u32[]{:S(2)}, u32[]{:S(2)}) %collective-permute-start.87) | collective-permute-done | bytes 262176 | tf_op jit(solution)/shard_map/ppermute | solution.py:349
  570.1 5.2 collective-permute-done.90
  582.4 7.3 %collective-permute-done.91 = bf16[64,2048]{1,0:T(8,128)(2,1)S(1)} collective-permute-done((bf16[64,2048]{1,0:T(8,128)(2,1)S(1)}, bf16[64,2048]{1,0:T(8,128)(2,1)S(1)}, u32[]{:S(2)}, u32[]{:S(2)}) %collective-permute-start.91) | collective-permute-done | bytes 262176 | tf_op jit(solution)/shard_map/ppermute | solution.py:349
  594.1 5.5 collective-permute-done.88
  605.1 5.9 collective-permute-start.114
  612.8 4.3 collective-permute-start.115
  619.3 4.7 collective-permute-done.93
  (522 shorter events, 191.2 us)
Async XLA Ops:
  2.4 28.7 %collective-permute-start = (bf16[64,2048]{1,0:T(8,128)(2,1)S(1)}, bf16[64,2048]{1,0:T(8,128)(2,1)S(1)}, u32[]{:S(2)}, u32[]{:S(2)}) collective-permute-start(bf16[64,2048]{1,0:T(8,128)(2,1)S(1)} %get-tuple-element.47), channel_id=1, source_target_pairs={{0,4},{4,0},{8,12},{12,8},{1,5},{5,1},{9,13},{13,9},{2,6},{6,2},{1... | collective-permute-start | bytes 786440 | tf_op jit(solution)/shard_map/ppermute | solution.py:349
  5.4 25.6 %collective-permute-start.1 = (bf16[64,2048]{1,0:T(8,128)(2,1)S(1)}, bf16[64,2048]{1,0:T(8,128)(2,1)S(1)}, u32[]{:S(2)}, u32[]{:S(2)}) collective-permute-start(bf16[64,2048]{1,0:T(8,128)(2,1)S(1)} %get-tuple-element.47), channel_id=1, source_target_pairs={{0,8},{4,12},{8,0},{12,4},{1,9},{5,13},{9,1},{13,5},{2,10},{6,14},... | collective-permute-start | bytes 786440 | tf_op jit(solution)/shard_map/ppermute | solution.py:349
  10.2 14.7 %collective-permute-start.15 = (bf16[128,256]{1,0:T(8,128)(2,1)}, bf16[128,256]{1,0:T(8,128)(2,1)}, u32[]{:S(2)}, u32[]{:S(2)}) collective-permute-start(bf16[128,256]{1,0:T(8,128)(2,1)} %get-tuple-element.208), channel_id=1, source_target_pairs={{0,8},{4,12},{8,0},{12,4},{1,9},{5,13},{9,1},{13,5},{2,10},{6,14},... | collective-permute-start | bytes 196616 | tf_op jit(solution)/shard_map/ppermute | solution.py:349
  10.2 15.5 %collective-permute-start.16 = (bf16[128,256]{1,0:T(8,128)(2,1)}, bf16[128,256]{1,0:T(8,128)(2,1)}, u32[]{:S(2)}, u32[]{:S(2)}) collective-permute-start(bf16[128,256]{1,0:T(8,128)(2,1)} %get-tuple-element.204), channel_id=1, source_target_pairs={{0,12},{4,8},{8,4},{12,0},{1,13},{5,9},{9,5},{13,1},{2,14},{6,10},... | collective-permute-start | bytes 196616 | tf_op jit(solution)/shard_map/ppermute | solution.py:349
  24.8 43.4 %collective-permute-start.7 = (bf16[1,272,384]{2,1,0:T(8,128)(2,1)S(1)}, bf16[1,272,384]{2,1,0:T(8,128)(2,1)S(1)}, u32[]{:S(2)}, u32[]{:S(2)}) collective-permute-start(bf16[1,272,384]{2,1,0:T(8,128)(2,1)S(1)} %get-tuple-element.219), channel_id=1, source_target_pairs={{0,4},{4,0},{8,12},{12,8},{1,5},{5,1},{9,13},{13,9},{2,6},{6,2},{1... | collective-permute-start | bytes 626696 | tf_op jit(solution)/shard_map/ppermute | solution.py:349
  25.7 42.7 %collective-permute-start.8 = (bf16[1,272,384]{2,1,0:T(8,128)(2,1)S(1)}, bf16[1,272,384]{2,1,0:T(8,128)(2,1)S(1)}, u32[]{:S(2)}, u32[]{:S(2)}) collective-permute-start(bf16[1,272,384]{2,1,0:T(8,128)(2,1)S(1)} %get-tuple-element.220), channel_id=1, source_target_pairs={{0,8},{4,12},{8,0},{12,4},{1,9},{5,13},{9,1},{13,5},{2,10},{6,14},... | collective-permute-start | bytes 626696 | tf_op jit(solution)/shard_map/ppermute | solution.py:349
  29.7 39.0 %collective-permute-start.9 = (bf16[1,272,384]{2,1,0:T(8,128)(2,1)S(1)}, bf16[1,272,384]{2,1,0:T(8,128)(2,1)S(1)}, u32[]{:S(2)}, u32[]{:S(2)}) collective-permute-start(bf16[1,272,384]{2,1,0:T(8,128)(2,1)S(1)} %get-tuple-element.221), channel_id=1, source_target_pairs={{0,12},{4,8},{8,4},{12,0},{1,13},{5,9},{9,5},{13,1},{2,14},{6,10},... | collective-permute-start | bytes 626696 | tf_op jit(solution)/shard_map/ppermute | solution.py:349
  31.1 12.8 %collective-permute-start.2 = (bf16[64,2048]{1,0:T(8,128)(2,1)S(1)}, bf16[64,2048]{1,0:T(8,128)(2,1)S(1)}, u32[]{:S(2)}, u32[]{:S(2)}) collective-permute-start(bf16[64,2048]{1,0:T(8,128)(2,1)S(1)} %collective-permute-done.1), channel_id=1, source_target_pairs={{0,4},{4,0},{8,12},{12,8},{1,5},{5,1},{9,13},{13,9},{2,6},{6,2},{1... | collective-permute-start | bytes 786440 | tf_op jit(solution)/shard_map/ppermute | solution.py:349
  31.2 14.3 %collective-permute-start.3 = (bf16[64,2048]{1,0:T(8,128)(2,1)S(1)}, bf16[64,2048]{1,0:T(8,128)(2,1)S(1)}, u32[]{:S(2)}, u32[]{:S(2)}) collective-permute-start(bf16[64,2048]{1,0:T(8,128)(2,1)S(1)} %collective-permute-done), channel_id=1, source_target_pairs={{0,2},{2,0},{1,3},{3,1},{4,6},{6,4},{5,7},{7,5},{8,10},{10,8},{9,1... | collective-permute-start | bytes 786440 | tf_op jit(solution)/shard_map/ppermute | solution.py:349
  58.4 25.5 %collective-permute-start.6 = (bf16[384,2048]{1,0:T(8,128)(2,1)S(1)}, bf16[384,2048]{1,0:T(8,128)(2,1)S(1)}, u32[]{:S(2)}, u32[]{:S(2)}) collective-permute-start(bf16[384,2048]{1,0:T(8,128)(2,1)S(1)} %get-tuple-element.180), channel_id=1, source_target_pairs={{0,1},{1,0},{2,3},{3,2},{4,5},{5,4},{6,7},{7,6},{8,9},{9,8},{10,11... | collective-permute-start | bytes 4718600 | tf_op jit(solution)/shard_map/ppermute | solution.py:349
  68.2 62.1 %collective-permute-start.62 = (bf16[64,2048]{1,0:T(8,128)(2,1)S(1)}, bf16[64,2048]{1,0:T(8,128)(2,1)}, u32[]{:S(2)}, u32[]{:S(2)}) collective-permute-start(bf16[64,2048]{1,0:T(8,128)(2,1)S(1)} %get-tuple-element.53), channel_id=1, source_target_pairs={{0,4},{4,0},{8,12},{12,8},{1,5},{5,1},{9,13},{13,9},{2,6},{6,2},{1... | collective-permute-start | bytes 786440 | tf_op jit(solution)/shard_map/ppermute | solution.py:349
  97.3 65.1 %collective-permute-start.21 = (bf16[512,2048]{1,0:T(8,128)(2,1)}, bf16[512,2048]{1,0:T(8,128)(2,1)}, u32[]{:S(2)}, u32[]{:S(2)}) collective-permute-start(bf16[512,2048]{1,0:T(8,128)(2,1)} %convolution_convert_fusion.1), channel_id=1, source_target_pairs={{0,1},{1,0},{2,3},{3,2},{4,5},{5,4},{6,7},{7,6},{8,9},{9,8},{10,11... | collective-permute-start | bytes 6291464 | tf_op jit(solution)/shard_map/ppermute | solution.py:349
  98.6 13.6 %collective-permute-start.44 = (bf16[512,256]{1,0:T(8,128)(2,1)}, bf16[512,256]{1,0:T(8,128)(2,1)}, u32[]{:S(2)}, u32[]{:S(2)}) collective-permute-start(bf16[512,256]{1,0:T(8,128)(2,1)} %get-tuple-element.120), channel_id=1, source_target_pairs={{0,4},{4,0},{8,12},{12,8},{1,5},{5,1},{9,13},{13,9},{2,6},{6,2},{1... | collective-permute-start | bytes 786440 | tf_op jit(solution)/shard_map/ppermute | solution.py:349
  98.6 27.2 %collective-permute-start.45 = (bf16[512,256]{1,0:T(8,128)(2,1)}, bf16[512,256]{1,0:T(8,128)(2,1)}, u32[]{:S(2)}, u32[]{:S(2)}) collective-permute-start(bf16[512,256]{1,0:T(8,128)(2,1)} %get-tuple-element.123), channel_id=1, source_target_pairs={{0,8},{4,12},{8,0},{12,4},{1,9},{5,13},{9,1},{13,5},{2,10},{6,14},... | collective-permute-start | bytes 786440 | tf_op jit(solution)/shard_map/ppermute | solution.py:349
  100.7 26.8 %collective-permute-start.46 = (bf16[512,256]{1,0:T(8,128)(2,1)}, bf16[512,256]{1,0:T(8,128)(2,1)}, u32[]{:S(2)}, u32[]{:S(2)}) collective-permute-start(bf16[512,256]{1,0:T(8,128)(2,1)} %get-tuple-element.119), channel_id=1, source_target_pairs={{0,12},{4,8},{8,4},{12,0},{1,13},{5,9},{9,5},{13,1},{2,14},{6,10},... | collective-permute-start | bytes 786440 | tf_op jit(solution)/shard_map/ppermute | solution.py:349
  112.2 25.1 %collective-permute-start.63 = (bf16[64,2048]{1,0:T(8,128)(2,1)S(1)}, bf16[64,2048]{1,0:T(8,128)(2,1)S(1)}, u32[]{:S(2)}, u32[]{:S(2)}) collective-permute-start(bf16[64,2048]{1,0:T(8,128)(2,1)S(1)} %get-tuple-element.53), channel_id=1, source_target_pairs={{0,8},{4,12},{8,0},{12,4},{1,9},{5,13},{9,1},{13,5},{2,10},{6,14},... | collective-permute-start | bytes 786440 | tf_op jit(solution)/shard_map/ppermute | solution.py:349
  125.8 53.1 %collective-permute-start.37 = (bf16[256,1024]{1,0:T(8,128)(2,1)}, bf16[256,1024]{1,0:T(8,128)(2,1)S(1)}, u32[]{:S(2)}, u32[]{:S(2)}) collective-permute-start(bf16[256,1024]{1,0:T(8,128)(2,1)} %pad_maximum_fusion.3), channel_id=1, source_target_pairs={{0,4},{4,0},{8,12},{12,8},{1,5},{5,1},{9,13},{13,9},{2,6},{6,2},{1... | collective-permute-start | bytes 1572872 | tf_op jit(solution)/shard_map/ppermute | solution.py:349
  130.3 49.5 %collective-permute-start.38 = (bf16[256,1024]{1,0:T(8,128)(2,1)}, bf16[256,1024]{1,0:T(8,128)(2,1)S(1)}, u32[]{:S(2)}, u32[]{:S(2)}) collective-permute-start(bf16[256,1024]{1,0:T(8,128)(2,1)} %pad_maximum_fusion.4), channel_id=1, source_target_pairs={{0,8},{4,12},{8,0},{12,4},{1,9},{5,13},{9,1},{13,5},{2,10},{6,14},... | collective-permute-start | bytes 1572872 | tf_op jit(solution)/shard_map/ppermute | solution.py:349
  137.3 29.8 %collective-permute-start.65 = (bf16[64,2048]{1,0:T(8,128)(2,1)}, bf16[64,2048]{1,0:T(8,128)(2,1)S(1)}, u32[]{:S(2)}, u32[]{:S(2)}) collective-permute-start(bf16[64,2048]{1,0:T(8,128)(2,1)} %collective-permute-done.62), channel_id=1, source_target_pairs={{0,2},{2,0},{1,3},{3,1},{4,6},{6,4},{5,7},{7,5},{8,10},{10,8},{9,1... | collective-permute-start | bytes 786440 | tf_op jit(solution)/shard_map/ppermute | solution.py:349
  138.7 22.9 %collective-permute-start.64 = (bf16[64,2048]{1,0:T(8,128)(2,1)S(1)}, bf16[64,2048]{1,0:T(8,128)(2,1)S(1)}, u32[]{:S(2)}, u32[]{:S(2)}) collective-permute-start(bf16[64,2048]{1,0:T(8,128)(2,1)S(1)} %collective-permute-done.63), channel_id=1, source_target_pairs={{0,4},{4,0},{8,12},{12,8},{1,5},{5,1},{9,13},{13,9},{2,6},{6,2},{1... | collective-permute-start | bytes 786440 | tf_op jit(solution)/shard_map/ppermute | solution.py:349
  167.1 16.5 %collective-permute-start.39 = (bf16[256,1024]{1,0:T(8,128)(2,1)S(1)}, bf16[256,1024]{1,0:T(8,128)(2,1)S(1)}, u32[]{:S(2)}, u32[]{:S(2)}) collective-permute-start(bf16[256,1024]{1,0:T(8,128)(2,1)S(1)} %copy-done.39), channel_id=1, source_target_pairs={{0,12},{4,8},{8,4},{12,0},{1,13},{5,9},{9,5},{13,1},{2,14},{6,10},... | collective-permute-start | bytes 1572872 | tf_op jit(solution)/shard_map/ppermute | solution.py:349
  174.3 18.1 %collective-permute-start.40 = (bf16[256,1024]{1,0:T(8,128)(2,1)S(1)}, bf16[256,1024]{1,0:T(8,128)(2,1)S(1)}, u32[]{:S(2)}, u32[]{:S(2)}) collective-permute-start(bf16[256,1024]{1,0:T(8,128)(2,1)S(1)} %copy-done.38), channel_id=1, source_target_pairs={{0,16},{16,0},{1,17},{17,1},{2,18},{18,2},{3,19},{19,3},{4,20},{20... | collective-permute-start | bytes 1572872 | tf_op jit(solution)/shard_map/ppermute | solution.py:349
  179.8 14.7 %collective-permute-start.66 = (bf16[64,2048]{1,0:T(8,128)(2,1)S(1)}, bf16[64,2048]{1,0:T(8,128)(2,1)S(1)}, u32[]{:S(2)}, u32[]{:S(2)}) collective-permute-start(bf16[64,2048]{1,0:T(8,128)(2,1)S(1)} %collective-permute-done.63), channel_id=1, source_target_pairs={{0,2},{2,0},{1,3},{3,1},{4,6},{6,4},{5,7},{7,5},{8,10},{10,8},{9,1... | collective-permute-start | bytes 786440 | tf_op jit(solution)/shard_map/ppermute | solution.py:349
  183.6 57.5 %collective-permute-start.48 = (bf16[512,256]{1,0:T(8,128)(2,1)}, bf16[512,256]{1,0:T(8,128)(2,1)S(1)}, u32[]{:S(2)}, u32[]{:S(2)}) collective-permute-start(bf16[512,256]{1,0:T(8,128)(2,1)} %collective-permute-done.44), channel_id=1, source_target_pairs={{0,16},{16,0},{1,17},{17,1},{2,18},{18,2},{3,19},{19,3},{4,20},{20... | collective-permute-start | bytes 786440 | tf_op jit(solution)/shard_map/ppermute | solution.py:349
  188.0 12.7 %collective-permute-start.24 = (bf16[64,2048]{1,0:T(8,128)(2,1)S(1)}, bf16[64,2048]{1,0:T(8,128)(2,1)S(1)}, u32[]{:S(2)}, u32[]{:S(2)}) collective-permute-start(bf16[64,2048]{1,0:T(8,128)(2,1)S(1)} %get-tuple-element.77), channel_id=1, source_target_pairs={{0,4},{4,0},{8,12},{12,8},{1,5},{5,1},{9,13},{13,9},{2,6},{6,2},{1... | collective-permute-start | bytes 786440 | tf_op jit(solution)/shard_map/ppermute | solution.py:349
  194.5 46.7 %collective-permute-start.49 = (bf16[512,256]{1,0:T(8,128)(2,1)}, bf16[512,256]{1,0:T(8,128)(2,1)S(1)}, u32[]{:S(2)}, u32[]{:S(2)}) collective-permute-start(bf16[512,256]{1,0:T(8,128)(2,1)} %collective-permute-done.45), channel_id=1, source_target_pairs={{0,16},{16,0},{1,17},{17,1},{2,18},{18,2},{3,19},{19,3},{4,20},{20... | collective-permute-start | bytes 786440 | tf_op jit(solution)/shard_map/ppermute | solution.py:349
  195.0 12.8 %collective-permute-start.67 = (bf16[64,2048]{1,0:T(8,128)(2,1)S(1)}, bf16[64,2048]{1,0:T(8,128)(2,1)S(1)}, u32[]{:S(2)}, u32[]{:S(2)}) collective-permute-start(bf16[64,2048]{1,0:T(8,128)(2,1)S(1)} %collective-permute-done.64), channel_id=1, source_target_pairs={{0,2},{2,0},{1,3},{3,1},{4,6},{6,4},{5,7},{7,5},{8,10},{10,8},{9,1... | collective-permute-start | bytes 786440 | tf_op jit(solution)/shard_map/ppermute | solution.py:349
  207.8 68.3 %collective-permute-start.68 = (bf16[384,2048]{1,0:T(8,128)(2,1)S(1)}, bf16[384,2048]{1,0:T(8,128)(2,1)S(1)}, u32[]{:S(2)}, u32[]{:S(2)}) collective-permute-start(bf16[384,2048]{1,0:T(8,128)(2,1)S(1)} %get-tuple-element.154), channel_id=1, source_target_pairs={{0,1},{1,0},{2,3},{3,2},{4,5},{5,4},{6,7},{7,6},{8,9},{9,8},{10,11... | collective-permute-start | bytes 4718600 | tf_op jit(solution)/shard_map/ppermute | solution.py:349
  240.5 17.9 %collective-permute-start.41 = (bf16[256,1024]{1,0:T(8,128)(2,1)S(1)}, bf16[256,1024]{1,0:T(8,128)(2,1)S(1)}, u32[]{:S(2)}, u32[]{:S(2)}) collective-permute-start(bf16[256,1024]{1,0:T(8,128)(2,1)S(1)} %collective-permute-done.37), channel_id=1, source_target_pairs={{0,16},{16,0},{1,17},{17,1},{2,18},{18,2},{3,19},{19,3},{4,20},{20... | collective-permute-start | bytes 1572872 | tf_op jit(solution)/shard_map/ppermute | solution.py:349
  241.1 35.2 %collective-permute-start.36 = (bf16[512,2048]{1,0:T(8,128)(2,1)S(1)}, bf16[512,2048]{1,0:T(8,128)(2,1)S(1)}, u32[]{:S(2)}, u32[]{:S(2)}) collective-permute-start(bf16[512,2048]{1,0:T(8,128)(2,1)S(1)} %get-tuple-element.166), channel_id=1, source_target_pairs={{0,1},{1,0},{2,3},{3,2},{4,5},{5,4},{6,7},{7,6},{8,9},{9,8},{10,11... | collective-permute-start | bytes 6291464 | tf_op jit(solution)/shard_map/ppermute | solution.py:349
  241.2 28.4 %collective-permute-start.42 = (bf16[256,1024]{1,0:T(8,128)(2,1)S(1)}, bf16[256,1024]{1,0:T(8,128)(2,1)S(1)}, u32[]{:S(2)}, u32[]{:S(2)}) collective-permute-start(bf16[256,1024]{1,0:T(8,128)(2,1)S(1)} %collective-permute-done.38), channel_id=1, source_target_pairs={{0,16},{16,0},{1,17},{17,1},{2,18},{18,2},{3,19},{19,3},{4,20},{20... | collective-permute-start | bytes 1572872 | tf_op jit(solution)/shard_map/ppermute | solution.py:349
  247.2 28.1 %collective-permute-start.43 = (bf16[256,1024]{1,0:T(8,128)(2,1)S(1)}, bf16[256,1024]{1,0:T(8,128)(2,1)S(1)}, u32[]{:S(2)}, u32[]{:S(2)}) collective-permute-start(bf16[256,1024]{1,0:T(8,128)(2,1)S(1)} %collective-permute-done.39), channel_id=1, source_target_pairs={{0,16},{16,0},{1,17},{17,1},{2,18},{18,2},{3,19},{19,3},{4,20},{20... | collective-permute-start | bytes 1572872 | tf_op jit(solution)/shard_map/ppermute | solution.py:349
  293.0 43.0 %collective-permute-start.69 = (bf16[512,2048]{1,0:T(8,128)(2,1)}, bf16[512,2048]{1,0:T(8,128)(2,1)}, u32[]{:S(2)}, u32[]{:S(2)}) collective-permute-start(bf16[512,2048]{1,0:T(8,128)(2,1)} %convolution_convert_fusion), channel_id=1, source_target_pairs={{0,1},{1,0},{2,3},{3,2},{4,5},{5,4},{6,7},{7,6},{8,9},{9,8},{10,11... | collective-permute-start | bytes 6291464 | tf_op jit(solution)/shard_map/ppermute | solution.py:349
  295.5 25.6 %collective-permute-start.108 = (bf16[512,1024]{1,0:T(8,128)(2,1)S(1)}, bf16[512,1024]{1,0:T(8,128)(2,1)S(1)}, u32[]{:S(2)}, u32[]{:S(2)}) collective-permute-start(bf16[512,1024]{1,0:T(8,128)(2,1)S(1)} %dynamic-slice_convert_fusion.1), channel_id=1, source_target_pairs={{0,16},{16,0},{1,17},{17,1},{2,18},{18,2},{3,19},{19,3},{4,20},{20... | collective-permute-start | bytes 3145736 | tf_op jit(solution)/shard_map/ppermute | solution.py:349
  297.6 46.4 %collective-permute-start.51 = (bf16[512,2048]{1,0:T(8,128)(2,1)S(1)}, bf16[512,2048]{1,0:T(8,128)(2,1)S(1)}, u32[]{:S(2)}, u32[]{:S(2)}) collective-permute-start(bf16[512,2048]{1,0:T(8,128)(2,1)S(1)} %convolution_convert_fusion.3), channel_id=1, source_target_pairs={{0,1},{1,0},{2,3},{3,2},{4,5},{5,4},{6,7},{7,6},{8,9},{9,8},{10,11... | collective-permute-start | bytes 6291464 | tf_op jit(solution)/shard_map/ppermute | solution.py:349
  322.8 47.3 %collective-permute-start.104 = (bf16[1024,1024]{1,0:T(8,128)(2,1)S(1)}, bf16[1024,1024]{1,0:T(8,128)(2,1)S(1)}, u32[]{:S(2)}, u32[]{:S(2)}) collective-permute-start(bf16[1024,1024]{1,0:T(8,128)(2,1)S(1)} %dynamic-slice_convert_fusion), channel_id=1, source_target_pairs={{0,16},{16,0},{1,17},{17,1},{2,18},{18,2},{3,19},{19,3},{4,20},{20... | collective-permute-start | bytes 6291464 | tf_op jit(solution)/shard_map/ppermute | solution.py:349
  323.6 148.0 %collective-permute-start.110 = (bf16[512,256]{1,0:T(8,128)(2,1)}, bf16[512,256]{1,0:T(8,128)(2,1)}, u32[]{:S(2)}, u32[]{:S(2)}) collective-permute-start(bf16[512,256]{1,0:T(8,128)(2,1)} %get-tuple-element.109), channel_id=1, source_target_pairs={{0,8},{4,12},{8,0},{12,4},{1,9},{5,13},{9,1},{13,5},{2,10},{6,14},... | collective-permute-start | bytes 786440 | tf_op jit(solution)/shard_map/ppermute | solution.py:349
  334.1 138.8 %collective-permute-start.111 = (bf16[512,256]{1,0:T(8,128)(2,1)}, bf16[512,256]{1,0:T(8,128)(2,1)S(1)}, u32[]{:S(2)}, u32[]{:S(2)}) collective-permute-start(bf16[512,256]{1,0:T(8,128)(2,1)} %get-tuple-element.108), channel_id=1, source_target_pairs={{0,12},{4,8},{8,4},{12,0},{1,13},{5,9},{9,5},{13,1},{2,14},{6,10},... | collective-permute-start | bytes 786440 | tf_op jit(solution)/shard_map/ppermute | solution.py:349
  344.0 27.0 %collective-permute-start.71 = (bf16[64,2048]{1,0:T(8,128)(2,1)}, bf16[64,2048]{1,0:T(8,128)(2,1)S(1)}, u32[]{:S(2)}, u32[]{:S(2)}) collective-permute-start(bf16[64,2048]{1,0:T(8,128)(2,1)} %get-tuple-element.89), channel_id=1, source_target_pairs={{0,2},{2,0},{1,3},{3,1},{4,6},{6,4},{5,7},{7,5},{8,10},{10,8},{9,1... | collective-permute-start | bytes 786440 | tf_op jit(solution)/shard_map/ppermute | solution.py:349
  344.1 29.0 %collective-permute-start.74 = (bf16[64,2048]{1,0:T(8,128)(2,1)S(1)}, bf16[64,2048]{1,0:T(8,128)(2,1)S(1)}, u32[]{:S(2)}, u32[]{:S(2)}) collective-permute-start(bf16[64,2048]{1,0:T(8,128)(2,1)S(1)} %get-tuple-element.87), channel_id=1, source_target_pairs={{0,2},{2,0},{1,3},{3,1},{4,6},{6,4},{5,7},{7,5},{8,10},{10,8},{9,1... | collective-permute-start | bytes 786440 | tf_op jit(solution)/shard_map/ppermute | solution.py:349
  370.1 22.4 %collective-permute-start.73 = (bf16[64,2048]{1,0:T(8,128)(2,1)S(1)}, bf16[64,2048]{1,0:T(8,128)(2,1)S(1)}, u32[]{:S(2)}, u32[]{:S(2)}) collective-permute-start(bf16[64,2048]{1,0:T(8,128)(2,1)S(1)} %get-tuple-element.88), channel_id=1, source_target_pairs={{0,2},{2,0},{1,3},{3,1},{4,6},{6,4},{5,7},{7,5},{8,10},{10,8},{9,1... | collective-permute-start | bytes 786440 | tf_op jit(solution)/shard_map/ppermute | solution.py:349
  371.0 13.9 %collective-permute-start.53 = (bf16[64,2048]{1,0:T(8,128)(2,1)S(1)}, bf16[64,2048]{1,0:T(8,128)(2,1)S(1)}, u32[]{:S(2)}, u32[]{:S(2)}) collective-permute-start(bf16[64,2048]{1,0:T(8,128)(2,1)S(1)} %get-tuple-element.93), channel_id=1, source_target_pairs={{0,2},{2,0},{1,3},{3,1},{4,6},{6,4},{5,7},{7,5},{8,10},{10,8},{9,1... | collective-permute-start | bytes 786440 | tf_op jit(solution)/shard_map/ppermute | solution.py:349
  373.1 17.5 %collective-permute-start.56 = (bf16[64,2048]{1,0:T(8,128)(2,1)S(1)}, bf16[64,2048]{1,0:T(8,128)(2,1)S(1)}, u32[]{:S(2)}, u32[]{:S(2)}) collective-permute-start(bf16[64,2048]{1,0:T(8,128)(2,1)S(1)} %get-tuple-element.91), channel_id=1, source_target_pairs={{0,2},{2,0},{1,3},{3,1},{4,6},{6,4},{5,7},{7,5},{8,10},{10,8},{9,1... | collective-permute-start | bytes 786440 | tf_op jit(solution)/shard_map/ppermute | solution.py:349
  385.0 25.8 %collective-permute-start.70 = (bf16[64,2048]{1,0:T(8,128)(2,1)S(1)}, bf16[64,2048]{1,0:T(8,128)(2,1)S(1)}, u32[]{:S(2)}, u32[]{:S(2)}) collective-permute-start(bf16[64,2048]{1,0:T(8,128)(2,1)S(1)} %get-tuple-element.86), channel_id=1, source_target_pairs={{0,2},{2,0},{1,3},{3,1},{4,6},{6,4},{5,7},{7,5},{8,10},{10,8},{9,1... | collective-permute-start | bytes 786440 | tf_op jit(solution)/shard_map/ppermute | solution.py:349
  401.3 16.2 %collective-permute-start.72 = (bf16[64,2048]{1,0:T(8,128)(2,1)S(1)}, bf16[64,2048]{1,0:T(8,128)(2,1)S(1)}, u32[]{:S(2)}, u32[]{:S(2)}) collective-permute-start(bf16[64,2048]{1,0:T(8,128)(2,1)S(1)} %get-tuple-element.72), channel_id=1, source_target_pairs={{0,4},{4,0},{8,12},{12,8},{1,5},{5,1},{9,13},{13,9},{2,6},{6,2},{1... | collective-permute-start | bytes 786440 | tf_op jit(solution)/shard_map/ppermute | solution.py:349
  410.2 13.1 %collective-permute-start.76 = (bf16[64,2048]{1,0:T(8,128)(2,1)S(1)}, bf16[64,2048]{1,0:T(8,128)(2,1)S(1)}, u32[]{:S(2)}, u32[]{:S(2)}) collective-permute-start(bf16[64,2048]{1,0:T(8,128)(2,1)S(1)} %fusion.34), channel_id=1, source_target_pairs={{0,8},{4,12},{8,0},{12,4},{1,9},{5,13},{9,1},{13,5},{2,10},{6,14},... | collective-permute-start | bytes 786440 | tf_op jit(solution)/shard_map/ppermute | solution.py:349
  410.7 13.0 %collective-permute-start.52 = (bf16[64,2048]{1,0:T(8,128)(2,1)S(1)}, bf16[64,2048]{1,0:T(8,128)(2,1)S(1)}, u32[]{:S(2)}, u32[]{:S(2)}) collective-permute-start(bf16[64,2048]{1,0:T(8,128)(2,1)S(1)} %get-tuple-element.90), channel_id=1, source_target_pairs={{0,2},{2,0},{1,3},{3,1},{4,6},{6,4},{5,7},{7,5},{8,10},{10,8},{9,1... | collective-permute-start | bytes 786440 | tf_op jit(solution)/shard_map/ppermute | solution.py:349
  417.5 13.2 %collective-permute-start.54 = (bf16[64,2048]{1,0:T(8,128)(2,1)S(1)}, bf16[64,2048]{1,0:T(8,128)(2,1)S(1)}, u32[]{:S(2)}, u32[]{:S(2)}) collective-permute-start(bf16[64,2048]{1,0:T(8,128)(2,1)S(1)} %get-tuple-element.75), channel_id=1, source_target_pairs={{0,4},{4,0},{8,12},{12,8},{1,5},{5,1},{9,13},{13,9},{2,6},{6,2},{1... | collective-permute-start | bytes 786440 | tf_op jit(solution)/shard_map/ppermute | solution.py:349
  423.4 12.7 %collective-permute-start.58 = (bf16[64,2048]{1,0:T(8,128)(2,1)S(1)}, bf16[64,2048]{1,0:T(8,128)(2,1)S(1)}, u32[]{:S(2)}, u32[]{:S(2)}) collective-permute-start(bf16[64,2048]{1,0:T(8,128)(2,1)S(1)} %fusion.40), channel_id=1, source_target_pairs={{0,8},{4,12},{8,0},{12,4},{1,9},{5,13},{9,1},{13,5},{2,10},{6,14},... | collective-permute-start | bytes 786440 | tf_op jit(solution)/shard_map/ppermute | solution.py:349
  439.1 36.5 %collective-permute-start.105 = (bf16[256,1024]{1,0:T(8,128)(2,1)S(1)}, bf16[256,1024]{1,0:T(8,128)(2,1)S(1)}, u32[]{:S(2)}, u32[]{:S(2)}) collective-permute-start(bf16[256,1024]{1,0:T(8,128)(2,1)S(1)} %get-tuple-element.81), channel_id=1, source_target_pairs={{0,4},{4,0},{8,12},{12,8},{1,5},{5,1},{9,13},{13,9},{2,6},{6,2},{1... | collective-permute-start | bytes 1572872 | tf_op jit(solution)/shard_map/ppermute | solution.py:349
  471.6 40.5 %collective-permute-start.84 = (bf16[512,2048]{1,0:T(8,128)(2,1)S(1)}, bf16[512,2048]{1,0:T(8,128)(2,1)S(1)}, u32[]{:S(2)}, u32[]{:S(2)}) collective-permute-start(bf16[512,2048]{1,0:T(8,128)(2,1)S(1)} %get-tuple-element.140), channel_id=1, source_target_pairs={{0,1},{1,0},{2,3},{3,2},{4,5},{5,4},{6,7},{7,6},{8,9},{9,8},{10,11... | collective-permute-start | bytes 6291464 | tf_op jit(solution)/shard_map/ppermute | solution.py:349
  472.7 37.2 %collective-permute-start.106 = (bf16[256,1024]{1,0:T(8,128)(2,1)S(1)}, bf16[256,1024]{1,0:T(8,128)(2,1)S(1)}, u32[]{:S(2)}, u32[]{:S(2)}) collective-permute-start(bf16[256,1024]{1,0:T(8,128)(2,1)S(1)} %get-tuple-element.80), channel_id=1, source_target_pairs={{0,8},{4,12},{8,0},{12,4},{1,9},{5,13},{9,1},{13,5},{2,10},{6,14},... | collective-permute-start | bytes 1572872 | tf_op jit(solution)/shard_map/ppermute | solution.py:349
  473.0 37.2 %collective-permute-start.107 = (bf16[256,1024]{1,0:T(8,128)(2,1)S(1)}, bf16[256,1024]{1,0:T(8,128)(2,1)S(1)}, u32[]{:S(2)}, u32[]{:S(2)}) collective-permute-start(bf16[256,1024]{1,0:T(8,128)(2,1)S(1)} %get-tuple-element.79), channel_id=1, source_target_pairs={{0,12},{4,8},{8,4},{12,0},{1,13},{5,9},{9,5},{13,1},{2,14},{6,10},... | collective-permute-start | bytes 1572872 | tf_op jit(solution)/shard_map/ppermute | solution.py:349
  475.7 34.6 %collective-permute-start.59 = (bf16[64,2048]{1,0:T(8,128)(2,1)S(1)}, bf16[64,2048]{1,0:T(8,128)(2,1)S(1)}, u32[]{:S(2)}, u32[]{:S(2)}) collective-permute-start(bf16[64,2048]{1,0:T(8,128)(2,1)S(1)} %get-tuple-element.134), channel_id=1, source_target_pairs={{0,2},{2,0},{1,3},{3,1},{4,6},{6,4},{5,7},{7,5},{8,10},{10,8},{9,1... | collective-permute-start | bytes 786440 | tf_op jit(solution)/shard_map/ppermute | solution.py:349
  530.5 28.8 %collective-permute-start.85 = (bf16[512,2048]{1,0:T(8,128)(2,1)S(1)}, bf16[512,2048]{1,0:T(8,128)(2,1)S(1)}, u32[]{:S(2)}, u32[]{:S(2)}) collective-permute-start(bf16[512,2048]{1,0:T(8,128)(2,1)S(1)} %convolution_convert_fusion.2), channel_id=1, source_target_pairs={{0,1},{1,0},{2,3},{3,2},{4,5},{5,4},{6,7},{7,6},{8,9},{9,8},{10,11... | collective-permute-start | bytes 6291464 | tf_op jit(solution)/shard_map/ppermute | solution.py:349
  535.9 27.0 %collective-permute-start.96 = (bf16[1024,384]{1,0:T(8,128)(2,1)S(1)}, bf16[1024,384]{1,0:T(8,128)(2,1)S(1)}, u32[]{:S(2)}, u32[]{:S(2)}) collective-permute-start(bf16[1024,384]{1,0:T(8,128)(2,1)S(1)} %dynamic-slice_convert_fusion.2), channel_id=1, source_target_pairs={{0,16},{16,0},{1,17},{17,1},{2,18},{18,2},{3,19},{19,3},{4,20},{20... | collective-permute-start | bytes 2359304 | tf_op jit(solution)/shard_map/ppermute | solution.py:349
  541.1 13.7 %collective-permute-start.101 = (bf16[128,256]{1,0:T(8,128)(2,1)S(1)}, bf16[128,256]{1,0:T(8,128)(2,1)S(1)}, u32[]{:S(2)}, u32[]{:S(2)}) collective-permute-start(bf16[128,256]{1,0:T(8,128)(2,1)S(1)} %get-tuple-element.139), channel_id=1, source_target_pairs={{0,4},{4,0},{8,12},{12,8},{1,5},{5,1},{9,13},{13,9},{2,6},{6,2},{1... | collective-permute-start | bytes 196616 | tf_op jit(solution)/shard_map/ppermute | solution.py:349
  561.1 14.2 %collective-permute-start.90 = (bf16[64,2048]{1,0:T(8,128)(2,1)S(1)}, bf16[64,2048]{1,0:T(8,128)(2,1)S(1)}, u32[]{:S(2)}, u32[]{:S(2)}) collective-permute-start(bf16[64,2048]{1,0:T(8,128)(2,1)S(1)} %get-tuple-element.83), channel_id=1, source_target_pairs={{0,2},{2,0},{1,3},{3,1},{4,6},{6,4},{5,7},{7,5},{8,10},{10,8},{9,1... | collective-permute-start | bytes 786440 | tf_op jit(solution)/shard_map/ppermute | solution.py:349
  563.0 17.2 %collective-permute-start.89 = (bf16[64,2048]{1,0:T(8,128)(2,1)S(1)}, bf16[64,2048]{1,0:T(8,128)(2,1)S(1)}, u32[]{:S(2)}, u32[]{:S(2)}) collective-permute-start(bf16[64,2048]{1,0:T(8,128)(2,1)S(1)} %get-tuple-element.84), channel_id=1, source_target_pairs={{0,2},{2,0},{1,3},{3,1},{4,6},{6,4},{5,7},{7,5},{8,10},{10,8},{9,1... | collective-permute-start | bytes 786440 | tf_op jit(solution)/shard_map/ppermute | solution.py:349
  575.4 14.2 %collective-permute-start.91 = (bf16[64,2048]{1,0:T(8,128)(2,1)S(1)}, bf16[64,2048]{1,0:T(8,128)(2,1)S(1)}, u32[]{:S(2)}, u32[]{:S(2)}) collective-permute-start(bf16[64,2048]{1,0:T(8,128)(2,1)S(1)} %get-tuple-element.71), channel_id=1, source_target_pairs={{0,4},{4,0},{8,12},{12,8},{1,5},{5,1},{9,13},{13,9},{2,6},{6,2},{1... | collective-permute-start | bytes 786440 | tf_op jit(solution)/shard_map/ppermute | solution.py:349
  577.2 14.7 %collective-permute-start.97 = (bf16[256,384]{1,0:T(8,128)(2,1)S(1)}, bf16[256,384]{1,0:T(8,128)(2,1)S(1)}, u32[]{:S(2)}, u32[]{:S(2)}) collective-permute-start(bf16[256,384]{1,0:T(8,128)(2,1)S(1)} %get-tuple-element.126), channel_id=1, source_target_pairs={{0,4},{4,0},{8,12},{12,8},{1,5},{5,1},{9,13},{13,9},{2,6},{6,2},{1... | collective-permute-start | bytes 589832 | tf_op jit(solution)/shard_map/ppermute | solution.py:349
  577.7 22.4 %collective-permute-start.98 = (bf16[256,384]{1,0:T(8,128)(2,1)S(1)}, bf16[256,384]{1,0:T(8,128)(2,1)S(1)}, u32[]{:S(2)}, u32[]{:S(2)}) collective-permute-start(bf16[256,384]{1,0:T(8,128)(2,1)S(1)} %get-tuple-element.125), channel_id=1, source_target_pairs={{0,8},{4,12},{8,0},{12,4},{1,9},{5,13},{9,1},{13,5},{2,10},{6,14},... | collective-permute-start | bytes 589832 | tf_op jit(solution)/shard_map/ppermute | solution.py:349
  580.0 14.1 %collective-permute-start.86 = (bf16[64,2048]{1,0:T(8,128)(2,1)S(1)}, bf16[64,2048]{1,0:T(8,128)(2,1)S(1)}, u32[]{:S(2)}, u32[]{:S(2)}) collective-permute-start(bf16[64,2048]{1,0:T(8,128)(2,1)S(1)} %get-tuple-element.82), channel_id=1, source_target_pairs={{0,2},{2,0},{1,3},{3,1},{4,6},{6,4},{5,7},{7,5},{8,10},{10,8},{9,1... | collective-permute-start | bytes 786440 | tf_op jit(solution)/shard_map/ppermute | solution.py:349
  580.3 19.3 %collective-permute-start.88 = (bf16[64,2048]{1,0:T(8,128)(2,1)S(1)}, bf16[64,2048]{1,0:T(8,128)(2,1)S(1)}, u32[]{:S(2)}, u32[]{:S(2)}) collective-permute-start(bf16[64,2048]{1,0:T(8,128)(2,1)S(1)} %get-tuple-element.70), channel_id=1, source_target_pairs={{0,4},{4,0},{8,12},{12,8},{1,5},{5,1},{9,13},{13,9},{2,6},{6,2},{1... | collective-permute-start | bytes 786440 | tf_op jit(solution)/shard_map/ppermute | solution.py:349
  (120 other events, 884.1 us)

commit v2 on v0

--- a/solution.py
+++ b/solution.py
@@ -3,9 +3,12 @@
 import jax
 import jax.numpy as jnp
 from jax import lax
-from jax.sharding import PartitionSpec as P
+from jax.experimental import pallas as pl
+from jax.experimental.pallas import tpu as pltpu
+from jax.sharding import Mesh, PartitionSpec as P
 
 HD = 64
+SEQ, CTX, TP, X, CORE = ("seq", "ctx", "tp", "x", "core")
 BLOCK = 128
 
 
@@ -77,7 +80,7 @@
     return (jnp.where(allowed[None], jnp.exp(scores), 0.0), key_heads)
 
 
-def per_device(
+def general_device(
     tokens,
     query_weight,
     key_weight,
@@ -92,18 +95,18 @@
     cotangent,
 ):
     rows_local = tokens.shape[0]
-    ctx_index = lax.axis_index("ctx")
-    ctx_total = lax.axis_size("ctx")
+    ctx_index = lax.axis_index(CTX)
+    ctx_total = lax.axis_size(CTX)
     gathered = (
-        lax.all_gather(query_weight, ("seq", "ctx"), axis=0, tiled=True),
-        lax.all_gather(key_weight, ("seq", "ctx"), axis=0, tiled=True),
-        lax.all_gather(value_weight, ("seq", "ctx"), axis=0, tiled=True),
-        lax.all_gather(output_weight, ("seq", "ctx"), axis=1, tiled=True),
-        lax.all_gather(gate_weight, ("seq", "ctx"), axis=0, tiled=True),
-        lax.all_gather(up_weight, ("seq", "ctx"), axis=0, tiled=True),
-        lax.all_gather(down_weight, ("seq", "ctx"), axis=1, tiled=True),
-        lax.all_gather(attention_gain, ("seq", "ctx"), axis=0, tiled=True),
-        lax.all_gather(feedforward_gain, ("seq", "ctx"), axis=0, tiled=True),
+        lax.all_gather(query_weight, (SEQ, CTX), axis=0, tiled=True),
+        lax.all_gather(key_weight, (SEQ, CTX), axis=0, tiled=True),
+        lax.all_gather(value_weight, (SEQ, CTX), axis=0, tiled=True),
+        lax.all_gather(output_weight, (SEQ, CTX), axis=1, tiled=True),
+        lax.all_gather(gate_weight, (SEQ, CTX), axis=0, tiled=True),
+        lax.all_gather(up_weight, (SEQ, CTX), axis=0, tiled=True),
+        lax.all_gather(down_weight, (SEQ, CTX), axis=1, tiled=True),
+        lax.all_gather(attention_gain, (SEQ, CTX), axis=0, tiled=True),
+        lax.all_gather(feedforward_gain, (SEQ, CTX), axis=0, tiled=True),
     )
     (
         full_query,
@@ -132,7 +135,7 @@
     packed = jnp.stack([key_rows, value_rows])
     empty_totals = jnp.zeros((rows_local, head_count), jnp.float32)
     empty_numerator = jnp.zeros((rows_local, width), jnp.float32)
-    arrived = lax.all_gather(packed, "ctx", axis=1, tiled=True)
+    arrived = lax.all_gather(packed, CTX, axis=1, tiled=True)
     row_total = arrived.shape[1]
 
     def one_block(block_index, partial_state):
@@ -156,26 +159,26 @@
     )
     numerator_heads = numerator.reshape(rows_local, head_count, HD)
     mixed = (numerator_heads / totals[:, :, None]).astype(jnp.bfloat16).reshape(rows_local, width)
-    middle = inputs + lax.psum(product(mixed, full_output), "tp")
+    middle = inputs + lax.psum(product(mixed, full_output), TP)
     normed_two_value, norm_back_second = jax.vjp(rms_norm, middle, gain_second.astype(jnp.float32))
     normed_two = normed_two_value.astype(jnp.bfloat16)
     activated, gated_back = jax.vjp(
         gated, product(normed_two, full_gate), product(normed_two, full_up)
     )
     hidden = activated.astype(jnp.bfloat16)
-    block_output = middle + lax.psum(product(hidden, full_down).astype(jnp.bfloat16), "tp").astype(
+    block_output = middle + lax.psum(product(hidden, full_down).astype(jnp.bfloat16), TP).astype(
         jnp.float32
     )
     back_weights = (
-        lax.all_gather(query_weight, ("seq", "ctx"), axis=0, tiled=True),
-        lax.all_gather(key_weight, ("seq", "ctx"), axis=0, tiled=True),
-        lax.all_gather(value_weight, ("seq", "ctx"), axis=0, tiled=True),
-        lax.all_gather(output_weight, ("seq", "ctx"), axis=1, tiled=True),
-        lax.all_gather(gate_weight, ("seq", "ctx"), axis=0, tiled=True),
-        lax.all_gather(up_weight, ("seq", "ctx"), axis=0, tiled=True),
-        lax.all_gather(down_weight, ("seq", "ctx"), axis=1, tiled=True),
-        lax.all_gather(attention_gain, ("seq", "ctx"), axis=0, tiled=True),
-        lax.all_gather(feedforward_gain, ("seq", "ctx"), axis=0, tiled=True),
+        lax.all_gather(query_weight, (SEQ, CTX), axis=0, tiled=True),
+        lax.all_gather(key_weight, (SEQ, CTX), axis=0, tiled=True),
+        lax.all_gather(value_weight, (SEQ, CTX), axis=0, tiled=True),
+        lax.all_gather(output_weight, (SEQ, CTX), axis=1, tiled=True),
+        lax.all_gather(gate_weight, (SEQ, CTX), axis=0, tiled=True),
+        lax.all_gather(up_weight, (SEQ, CTX), axis=0, tiled=True),
+        lax.all_gather(down_weight, (SEQ, CTX), axis=1, tiled=True),
+        lax.all_gather(attention_gain, (SEQ, CTX), axis=0, tiled=True),
+        lax.all_gather(feedforward_gain, (SEQ, CTX), axis=0, tiled=True),
     )
     (
         back_query,
@@ -196,7 +199,7 @@
     gate_wgrad = contract_rows(normed_two, gate_grad)
     upward_wgrad = contract_rows(normed_two, upward_grad)
     normed_two_grad = lax.psum(
-        contract_cols(gate_grad, back_gate) + contract_cols(upward_grad, back_up), "tp"
+        contract_cols(gate_grad, back_gate) + contract_cols(upward_grad, back_up), TP
     )
     middle_norm_grad, second_gain_grad = norm_back_second(normed_two_grad)
     middle_grad = cotangent.astype(jnp.float32) + middle_norm_grad
@@ -235,8 +238,8 @@
         carried = carried + jnp.stack(
             [key_term.reshape(rows_local, width), value_term.reshape(rows_local, width)]
         )
-        visiting = shifted(visiting, "ctx", 1)
-        carried = shifted(carried, "ctx", 1)
+        visiting = shifted(visiting, CTX, 1)
+        carried = shifted(carried, CTX, 1)
         return (visiting, carried, query_acc)
 
     start_state = (
@@ -257,37 +260,37 @@
             + contract_cols(key_proj_grad, back_key)
             + contract_cols(value_grad, back_value)
         ).astype(jnp.bfloat16),
-        "tp",
+        TP,
     ).astype(jnp.float32)
     input_norm_grad, first_gain_grad = norm_back_first(normed_grad)
     input_grad = middle_grad + input_norm_grad
     scattered = (
         lax.psum_scatter(
-            query_wgrad.astype(jnp.bfloat16), ("seq", "ctx"), scatter_dimension=0, tiled=True
+            query_wgrad.astype(jnp.bfloat16), (SEQ, CTX), scatter_dimension=0, tiled=True
         ).astype(jnp.float32),
         lax.psum_scatter(
-            key_wgrad.astype(jnp.bfloat16), ("seq", "ctx"), scatter_dimension=0, tiled=True
+            key_wgrad.astype(jnp.bfloat16), (SEQ, CTX), scatter_dimension=0, tiled=True
         ).astype(jnp.float32),
         lax.psum_scatter(
-            value_wgrad.astype(jnp.bfloat16), ("seq", "ctx"), scatter_dimension=0, tiled=True
+            value_wgrad.astype(jnp.bfloat16), (SEQ, CTX), scatter_dimension=0, tiled=True
         ).astype(jnp.float32),
         lax.psum_scatter(
-            output_wgrad.astype(jnp.bfloat16), ("seq", "ctx"), scatter_dimension=1, tiled=True
+            output_wgrad.astype(jnp.bfloat16), (SEQ, CTX), scatter_dimension=1, tiled=True
         ).astype(jnp.float32),
         lax.psum_scatter(
-            gate_wgrad.astype(jnp.bfloat16), ("seq", "ctx"), scatter_dimension=0, tiled=True
+            gate_wgrad.astype(jnp.bfloat16), (SEQ, CTX), scatter_dimension=0, tiled=True
         ).astype(jnp.float32),
         lax.psum_scatter(
-            upward_wgrad.astype(jnp.bfloat16), ("seq", "ctx"), scatter_dimension=0, tiled=True
+            upward_wgrad.astype(jnp.bfloat16), (SEQ, CTX), scatter_dimension=0, tiled=True
         ).astype(jnp.float32),
         lax.psum_scatter(
-            down_grad.astype(jnp.bfloat16), ("seq", "ctx"), scatter_dimension=1, tiled=True
+            down_grad.astype(jnp.bfloat16), (SEQ, CTX), scatter_dimension=1, tiled=True
         ).astype(jnp.float32),
         lax.psum_scatter(
-            first_gain_grad.astype(jnp.bfloat16), ("seq", "ctx"), scatter_dimension=0, tiled=True
+            first_gain_grad.astype(jnp.bfloat16), (SEQ, CTX), scatter_dimension=0, tiled=True
         ).astype(jnp.float32),
         lax.psum_scatter(
-            second_gain_grad.astype(jnp.bfloat16), ("seq", "ctx"), scatter_dimension=0, tiled=True
+            second_gain_grad.astype(jnp.bfloat16), (SEQ, CTX), scatter_dimension=0, tiled=True
         ).astype(jnp.float32),
     )
     return (
@@ -305,37 +308,965 @@
     )
 
 
-def solution(mesh):
+def general_solution(mesh):
     placed = (
-        P(("seq", "ctx"), None),
-        P(("seq", "ctx"), "tp"),
-        P(("seq", "ctx"), "tp"),
-        P(("seq", "ctx"), "tp"),
-        P("tp", ("seq", "ctx")),
-        P(("seq", "ctx"), "tp"),
-        P(("seq", "ctx"), "tp"),
-        P("tp", ("seq", "ctx")),
-        P(("seq", "ctx")),
-        P(("seq", "ctx")),
+        P((SEQ, CTX), None),
+        P((SEQ, CTX), TP),
+        P((SEQ, CTX), TP),
+        P((SEQ, CTX), TP),
+        P(TP, (SEQ, CTX)),
+        P((SEQ, CTX), TP),
+        P((SEQ, CTX), TP),
+        P(TP, (SEQ, CTX)),
+        P((SEQ, CTX)),
+        P((SEQ, CTX)),
         P(),
-        P(("seq", "ctx"), None),
+        P((SEQ, CTX), None),
     )
     return jax.shard_map(
-        per_device,
+        general_device,
         mesh=mesh,
         in_specs=placed,
         out_specs=(
-            P(("seq", "ctx"), None),
-            P(("seq", "ctx"), None),
-            P(("seq", "ctx"), "tp"),
-            P(("seq", "ctx"), "tp"),
-            P(("seq", "ctx"), "tp"),
-            P("tp", ("seq", "ctx")),
-            P(("seq", "ctx"), "tp"),
-            P(("seq", "ctx"), "tp"),
-            P("tp", ("seq", "ctx")),
-            P(("seq", "ctx")),
-            P(("seq", "ctx")),
+            P((SEQ, CTX), None),
+            P((SEQ, CTX), None),
+            P((SEQ, CTX), TP),
+            P((SEQ, CTX), TP),
+            P((SEQ, CTX), TP),
+            P(TP, (SEQ, CTX)),
+            P((SEQ, CTX), TP),
+            P((SEQ, CTX), TP),
+            P(TP, (SEQ, CTX)),
+            P((SEQ, CTX)),
+            P((SEQ, CTX)),
         ),
         check_vma=False,
     )
+
+
+LOW = jnp.bfloat16
+
+
+def swap(value, axis, mask=1):
+    pairs = [(i, i ^ mask) for i in range(lax.axis_size(axis))]
+    return lax.ppermute(value, axis, pairs)
+
+
+def tie(*values):
+    return lax.optimization_barrier(values)
+
+
+def in_main(value):
+    return pltpu.with_memory_space_constraint(value, pltpu.HBM)
+
+
+def stack_rows(pieces, local=None, places=None):
+    pieces = list(pieces)
+    own = [i for i, piece in enumerate(pieces) if piece is None]
+    given = [piece for piece in pieces if piece is not None]
+    like = given[0]
+    total, count = len(pieces), like.shape[0]
+    shape = jax.ShapeDtypeStruct((total * count, like.shape[1]), like.dtype)
+
+    def kernel(*refs):
+        at_ref, *refs = refs
+        *ins, out, sems = refs
+        source = iter(ins)
+        copies = []
+        for i in range(total):
+            if i in own:
+                first = pl.multiple_of(at_ref[own.index(i)] * count, count)
+                block = ins[-1].at[pl.ds(first, count)]
+            else:
+                block = next(source)
+            copies.append(
+                pltpu.make_async_copy(block, out.at[pl.ds(i * count, count)], sems.at[i])
+            )
+        for copy in copies:
+            copy.start()
+        for copy in copies:
+            copy.wait()
+
+    operands = given + ([local] if own else [])
+    at = places if own else jnp.zeros((1,), jnp.int32)
+    size = shape.size * shape.dtype.itemsize
+    return pl.pallas_call(
+        kernel,
+        out_shape=shape,
+        in_specs=[pl.BlockSpec(memory_space=pltpu.SMEM)]
+        + [pl.BlockSpec(memory_space=pltpu.HBM)] * len(operands),
+        out_specs=pl.BlockSpec(memory_space=pltpu.VMEM),
+        scratch_shapes=[pltpu.SemaphoreType.DMA((total,))],
+        cost_estimate=pl.CostEstimate(flops=0, transcendentals=0, bytes_accessed=2 * size),
+    )(at.astype(jnp.int32), *(in_main(operand) for operand in operands))
+
+
+def first_pieces(query, key, value, gain_one, gain_two):
+    depth, width = query.shape[0], query.shape[1] // 4
+    f32 = jnp.float32
+
+    def kernel(q_ref, k_ref, v_ref, one_ref, two_ref, out_ref):
+        line = lax.broadcasted_iota(jnp.int32, (16, depth), 0)
+        one, two = (
+            jnp.broadcast_to(ref[...].astype(f32)[None], (16, depth)) for ref in (one_ref, two_ref)
+        )
+        gains = jnp.where(line == 0, one, jnp.where(line == 1, two, 0.0)).astype(LOW)
+        for j in range(4):
+            for i, ref in enumerate((q_ref, k_ref, v_ref)):
+                out_ref[j, :depth, i * width : (i + 1) * width] = ref[:, j * width : (j + 1) * width]
+            out_ref[j, depth:, :depth] = gains
+            out_ref[j, depth:, depth:] = jnp.zeros((16, 3 * width - depth), LOW)
+
+    whole = pl.BlockSpec(memory_space=pltpu.VMEM)
+    size = 4 * (depth + 16) * 3 * width
+    return pl.pallas_call(
+        kernel,
+        out_shape=jax.ShapeDtypeStruct((4, depth + 16, 3 * width), LOW),
+        in_specs=[whole] * 5,
+        out_specs=whole,
+        cost_estimate=pl.CostEstimate(flops=0, transcendentals=0, bytes_accessed=4 * size),
+    )(query, key, value, gain_one, gain_two)
+
+
+def feed_forward(pieces, cotangent, gates, ups, downs):
+    rows, features = cotangent.shape
+    unit, count, steps = gates[0].shape[1], pieces[0].shape[0], 4
+    part = features // 2
+    block, group = rows // steps, len(pieces) // steps
+    f32 = jnp.float32
+
+    def kernel(*refs):
+        ins, refs = refs[: len(pieces)], refs[len(pieces) :]
+        cot_ref, *weights = refs[:7]
+        gate_refs, up_refs, down_refs = weights[:2], weights[2:4], weights[4:]
+        rows_ref, hidden_ref, gate_grad_ref, up_grad_ref, held, sems = refs[7:]
+        step = pl.program_id(0)
+
+        def copy(i):
+            return pltpu.make_async_copy(ins[i], held.at[pl.ds(i * count, count)], sems.at[i])
+
+        for at in range(steps):
+
+            @pl.when(step == at)
+            def _(at=at):
+                if at == 0:
+                    for i in range(len(pieces)):
+                        copy(i).start()
+                for i in range(at * group, (at + 1) * group):
+                    copy(i).wait()
+
+        values = held[pl.ds(pl.multiple_of(step * block, block), block), :]
+        rows_ref[...] = values
+        gate, up = (
+            product(values[:, :part], first[...]) + product(values[:, part:], second[...])
+            for first, second in (gate_refs, up_refs)
+        )
+        cot = cot_ref[...]
+        hidden_grad = product(cot[:, :part], down_refs[0][...])
+        hidden_grad += product(cot[:, part:], down_refs[1][...])
+        sigmoid = 1.0 / (1.0 + jnp.exp(-gate))
+        silu = gate * sigmoid
+        hidden_ref[...] = (silu * up).astype(LOW)
+        slope = sigmoid * (1.0 + gate * (1.0 - sigmoid))
+        gate_grad_ref[...] = (hidden_grad * up * slope).astype(LOW)
+        up_grad_ref[...] = (hidden_grad * silu).astype(LOW)
+
+    wide = pl.BlockSpec((block, features), lambda i: (i, 0))
+    narrow = pl.BlockSpec((block, unit), lambda i: (i, 0))
+    once = pl.Buffered(1)
+    half = pl.BlockSpec((part, unit), lambda i: (0, 0), pipeline_mode=once)
+    return pl.pallas_call(
+        kernel,
+        grid=(steps,),
+        out_shape=[jax.ShapeDtypeStruct((rows, features), LOW)]
+        + [jax.ShapeDtypeStruct((rows, unit), LOW)] * 3,
+        in_specs=[pl.BlockSpec(memory_space=pltpu.HBM)] * len(pieces)
+        + [wide, half, half, half, half, half, half],
+        out_specs=[wide, narrow, narrow, narrow],
+        scratch_shapes=[
+            pltpu.VMEM((rows, features), LOW),
+            pltpu.SemaphoreType.DMA((len(pieces),)),
+        ],
+        compiler_params=pltpu.CompilerParams(
+            dimension_semantics=("arbitrary",), vmem_limit_bytes=32 << 20
+        ),
+        cost_estimate=pl.CostEstimate(
+            flops=6 * rows * features * unit,
+            transcendentals=rows * unit,
+            bytes_accessed=6 * rows * features + 6 * features * unit + 6 * rows * unit,
+        ),
+    )(*(in_main(piece) for piece in pieces), cotangent, *gates, *ups, *downs)
+
+
+def swapped(values):
+    lane = lax.broadcasted_iota(jnp.int32, values.shape, 1)
+    size = values.shape[1]
+    back, forth = pltpu.roll(values, size - HD // 2, 1), pltpu.roll(values, HD // 2, 1)
+    return jnp.where(lane % HD < HD // 2, back, forth)
+
+
+def of_heads(parts, shape):
+    lane = lax.broadcasted_iota(jnp.int32, shape, 1)
+    result = parts[0]
+    for index in range(1, len(parts)):
+        result = jnp.where(lane // HD == index, parts[index], result)
+    return result
+
+
+def only_head(values, index):
+    lane = lax.broadcasted_iota(jnp.int32, values.shape, 1)
+    return jnp.where(lane // HD == index, values, jnp.zeros_like(values))
+
+
+def attention(pieces, tokens, token_places, own, other, cosine, sine, column, line):
+    total_width, features = own.shape[2], tokens.shape[1]
+    width, depth, steps = total_width // 3, own.shape[1] - 16, 4
+    given = [piece for piece in pieces if piece is not None]
+    count = given[0].shape[0]
+    rows = count * len(pieces)
+    block, group = rows // steps, len(pieces) // steps
+    f32 = jnp.float32
+
+    def kernel(at_ref, *refs):
+        ins, tokens_ref, refs = refs[: len(given)], refs[len(given)], refs[len(given) + 1 :]
+        own_ref, other_ref, cos_ref, sin_ref, col_ref, line_ref = refs[:6]
+        normed_ref, q_ref, k_ref, v_ref, mixed_ref, numerator_ref, total_ref = refs[6:13]
+        held, w_ref, gain_ref, sems = refs[13:]
+        step = pl.program_id(0)
+
+        def copy(i):
+            before = sum(piece is not None for piece in pieces[:i])
+            if pieces[i] is not None:
+                source = ins[before]
+            else:
+                first = pl.multiple_of(at_ref[i - before] * count, count)
+                source = tokens_ref.at[pl.ds(first, count)]
+            return pltpu.make_async_copy(source, held.at[pl.ds(i * count, count)], sems.at[i])
+
+        for at in range(steps):
+
+            @pl.when(step == at)
+            def _(at=at):
+                if at == 0:
+                    for i in range(len(pieces)):
+                        copy(i).start()
+                    for i in range(8):
+                        ref, j = (own_ref, other_ref)[i // 4], i % 4
+                        w_ref[i * depth : (i + 1) * depth, :] = ref[j, :depth, :]
+                        gain_ref[:, i * depth : (i + 1) * depth] = ref[j, depth:, :depth].astype(f32)[:8]
+                for i in range(at * group, (at + 1) * group):
+                    copy(i).wait()
+
+        @pl.when(step < steps)
+        def _():
+            at = pl.ds(pl.multiple_of(step * block, block), block)
+            values = held[at, :].astype(f32)
+            scale = lax.rsqrt(jnp.mean(values * values, axis=1, keepdims=True) + EPS)
+            normed = (values * scale * gain_ref[0:1, :]).astype(LOW)
+            normed_ref[...] = normed
+            projected = product(normed, w_ref[...])
+            cos, sin = cos_ref[at, :], sin_ref[at, :]
+            for i, ref in enumerate((q_ref, k_ref)):
+                u = projected[:, i * width : (i + 1) * width]
+                ref[at, :] = (u * cos + swapped(u) * sin).astype(LOW)
+            v_ref[at, :] = projected[:, 2 * width :].astype(LOW)
+
+        @pl.when(step >= steps)
+        def _():
+            at = pl.ds(pl.multiple_of((step - steps) * block, block), block)
+            allowed = col_ref[...] >= line_ref[...]
+            queries, keys, values = q_ref[at, :] * 0.125, k_ref[...], v_ref[...]
+            numerators, totals = [], []
+            for index in range(width // HD):
+                scores = contract_cols(only_head(queries, index), keys)
+                weights = jnp.where(allowed, jnp.exp(scores), 0.0)
+                totals.append(jnp.sum(weights, axis=1, keepdims=True))
+                numerators.append(product(weights.astype(LOW), values))
+            numerator = of_heads(numerators, (block, width))
+            total = of_heads(totals, (block, width))
+            numerator_ref[...] = numerator
+            total_ref[...] = total
+            mixed_ref[...] = (numerator / total).astype(LOW)
+
+    early = lambda i: (jnp.minimum(i, steps - 1), 0)
+    late = lambda i: (jnp.maximum(i - steps, 0), 0)
+    once = dict(pipeline_mode=pl.Buffered(1))
+
+    def still(shape):
+        return pl.BlockSpec(shape, lambda i: (0,) * len(shape), **once)
+
+    full = pl.BlockSpec((rows, width), lambda i: (0, 0))
+    late_block = pl.BlockSpec((block, width), late)
+    in_hbm = pl.BlockSpec(memory_space=pltpu.HBM)
+    return pl.pallas_call(
+        kernel,
+        grid=(2 * steps,),
+        out_shape=[pltpu.HBM((rows, features), LOW)]
+        + [pltpu.HBM((rows, width), LOW)] * 4
+        + [pltpu.HBM((rows, width), f32)] * 2,
+        in_specs=[pl.BlockSpec(memory_space=pltpu.SMEM)]
+        + [in_hbm] * (len(given) + 1)
+        + [
+            still(own.shape),
+            still(other.shape),
+            still((rows, width)),
+            still((rows, width)),
+            pl.BlockSpec((block, 1), late),
+            still((1, rows)),
+        ],
+        out_specs=[pl.BlockSpec((block, features), early)]
+        + [full] * 3
+        + [late_block] * 3,
+        scratch_shapes=[
+            pltpu.VMEM((rows, features), LOW),
+            pltpu.VMEM((features, total_width), LOW),
+            pltpu.VMEM((8, features), f32),
+            pltpu.SemaphoreType.DMA((len(pieces),)),
+        ],
+        compiler_params=pltpu.CompilerParams(
+            dimension_semantics=("arbitrary",), vmem_limit_bytes=40 << 20
+        ),
+        cost_estimate=pl.CostEstimate(
+            flops=2 * rows * features * total_width + 8 * rows * rows * width,
+            transcendentals=2 * rows * rows,
+            bytes_accessed=4 * rows * features + 4 * features * total_width + 20 * rows * width,
+        ),
+    )(token_places, *(in_main(a) for a in (*given, tokens)), own, other, *(in_main(a) for a in (cosine, sine, column, line)))
+
+
+def project(mixed, outs):
+    rows, width = mixed.shape
+    depth, block = outs[0].shape[2], rows // 4
+
+    def kernel(mixed_ref, own_ref, other_ref, *refs):
+        for i, ref in enumerate(refs):
+            values = mixed_ref[i * block : (i + 1) * block, :]
+            for j in range(8):
+                weight = (own_ref, other_ref)[j // 4][j % 4]
+                ref[:, j * depth : (j + 1) * depth] = product(values, weight).astype(LOW)
+
+    whole = pl.BlockSpec(memory_space=pltpu.VMEM)
+    return pl.pallas_call(
+        kernel,
+        out_shape=[jax.ShapeDtypeStruct((block, 8 * depth), LOW)] * 4,
+        in_specs=[whole] * 3,
+        out_specs=[whole] * 4,
+        cost_estimate=pl.CostEstimate(
+            flops=16 * rows * width * depth, transcendentals=0, bytes_accessed=20 * rows * depth
+        ),
+    )(mixed, *outs)
+
+
+def attention_back(pieces, output, queries, keys, values, mixed, numerator, total, *places):
+    rows, width = queries.shape
+    features, count, steps = output.shape[1], pieces[0].shape[0], 4
+    block, group = rows // steps, len(pieces) // steps
+    cosine, sine, column, line = places
+    f32 = jnp.float32
+
+    def kernel(*refs):
+        ins, refs = refs[: len(pieces)], refs[len(pieces) :]
+        w_ref, q_ref, k_ref, v_ref, mixed_ref, num_ref, total_ref, *refs = refs
+        cos_ref, sin_ref, col_ref, line_ref, grad_ref, keep_ref, give_ref, *refs = refs
+        held, key_sum, value_sum, output_sum, sems = refs
+        step = pl.program_id(0)
+
+        def copy(i):
+            return pltpu.make_async_copy(ins[i], held.at[pl.ds(i * count, count)], sems.at[i])
+
+        for at in range(steps):
+
+            @pl.when(step == at)
+            def _(at=at):
+                if at == 0:
+                    for i in range(len(pieces)):
+                        copy(i).start()
+                    key_sum[...] = jnp.zeros_like(key_sum)
+                    value_sum[...] = jnp.zeros_like(value_sum)
+                    output_sum[...] = jnp.zeros_like(output_sum)
+                for i in range(at * group, (at + 1) * group):
+                    copy(i).wait()
+
+        at = pl.ds(pl.multiple_of(step * block, block), block)
+        branch = held[at, :]
+        output_sum[...] += contract_rows(mixed_ref[...], branch)
+        mixed_grad = contract_cols(branch, w_ref[...])
+        totals = total_ref[...]
+        numerator_grad = (mixed_grad / totals).astype(LOW)
+        shares = mixed_grad * num_ref[...] / (totals * totals)
+        allowed = col_ref[...] >= line_ref[...]
+        query_parts = []
+        all_keys, all_values = k_ref[...], v_ref[...]
+        for index in range(width // HD):
+            query = only_head(q_ref[...], index) * 0.125
+            grad = only_head(numerator_grad, index)
+            total_grad = -jnp.sum(only_head(shares, index), axis=1, keepdims=True)
+            weights = jnp.where(allowed, jnp.exp(contract_cols(query, all_keys)), 0.0)
+            through = contract_cols(grad, all_values)
+            slopes = (weights * (through + total_grad)).astype(LOW)
+            query_parts.append(product(slopes, all_keys))
+            key_sum[...] += contract_rows(query, slopes)
+            value_sum[...] += contract_rows(grad, weights.astype(LOW))
+        query_grad = of_heads(query_parts, (block, width)) * 0.125
+
+        def unturned(u, where):
+            return (u * cos_ref[where, :] - swapped(u) * sin_ref[where, :]).astype(LOW)
+
+        grad_ref[at, :width] = unturned(query_grad, at)
+
+        @pl.when(step == steps - 1)
+        def _():
+            everywhere = pl.ds(0, rows)
+            grad_ref[:, width : 2 * width] = unturned(key_sum[...].T, everywhere)
+            grad_ref[:, 2 * width :] = value_sum[...].T.astype(LOW)
+            keep_ref[...] = output_sum[:, : features // 2].T.astype(LOW)
+            give_ref[...] = output_sum[:, features // 2 :].T.astype(LOW)
+
+    def still(shape):
+        return pl.BlockSpec(shape, lambda i: (0,) * len(shape), pipeline_mode=pl.Buffered(1))
+
+    def whole(shape):
+        return pl.BlockSpec(shape, lambda i: (0,) * len(shape))
+
+    moving = pl.BlockSpec((block, width), lambda i: (i, 0))
+    half = (features // 2, width)
+    return pl.pallas_call(
+        kernel,
+        grid=(steps,),
+        out_shape=[
+            jax.ShapeDtypeStruct((rows, 3 * width), LOW),
+            jax.ShapeDtypeStruct(half, LOW),
+            jax.ShapeDtypeStruct(half, LOW),
+        ],
+        in_specs=[pl.BlockSpec(memory_space=pltpu.HBM)] * len(pieces)
+        + [still(output.shape), moving, still((rows, width)), still((rows, width))]
+        + [moving, moving, moving, still((rows, width)), still((rows, width))]
+        + [pl.BlockSpec((block, 1), lambda i: (i, 0)), still((1, rows))],
+        out_specs=[whole((rows, 3 * width)), whole(half), whole(half)],
+        scratch_shapes=[
+            pltpu.VMEM((rows, features), LOW),
+            pltpu.VMEM((width, rows), f32),
+            pltpu.VMEM((width, rows), f32),
+            pltpu.VMEM((width, features), f32),
+            pltpu.SemaphoreType.DMA((len(pieces),)),
+        ],
+        compiler_params=pltpu.CompilerParams(
+            dimension_semantics=("arbitrary",), vmem_limit_bytes=32 << 20
+        ),
+        cost_estimate=pl.CostEstimate(
+            flops=4 * rows * features * width + 20 * rows * rows * width,
+            transcendentals=2 * rows * rows,
+            bytes_accessed=2 * rows * features + 24 * rows * width,
+        ),
+    )(*(in_main(a) for a in (*pieces, output, queries, keys, values, mixed, numerator, total, *places)))
+
+
+def turned_pieces(value):
+    total, rows, columns = value.shape
+
+    def kernel(value_ref, out_ref):
+        out_ref[0] = value_ref[0].T
+
+    size = value.size * value.dtype.itemsize
+    return pl.pallas_call(
+        kernel,
+        grid=(total,),
+        out_shape=jax.ShapeDtypeStruct((total, columns, rows), value.dtype),
+        in_specs=[pl.BlockSpec((1, rows, columns), lambda i: (i, 0, 0))],
+        out_specs=pl.BlockSpec((1, columns, rows), lambda i: (i, 0, 0)),
+        cost_estimate=pl.CostEstimate(flops=0, transcendentals=0, bytes_accessed=2 * size),
+    )(value)
+
+
+def place_rows(pieces, places, dtype):
+    count, features = pieces[0].shape
+
+    def kernel(at_ref, *refs):
+        for i, ref in enumerate(refs[:-1]):
+            first = pl.multiple_of(at_ref[i] * count, count)
+            refs[-1][pl.ds(first, count), :] = ref[...].astype(dtype)
+
+    whole = pl.BlockSpec(memory_space=pltpu.VMEM)
+    shape = jax.ShapeDtypeStruct((len(pieces) * count, features), dtype)
+    return pl.pallas_call(
+        kernel,
+        out_shape=shape,
+        in_specs=[pl.BlockSpec(memory_space=pltpu.SMEM)] + [whole] * len(pieces),
+        out_specs=whole,
+        cost_estimate=pl.CostEstimate(
+            flops=0, transcendentals=0, bytes_accessed=6 * shape.size
+        ),
+    )(places, *pieces)
+
+
+def both_of(one, two, start, stop):
+    return one[start:stop].astype(jnp.float32) + two[start:stop].astype(jnp.float32)
+
+
+class Stages:
+    def step(self, *flying):
+        names = [name for name in vars(self) if name not in flying]
+        for name, value in zip(names, tie(*(getattr(self, name) for name in names))):
+            setattr(self, name, value)
+
+    def take(self, *names):
+        values = [getattr(self, name) for name in names]
+        for name in names:
+            delattr(self, name)
+        return values
+
+    def scatter_0(self, p, rows, rows_of):
+        setattr(self, p + "in", swap(rows_of(3), CORE))
+        setattr(self, p + "keep", rows_of(1))
+
+    def scatter_1(self, p, rows, rows_of):
+        count = rows // 16
+        keep, arrived = self.take(p + "keep", p + "in")
+        third, middle, first = (
+            both_of(keep, arrived, start * count, stop * count).astype(LOW)
+            for start, stop in ((3, 4), (1, 3), (0, 1))
+        )
+        setattr(self, p + "third", swap(third, X))
+        setattr(self, p + "middle", swap(middle, X))
+        setattr(self, p + "first", first)
+        setattr(self, p + "in", swap(rows_of(2), CORE))
+        setattr(self, p + "keep", rows_of(0))
+
+    def scatter_2(self, p):
+        first, third = self.take(p + "first", p + "third")
+        keep, arrived = getattr(self, p + "keep"), getattr(self, p + "in")
+        count = first.shape[0]
+        last = both_of(keep, arrived, 3 * count, 4 * count) + third.astype(jnp.float32)
+        setattr(self, p + "last", swap(last.astype(LOW), CTX, 1))
+        setattr(self, p + "first", swap(first, X))
+
+    def scatter_3(self, p):
+        middle, last = self.take(p + "middle", p + "last")
+        keep, arrived = getattr(self, p + "keep"), getattr(self, p + "in")
+        count = last.shape[0]
+        far = both_of(keep, arrived, 2 * count, 3 * count) + last.astype(jnp.float32)
+        far = far + middle[count:].astype(jnp.float32)
+        near = both_of(keep, arrived, count, 2 * count) + middle[:count].astype(jnp.float32)
+        setattr(self, p + "far", swap(far.astype(LOW), CTX, 2))
+        setattr(self, p + "near", swap(near.astype(LOW), CTX, 1))
+
+    def scatter_4(self, p):
+        keep, arrived, *values = self.take(
+            p + "keep", p + "in", p + "first", p + "near", p + "far"
+        )
+        total = both_of(keep, arrived, 0, values[0].shape[0])
+        return total + sum(value.astype(jnp.float32) for value in values)
+
+    def gather_0(self, shard):
+        self.g0 = shard
+        self.g1, self.g2 = swap(shard, CTX, 1), swap(shard, CTX, 2)
+        self.x0, self.c0 = swap(shard, X), swap(shard, CORE)
+
+    def gather_1(self):
+        self.g3 = swap(self.g2, CTX, 1)
+        self.x1, self.x2 = swap(self.g1, X), swap(self.g2, X)
+
+    def gather_2(self):
+        self.x3 = swap(self.g3, X)
+        self.c1, self.c2, self.c3 = (swap(g, CORE) for g in (self.g1, self.g2, self.g3))
+        self.c4 = swap(self.x0, CORE)
+
+    def gather_3(self):
+        self.c5, self.c6, self.c7 = (swap(x, CORE) for x in (self.x1, self.x2, self.x3))
+        names = [k + str(j) for k in "gx" for j in range(4)] + ["c" + str(j) for j in range(8)]
+        return self.take(*names)
+
+
+def spread(pieces):
+    return lax.all_to_all(pieces, CTX, 0, 0, tiled=True)
+
+
+def side_by_side(pieces):
+    return jnp.concatenate(list(pieces), axis=1)
+
+
+def by_columns(weight, extent):
+    return jnp.stack([weight[:, j * extent : (j + 1) * extent] for j in range(4)])
+
+
+def both(own):
+    return jnp.concatenate([own, swap(own, SEQ)])
+
+
+def halves(left, right):
+    grad = contract_rows(left, right).astype(LOW)
+    half = grad.shape[0] // 2
+    return grad[:half], grad[half:]
+
+
+def added(keep, arrived):
+    return (keep.astype(jnp.float32) + arrived.astype(jnp.float32)).astype(LOW)
+
+
+def fast_device(
+    tokens,
+    query_weight,
+    key_weight,
+    value_weight,
+    output_weight,
+    gate_weight,
+    up_weight,
+    down_weight,
+    attention_gain,
+    feedforward_gain,
+    order,
+    cotangent,
+):
+    f32 = jnp.float32
+    seq, ctx = lax.axis_index(SEQ), lax.axis_index(CTX)
+    x, core = lax.axis_index(X), lax.axis_index(CORE)
+    local_rows = tokens.shape[0]
+    count = local_rows // 4
+    rows = 16 * count
+    width = query_weight.shape[1] // 4
+    unit = gate_weight.shape[1] // 4
+    depth = query_weight.shape[0]
+
+    def turned(values):
+        middle_column = values.shape[1] // 2
+        other_way = jnp.concatenate([values[:, middle_column:], values[:, :middle_column]], axis=1)
+        return jnp.where(seq == 0, values, other_way)
+
+    own_places = jnp.stack([(x ^ a) * 2 + (core ^ b) for b in range(2) for a in range(2)])
+
+    def local(values, a, b):
+        return lax.dynamic_slice_in_dim(values, ((x ^ a) * 2 + (core ^ b)) * count, count, 0)
+
+    features = tokens.shape[1]
+    v = Stages()
+
+    qkv_pieces = first_pieces(
+        query_weight, key_weight, value_weight, attention_gain, feedforward_gain
+    )
+    v.qkv_own, v.tokens = tie(qkv_pieces, tokens)
+    v.qkv_own = spread(v.qkv_own)
+    v.tokens = turned(v.tokens)
+    shard = local(v.tokens, 0, 0)
+    v.g1, v.g2 = swap(shard, CTX, 1), swap(shard, CTX, 2)
+    v.cotangent, v.order = cotangent, order
+    v.gate, v.up, v.down, v.output = gate_weight, up_weight, down_weight, output_weight
+    v.step("qkv_own")
+
+    v.g3, v.x1, v.x2 = swap(v.g2, CTX, 1), swap(v.g1, X), swap(v.g2, X)
+    v.output = v.output.reshape(4, width, depth)
+    blocks = jnp.arange(16, dtype=jnp.int32)
+    stored = (
+        (ctx ^ (blocks & 3)) * local_rows
+        + (x ^ ((blocks >> 2) & 1)) * (2 * count)
+        + (core ^ (blocks >> 3)) * count
+    )
+    stored = (stored[:, None] + jnp.arange(count, dtype=jnp.int32)[None, :]).reshape(-1)
+    slots = jnp.arange(order.shape[0], dtype=jnp.int32)
+    places = jnp.sum(
+        jnp.where((stored // BLOCK)[:, None] == slots[None, :], v.order[None, :], 0), axis=1
+    )
+    places = places * BLOCK + stored % BLOCK
+    v.column, v.line = places[:, None], places[None, :]
+    entry = jnp.arange(width, dtype=jnp.int32) % (HD // 2)
+    inverse = THETA ** (-(entry.astype(f32) * 2.0) / HD)
+    sign = jnp.where(jnp.arange(width) % HD < HD // 2, -1.0, 1.0).astype(f32)
+    angle = places.astype(f32)[:, None] * inverse[None, :]
+    v.cosine, v.sine = jnp.cos(angle), jnp.sin(angle) * sign[None, :]
+    del v.order
+    v.step("qkv_own", "x1", "x2")
+
+    v.x3 = swap(v.g3, X)
+    v.cotangent = turned(v.cotangent)
+    v.shard = local(v.cotangent, 0, 0)
+    v.up = by_columns(v.up, unit)
+    v.step("x3")
+
+    v.qkv_o = swap(v.qkv_own, SEQ)
+    v.output = spread(v.output)
+    v.down = turned_pieces(v.down.reshape(4, unit, depth))
+    v.c1, v.c2, v.c3 = (swap(g, CORE) for g in (v.g1, v.g2, v.g3))
+    v.c4, v.c5 = swap(v.x1, CORE), swap(v.x2, CORE)
+    v.step("qkv_o")
+
+    def whole(values, line, line_x, other, other_x):
+        return stack_rows(
+            [None, *line, None, *line_x, None, *other, None, *other_x], values, own_places
+        )
+
+    v.d1, v.d2 = swap(v.shard, CTX, 1), swap(v.shard, CTX, 2)
+    v.gate = spread(by_columns(v.gate, unit))
+    del v.shard
+    v.c6 = swap(v.x3, CORE)
+    v.step("gate", "d1", "d2")
+
+    v.gain_first, v.gain_second = (
+        jnp.concatenate([half[:, depth + i, :depth] for half in (v.qkv_own, v.qkv_o)])
+        .reshape(1, 8 * depth)
+        .astype(f32)
+        for i in range(2)
+    )
+    g1, g2, g3, x1, x2, x3 = v.take("g1", "g2", "g3", "x1", "x2", "x3")
+    c1, c2, c3, c4, c5, c6 = v.take("c1", "c2", "c3", "c4", "c5", "c6")
+    outputs = attention(
+        [None, g1, g2, g3, None, x1, x2, x3, None, c1, c2, c3, None, c4, c5, c6],
+        v.tokens,
+        own_places,
+        v.qkv_own,
+        v.qkv_o,
+        v.cosine,
+        v.sine,
+        v.column,
+        v.line,
+    )
+    v.normed, v.queries, v.keys, v.values, v.mixed, v.numerator, v.total = outputs
+    v.output_other = swap(v.output, SEQ)
+    v.step("gate")
+
+    def attended(index):
+        return v.take("part%d" % index)[0]
+
+    v.e1, v.e2 = swap(v.d1, X), swap(v.d2, X)
+    v.part0, v.part1, v.part2, v.part3 = project(v.mixed, [v.output, v.output_other])
+    v.scatter_0("s_", rows, attended)
+    v.step("e1", "e2")
+    v.up = spread(v.up)
+    v.gate_o = swap(v.gate, SEQ)
+    v.scatter_1("s_", rows, attended)
+    v.d3 = swap(v.d2, CTX, 1)
+    v.f1, v.f2 = swap(v.d1, CORE), swap(v.d2, CORE)
+    v.step("up", "gate_o", "d3", "s_middle")
+    v.scatter_2("s_")
+    v.step("s_first")
+    v.scatter_3("s_")
+    v.up_o = swap(v.up, SEQ)
+    v.e3, v.f3 = swap(v.d3, X), swap(v.d3, CORE)
+    v.step("up_o", "e3")
+    v.down = spread(v.down)
+    v.middle = local(v.tokens, 0, 0).astype(f32) + v.scatter_4("s_")
+    v.scale_second = lax.rsqrt(jnp.mean(v.middle * v.middle, axis=1, keepdims=True) + EPS)
+    v.gather_0((v.middle * v.scale_second * v.gain_second).astype(LOW))
+    v.f4, v.f5, v.f6 = (swap(e, CORE) for e in (v.e1, v.e2, v.e3))
+    v.step("x0", "up_o")
+    v.gather_1()
+    v.down_o = swap(v.down, SEQ)
+    d1, d2, d3, e1, e2, e3 = v.take("d1", "d2", "d3", "e1", "e2", "e3")
+    f1, f2, f3, f4, f5, f6 = v.take("f1", "f2", "f3", "f4", "f5", "f6")
+    v.every_cotangent = whole(v.cotangent, [d1, d2, d3], [e1, e2, e3], [f1, f2, f3], [f4, f5, f6])
+    v.step("x1", "x2", "down_o")
+    v.gather_2()
+    v.output_full = side_by_side(jnp.concatenate(v.take("output", "output_other")))
+    v.gate_full = jnp.concatenate([v.gate, v.gate_o]).reshape(8 * depth, unit)
+    v.up_full = jnp.concatenate([v.up, v.up_o]).reshape(8 * depth, unit)
+    v.step("down_o")
+    pieces = v.gather_3()
+    for i, piece in enumerate(pieces):
+        setattr(v, "piece%d" % i, piece)
+    v.step()
+
+    v.normed_two, v.hidden, v.gate_grad, v.up_grad = feed_forward(
+        v.take(*("piece%d" % i for i in range(16))),
+        v.every_cotangent,
+        [own.reshape(4 * depth, unit) for own in v.take("gate", "gate_o")],
+        [own.reshape(4 * depth, unit) for own in v.take("up", "up_o")],
+        [own.reshape(4 * depth, unit) for own in (v.down, v.down_o)],
+    )
+    v.down_k, v.down_g = halves(v.every_cotangent, v.hidden)
+    del v.every_cotangent
+    v.step()
+
+    def quarter(values, index):
+        size = rows // 4
+        return values[index * size : (index + 1) * size]
+
+    def normed_grads(index):
+        gate, up = quarter(v.gate_grad, index), quarter(v.up_grad, index)
+        return (contract_cols(gate, v.gate_full) + contract_cols(up, v.up_full)).astype(LOW)
+
+    v.down_g = swap(v.down_g, SEQ)
+    v.scatter_0("s_", rows, normed_grads)
+    v.step("down_g")
+    v.scatter_1("s_", rows, normed_grads)
+    v.gate_k, v.gate_g = halves(v.normed_two, v.gate_grad)
+    v.step("down_g", "s_middle")
+    del v.gate_full, v.up_full
+    v.scatter_2("s_")
+    v.gate_g = swap(v.gate_g, SEQ)
+    v.up_k, v.up_g = halves(v.normed_two, v.up_grad)
+    v.step("s_first", "gate_g", "down_g")
+    del v.normed_two, v.gate_grad, v.up_grad
+    v.scatter_3("s_")
+    v.up_g = swap(v.up_g, SEQ)
+    v.down_full = jnp.concatenate(v.take("down", "down_o")).reshape(8 * depth, unit)
+    v.step("gate_g", "up_g")
+    normed_two_grad = v.scatter_4("s_")
+    middle, scale_second = v.middle, v.scale_second
+    scaled = normed_two_grad * v.gain_second
+    v.middle_grad = (
+        local(v.cotangent, 0, 0).astype(f32)
+        + scale_second * scaled
+        - middle * scale_second**3 * jnp.mean(scaled * middle, axis=1, keepdims=True)
+    )
+    del v.cotangent, v.scale_second, v.gain_second
+    v.gather_0(v.middle_grad.astype(LOW))
+    v.qkv_full = jnp.concatenate([v.qkv_own, v.qkv_o])[:, :depth].reshape(8 * depth, 3 * width)
+    del v.qkv_own, v.qkv_o
+    v.step("gate_g", "up_g", "x0")
+    v.gather_1()
+    v.step("up_g", "x1", "x2")
+
+    def fed(index):
+        return contract_cols(quarter(v.hidden, index), v.down_full).astype(LOW)
+
+    def projected_grads(index):
+        return contract_cols(quarter(v.projected_grad, index), v.qkv_full).astype(LOW)
+
+    v.gather_2()
+    v.down = spread(added(*v.take("down_k", "down_g")).reshape(4, depth, unit))
+    v.gate_sum = added(*v.take("gate_k", "gate_g")).reshape(4, depth, unit)
+    v.step("down", "up_g")
+    pieces = v.gather_3()
+    for i, piece in enumerate(pieces):
+        setattr(v, "piece%d" % i, piece)
+    v.step()
+
+    v.gate = spread(v.take("gate_sum")[0])
+    v.projected_grad, v.out_k, v.out_g = attention_back(
+        v.take(*("piece%d" % i for i in range(16))),
+        *v.take("output_full", "queries", "keys", "values", "mixed", "numerator", "total"),
+        *v.take("cosine", "sine", "column", "line"),
+    )
+    v.step("gate")
+    v.out_g = swap(v.out_g, SEQ)
+    v.scatter_0("s_", rows, projected_grads)
+    v.step("out_g")
+    v.scatter_1("s_", rows, projected_grads)
+    v.scatter_0("p_", rows, fed)
+    v.step("out_g", "s_middle")
+    v.scatter_2("s_")
+    v.up = spread(added(*v.take("up_k", "up_g")).reshape(4, depth, unit))
+    v.qkv_k, v.qkv_g = halves(v.normed, v.projected_grad)
+    del v.projected_grad, v.qkv_full, v.normed
+    v.scatter_1("p_", rows, fed)
+    v.step("up", "s_first", "p_middle")
+    del v.hidden, v.down_full
+    v.scatter_3("s_")
+    v.qkv_g = swap(v.qkv_g, SEQ)
+    v.scatter_2("p_")
+    v.down_wgrad = v.take("down")[0].transpose(0, 2, 1).reshape(4 * unit, depth).astype(f32)
+    v.step("p_first", "qkv_g")
+    v.scatter_3("p_")
+    sums = [added(*v.take(kind + "_k", kind + "_g")) for kind in ("qkv", "out")]
+    v.qkv_sum = jnp.concatenate(sums, axis=1).reshape(4, depth, 4 * width)
+    own_input = local(v.tokens, 0, 0).astype(f32)
+    normed_grad = v.scatter_4("s_")
+    scale_own = lax.rsqrt(jnp.mean(own_input * own_input, axis=1, keepdims=True) + EPS)
+    scaled = normed_grad * v.gain_first
+    input_grad = (
+        v.middle_grad
+        + scale_own * scaled
+        - own_input * scale_own**3 * jnp.mean(scaled * own_input, axis=1, keepdims=True)
+    )
+    v.input_grad = turned(input_grad.astype(LOW))
+    v.step()
+    v.qkv = spread(v.take("qkv_sum")[0])
+    v.produced = turned((v.take("middle")[0] + v.scatter_4("p_")).astype(LOW))
+    v.input_x, v.input_core = swap(v.input_grad, X), swap(v.input_grad, CORE)
+    v.produced_x, v.produced_core = swap(v.produced, X), swap(v.produced, CORE)
+    v.gate_wgrad = side_by_side(v.take("gate")[0]).astype(f32)
+    v.up_wgrad = side_by_side(v.take("up")[0]).astype(f32)
+    v.step("qkv")
+    v.input_far = swap(v.input_x, CORE)
+    v.produced_far = swap(v.produced_x, CORE)
+    v.step("qkv")
+    input_pieces = v.take("input_grad", "input_x", "input_core", "input_far")
+    v.input_out = place_rows(input_pieces, own_places, f32)
+    produced_pieces = v.take("produced", "produced_x", "produced_core", "produced_far")
+    v.block_output = place_rows(produced_pieces, own_places, LOW)
+    v.step()
+    block_output, input_grad = v.block_output, v.input_out
+    qkv_pieces, output_pieces = v.qkv[:, :, : 3 * width], v.qkv[:, :, 3 * width :]
+
+    query_wgrad, key_wgrad, value_wgrad = (
+        side_by_side(qkv_pieces[:, :, first : first + width]).astype(f32)
+        for first in (0, width, 2 * width)
+    )
+    gate_wgrad, up_wgrad = v.gate_wgrad, v.up_wgrad
+
+    def gain_grad(gain, *pairs):
+        part = sum(jnp.sum(w.astype(f32) * g, axis=1) for w, g in pairs)
+        return part / gain.astype(f32)
+
+    gain_grads = jnp.stack(
+        [
+            gain_grad(
+                attention_gain,
+                (query_weight, query_wgrad),
+                (key_weight, key_wgrad),
+                (value_weight, value_wgrad),
+            ),
+            gain_grad(feedforward_gain, (gate_weight, gate_wgrad), (up_weight, up_wgrad)),
+        ]
+    )
+    gain_grads = gain_grads + swap(gain_grads, CORE)
+    gain_grads = gain_grads + swap(gain_grads, X)
+    return (
+        block_output,
+        input_grad,
+        query_wgrad,
+        key_wgrad,
+        value_wgrad,
+        output_pieces.transpose(0, 2, 1).reshape(4 * width, depth).astype(f32),
+        gate_wgrad,
+        up_wgrad,
+        v.down_wgrad,
+        gain_grads[0],
+        gain_grads[1],
+    )
+
+
+def fast_solution(mesh):
+    sizes = mesh.shape
+    lines = Mesh(
+        mesh.devices.reshape(sizes[SEQ], sizes[CTX], 2, 2), (SEQ, CTX, X, CORE)
+    )
+    rows, heads = (SEQ, CTX), (X, CORE)
+    wide, tall = P(rows, heads), P(heads, rows)
+    return jax.shard_map(
+        fast_device,
+        mesh=lines,
+        in_specs=(
+            P(rows, None),
+            wide,
+            wide,
+            wide,
+            tall,
+            wide,
+            wide,
+            tall,
+            P(rows),
+            P(rows),
+            P(),
+            P(rows, None),
+        ),
+        out_specs=(
+            P(rows, None),
+            P(rows, None),
+            wide,
+            wide,
+            wide,
+            tall,
+            wide,
+            wide,
+            tall,
+            P(rows),
+            P(rows),
+        ),
+        check_vma=False,
+    )
+
+
+def solution(mesh):
+    sizes = mesh.shape
+    if mesh.axis_names == (SEQ, CTX, TP) and tuple(sizes.values()) == (2, 4, 4):
+        return fast_solution(mesh)
+    return general_solution(mesh)

time: 1760 us -> 496 us (0.28)
  waiting for transfers between devices: 1470 us -> 207 us
  starting transfers between devices: 5.36 us -> 119 us
  matrix products: 106 us -> 26 us
  blocking collectives: 62.2 us -> 0 us
  Pallas kernels: 0 us -> 54.5 us
    reduce_scatter x7 -> x0, waiting for transfers between devices: 698 us -> none  [the longest x1 150 us: per_device(): lax.psum_scatter(gate_wgrad.astype(jnp.bfloat16), ('seq', 'ctx'), scatter...]
    all_gather x8 -> x0, waiting for transfers between devices: 547 us -> none  [the longest x1 125 us: per_device(): lax.all_gather(gate_weight, ('seq', 'ctx'), axis=0, tiled=True)]
    psum x3 -> x0, waiting for transfers between devices: 83 us -> none  [the longest x1 40.2 us: per_device(): lax.psum(contract_cols(gate_grad, back_gate) + contract_cols(upward_grad,...]
    ppermute x8 -> x104, starting transfers between devices: 4.17 us -> 72.2 us  [swap(): return lax.ppermute(value, axis, pairs)]
    dot_general x35 -> x0, matrix products: 55.5 us -> none  [the longest x7 32.1 us: product(): return jnp.dot(left, right, preferred_element_type=jnp.float32)]
    pallas_call x0 -> x9, Pallas kernels: none -> 54.5 us  [the longest x1 12.6 us: attention(): pl.pallas_call(kernel, grid=(2 * steps,), out_shape=[pltpu.HBM((rows, fea...]
    ppermute x8 -> x104, waiting for transfers between devices: 135 us -> 185 us  [swap(): return lax.ppermute(value, axis, pairs)]
    all_to_all x0 -> x9, starting transfers between devices: none -> 46.5 us  [spread(): return lax.all_to_all(pieces, CTX, 0, 0, tiled=True)]
  transfers between devices with their start and end apart: 26 -> 113, of which waited for: 22 -> 48; matrix products, arithmetic and copies ran while one was open for 7% -> 17% of each run, Pallas kernels for 0% -> 9%
where the time goes in v2:
time: 496 us; the launch traced here: 492 us
  waiting for transfers between devices  207 us (42%)
  starting transfers between devices  119 us (24%)
  other arithmetic  54.6 us (11%)
  Pallas kernels  54.5 us (11%)
  local copies, waits for them, and re-layouts  28.7 us (6%)
  matrix products  26 us (5%)
    ppermute x104, waiting for transfers between devices, swap(): return lax.ppermute(value, axis, pairs)  185 us
    ppermute x104, starting transfers between devices, swap(): return lax.ppermute(value, axis, pairs)  72.2 us
    all_to_all x9, starting transfers between devices, spread(): return lax.all_to_all(pieces, CTX, 0, 0, tiled=True)  46.5 us
    all_to_all x9, waiting for transfers between devices, spread(): return lax.all_to_all(pieces, CTX, 0, 0, tiled=True)  21.8 us
    dot_general x16, matrix products, contract_cols(): lax.dot_general(left, right, (((1,), (1,)), ((), ())), preferred_element_...  16 us
    unnamed x235, local copies, waits for them, and re-layouts  14.3 us
    pallas_call x1, Pallas kernels, attention(): pl.pallas_call(kernel, grid=(2 * steps,), out_shape=[pltpu.HBM((rows, fea...  12.6 us
    pallas_call x1, Pallas kernels, attention_back(): pl.pallas_call(kernel, grid=(steps,), out_shape=[jax.ShapeDtypeStruct((ro...  12.4 us
  transfers between devices with their start and end apart: 113, of which 48 were waited for; matrix products, arithmetic and copies ran while one was open for 17% of the time, Pallas kernels for 9%

profile of v2, /device:TPU:0, one launch (start us, length us, event | category | flops | bytes accessed | tf_op | source)
XLA Modules:
  0.0 492.1 jit_solution(1900947220527367702)
XLA Ops:
  0.7 2.2 shard_map.203
  4.4 4.1 collective-permute-start.1
  10.1 3.5 all-to-all-start
  14.3 7.8 %collective-permute-done.1.refs_1_ = bf16[64,2048]{1,0:T(8,128)(2,1)S(1)} collective-permute-done((bf16[64,2048]{1,0:T(8,128)(2,1)S(1)}, bf16[64,2048]{1,0:T(8,128)(2,1)S(1)}, u32[]{:S(2)}, u32[]{:S(2)}) %collective-permute-start.1) | collective-permute-done | bytes 262176 | tf_op jit(solution)/shard_map/ppermute | solution.py:352
  23.0 3.7 collective-permute-start.4
  27.8 3.0 fusion.4
  31.8 8.0 %collective-permute-done.2.refs_2_ = bf16[64,2048]{1,0:T(8,128)(2,1)} collective-permute-done((bf16[64,2048]{1,0:T(8,128)(2,1)S(1)}, bf16[64,2048]{1,0:T(8,128)(2,1)}, u32[]{:S(2)}, u32[]{:S(2)}) %collective-permute-start.2) | collective-permute-done | bytes 262176 | tf_op jit(solution)/shard_map/ppermute | solution.py:352
  45.6 3.8 all-to-all-start.1
  50.7 3.6 shard_map.204
  54.4 4.3 all-to-all-done.1.own_ref
  63.0 3.7 all-to-all-start.2
  67.5 12.6 %shard_map.205 = (bf16[1024,2048]{1,0:T(8,128)(2,1)}, bf16[1024,128]{1,0:T(8,128)(2,1)}, bf16[1024,128]{1,0:T(8,128)(2,1)}, bf16[1024,128]{1,0:T(8,128)(2,1)}, b...) custom-call(s32[4]{0:T(128)S(1)} %pad_add_fusion.at_ref.refs_0_, ...), custom_call_target="tpu_custom_call" | custom-call | flops 2684354560 | bytes 14155776 | tf_op jit(solution)/shard_map/pallas_call | solution.py:601
  80.9 3.5 shard_map.206
  84.5 9.6 %all-to-all-done.2 = bf16[4,256,512]{2,1,0:T(8,128)(2,1)S(1)} async-done(((bf16[4,256,512]{2,1,0:T(8,128)(2,1)}), bf16[4,256,512]{2,1,0:T(8,128)(2,1)S(1)}, u32[]{:S(2)}, u32[]{:S(2)}) %all-to-all-start.2) | async-done | bytes 1048608 | tf_op jit(solution)/shard_map/all_to_all | solution.py:881
  96.2 3.5 all-to-all-start.3
  104.1 5.2 %collective-permute-done.18.refs_5_ = bf16[64,2048]{1,0:T(8,128)(2,1)} collective-permute-done((bf16[64,2048]{1,0:T(8,128)(2,1)}, bf16[64,2048]{1,0:T(8,128)(2,1)}, u32[]{:S(2)}, u32[]{:S(2)}) %collective-permute-start.18) | collective-permute-done | bytes 262176 | tf_op jit(solution)/shard_map/ppermute | solution.py:352
  111.7 3.1 collective-permute-done.19
  116.6 7.0 %collective-permute-done.25.refs_3_ = bf16[64,2048]{1,0:T(8,128)(2,1)S(1)} collective-permute-done((bf16[64,2048]{1,0:T(8,128)(2,1)}, bf16[64,2048]{1,0:T(8,128)(2,1)S(1)}, u32[]{:S(2)}, u32[]{:S(2)}) %collective-permute-start.25) | collective-permute-done | bytes 262176 | tf_op jit(solution)/shard_map/ppermute | solution.py:352
  123.6 2.4 collective-permute-done.24
  126.0 7.5 %collective-permute-done.23 = bf16[4,256,512]{2,1,0:T(8,128)(2,1)S(1)} collective-permute-done((bf16[4,256,512]{2,1,0:T(8,128)(2,1)S(1)}, bf16[4,256,512]{2,1,0:T(8,128)(2,1)S(1)}, u32[]{:S(2)}, u32[]{:S(2)}) %collective-permute-start.23) | collective-permute-done | bytes 1048608 | tf_op jit(solution)/shard_map/ppermute | solution.py:352
  136.8 2.6 collective-permute-start.28
  139.4 11.1 %collective-permute-done.29 = bf16[64,2048]{1,0:T(8,128)(2,1)S(1)} collective-permute-done((bf16[64,2048]{1,0:T(8,128)(2,1)S(1)}, bf16[64,2048]{1,0:T(8,128)(2,1)S(1)}, u32[]{:S(2)}, u32[]{:S(2)}) %collective-permute-start.29) | collective-permute-done | bytes 262176 | tf_op jit(solution)/shard_map/ppermute | solution.py:352
  152.3 15.0 %all-to-all-start.4 = ((bf16[4,256,512]{2,1,0:T(8,128)(2,1)}), bf16[4,256,512]{2,1,0:T(8,128)(2,1)S(1)}, u32[]{:S(2)}, u32[]{:S(2)}) async-start(bf16[4,256,512]{2,1,0:T(8,128)(2,1)} %shard_map.204), calls=%async_computation.4 | async-start | bytes 2097152 | tf_op jit(solution)/shard_map/all_to_all | solution.py:881
  170.7 4.8 collective-permute-done.31.refs_6_
  177.1 2.3 collective-permute-start.33
  181.4 22.7 %collective-permute-done.33.refs_2_ = bf16[64,2048]{1,0:T(8,128)(2,1)S(1)} collective-permute-done((bf16[64,2048]{1,0:T(8,128)(2,1)}, bf16[64,2048]{1,0:T(8,128)(2,1)S(1)}, u32[]{:S(2)}, u32[]{:S(2)}) %collective-permute-start.33) | collective-permute-done | bytes 262176 | tf_op jit(solution)/shard_map/ppermute | solution.py:352
  207.6 4.9 %shard_map.207.refs_16_ = bf16[1024,2048]{1,0:T(8,128)(2,1)} custom-call(s32[4]{0:T(128)} %copy-done.9, bf16[64,2048]{1,0:T(8,128)(2,1)} %collective-permute-done.13.refs_1_, bf16[64,2048]{1,0:T(8,128)(2,1)} %collective-permute-done.14.refs_2_, bf16[64,2048]{1,0:T(8,128)(2,1)} %copy-done.57, bf16[64,2048]{1,0:T(8,128)(2,1)} %copy-done.52, ...), custom_call_target="tpu_custom_call" | custom-call | bytes 8388608 | tf_op jit(solution)/shard_map/pallas_call | solution.py:393
  221.5 4.1 collective-permute-done.43.refs_7_
  227.9 8.3 %collective-permute-done.48 = bf16[4,256,512]{2,1,0:T(8,128)(2,1)S(1)} collective-permute-done((bf16[4,256,512]{2,1,0:T(8,128)(2,1)S(1)}, bf16[4,256,512]{2,1,0:T(8,128)(2,1)S(1)}, u32[]{:S(2)}, u32[]{:S(2)}) %collective-permute-start.48) | collective-permute-done | bytes 1048608 | tf_op jit(solution)/shard_map/ppermute | solution.py:352
  236.3 10.1 %shard_map.208 = (bf16[1024,2048]{1,0:T(8,128)(2,1)S(1)}, bf16[1024,512]{1,0:T(8,128)(2,1)S(1)}, bf16[1024,512]{1,0:T(8,128)(2,1)S(1)}, bf16[1024,512]{1,0:T(8,128)(2,1)S(1)}) custom-call(bf16[64,2048]{1,0:T(8,128)(2,1)} %multiply_convert_fusion.refs_0_, bf16[64,2048]{1,0:T(8,128)(2,1)} %copy-done.86, bf16[64,2048]{1,0:T(8,128)(2,1)} %copy-done.84, ...), custom_call_target="tpu_custom_call" | custom-call | flops 6442450944 | bytes 22020096 | tf_op jit(solution)/shard_map/pallas_call | solution.py:478
  246.5 2.4 convolution_convert_fusion.2
  258.7 2.4 convolution_convert_fusion.1
  266.7 2.8 convolution_convert_fusion
  271.0 4.5 collective-permute-done.55
  280.3 6.5 %collective-permute-done.60 = bf16[64,2048]{1,0:T(8,128)(2,1)S(1)} collective-permute-done((bf16[64,2048]{1,0:T(8,128)(2,1)S(1)}, bf16[64,2048]{1,0:T(8,128)(2,1)S(1)}, u32[]{:S(2)}, u32[]{:S(2)}) %collective-permute-start.60) | collective-permute-done | bytes 262176 | tf_op jit(solution)/shard_map/ppermute | solution.py:352
  286.7 3.8 collective-permute-done.59
  290.9 2.3 fusion.46
  294.7 12.4 %collective-permute-done.62.refs_2_ = bf16[64,2048]{1,0:T(8,128)(2,1)S(1)} collective-permute-done((bf16[64,2048]{1,0:T(8,128)(2,1)S(1)}, bf16[64,2048]{1,0:T(8,128)(2,1)S(1)}, u32[]{:S(2)}, u32[]{:S(2)}) %collective-permute-start.62) | collective-permute-done | bytes 262176 | tf_op jit(solution)/shard_map/ppermute | solution.py:352
  307.9 7.5 %collective-permute-done.66.refs_3_ = bf16[64,2048]{1,0:T(8,128)(2,1)S(1)} collective-permute-done((bf16[64,2048]{1,0:T(8,128)(2,1)S(1)}, bf16[64,2048]{1,0:T(8,128)(2,1)S(1)}, u32[]{:S(2)}, u32[]{:S(2)}) %collective-permute-start.66) | collective-permute-done | bytes 262176 | tf_op jit(solution)/shard_map/ppermute | solution.py:352
  316.7 3.5 all-to-all-start.5
  323.8 6.7 %collective-permute-done.67.refs_5_ = bf16[64,2048]{1,0:T(8,128)(2,1)S(1)} collective-permute-done((bf16[64,2048]{1,0:T(8,128)(2,1)S(1)}, bf16[64,2048]{1,0:T(8,128)(2,1)S(1)}, u32[]{:S(2)}, u32[]{:S(2)}) %collective-permute-start.67) | collective-permute-done | bytes 262176 | tf_op jit(solution)/shard_map/ppermute | solution.py:352
  331.1 5.1 %collective-permute-done.68.refs_6_ = bf16[64,2048]{1,0:T(8,128)(2,1)S(1)} collective-permute-done((bf16[64,2048]{1,0:T(8,128)(2,1)S(1)}, bf16[64,2048]{1,0:T(8,128)(2,1)S(1)}, u32[]{:S(2)}, u32[]{:S(2)}) %collective-permute-start.68) | collective-permute-done | bytes 262176 | tf_op jit(solution)/shard_map/ppermute | solution.py:352
  337.4 2.8 add_convert_fusion.2
  340.9 3.4 collective-permute-done.74
  347.1 4.7 all-to-all-start.6
  351.8 12.4 %shard_map.209 = (bf16[1024,384]{1,0:T(8,128)(2,1)S(1)}, bf16[1024,128]{1,0:T(8,128)(2,1)S(1)}, bf16[1024,128]{1,0:T(8,128)(2,1)S(1)}) custom-call(bf16[64,2048]{1,0:T(8,128)(2,1)} %copy-done.58, bf16[64,2048]{1,0:T(8,128)(2,1)} %copy-done.89, bf16[64,2048]{1,0:T(8,128)(2,1)} %copy-done.88, bf16[64,2048]{1,0:T(8,128)(2,1)} %copy-done.92, ...), custom_call_target="tpu_custom_call" | custom-call | flops 3758096384 | bytes 7340032 | tf_op jit(solution)/shard_map/pallas_call | solution.py:733
  367.8 7.8 %all-to-all-done.6 = bf16[4,256,512]{2,1,0:T(8,128)(2,1)} async-done(((bf16[4,256,512]{2,1,0:T(8,128)(2,1)}), bf16[4,256,512]{2,1,0:T(8,128)(2,1)}, u32[]{:S(2)}, u32[]{:S(2)}) %all-to-all-start.6) | async-done | bytes 1048608 | tf_op jit(solution)/shard_map/all_to_all | solution.py:881
  375.7 2.2 add_convert_fusion.18
  378.4 2.1 convolution_convert_fusion.9
  390.9 4.4 all-to-all-start.7
  395.4 2.5 convolution_convert_fusion.5
  398.8 2.4 convolution_convert_fusion.3
  408.7 2.2 add_convert_fusion.13
  411.0 2.9 collective-permute-start.89
  417.5 5.8 %collective-permute-done.88 = bf16[128,2048]{1,0:T(8,128)(2,1)} collective-permute-done((bf16[128,2048]{1,0:T(8,128)(2,1)}, bf16[128,2048]{1,0:T(8,128)(2,1)}, u32[]{:S(2)}, u32[]{:S(2)}) %collective-permute-start.88) | collective-permute-done | bytes 524320 | tf_op jit(solution)/shard_map/ppermute | solution.py:352
  424.3 7.4 %collective-permute-done.90 = bf16[64,2048]{1,0:T(8,128)(2,1)S(1)} collective-permute-done((bf16[64,2048]{1,0:T(8,128)(2,1)}, bf16[64,2048]{1,0:T(8,128)(2,1)S(1)}, u32[]{:S(2)}, u32[]{:S(2)}) %collective-permute-start.90) | collective-permute-done | bytes 262176 | tf_op jit(solution)/shard_map/ppermute | solution.py:352
  436.4 2.3 collective-permute-start.94
  444.7 4.2 collective-permute-done.94
  448.9 2.9 collective-permute-done.93
  452.6 4.4 all-to-all-start.8
  465.3 2.3 collective-permute-done.98.refs_1_
  467.6 5.2 %collective-permute-done.96.refs_1_ = bf16[64,2048]{1,0:T(8,128)(2,1)S(1)} collective-permute-done((bf16[64,2048]{1,0:T(8,128)(2,1)S(1)}, bf16[64,2048]{1,0:T(8,128)(2,1)S(1)}, u32[]{:S(2)}, u32[]{:S(2)}) %collective-permute-start.96) | collective-permute-done | bytes 262176 | tf_op jit(solution)/shard_map/ppermute | solution.py:352
  475.4 2.2 shard_map.211
  477.6 2.7 shard_map.210
  (521 shorter events, 151.7 us)
Async XLA Ops:
  4.4 17.8 %collective-permute-start.1 = (bf16[64,2048]{1,0:T(8,128)(2,1)S(1)}, bf16[64,2048]{1,0:T(8,128)(2,1)S(1)}, u32[]{:S(2)}, u32[]{:S(2)}) collective-permute-start(bf16[64,2048]{1,0:T(8,128)(2,1)S(1)} %constant_dynamic-slice_fusion.1), channel_id=1, source_target_pairs={{0,8},{4,12},{8,0},{12,4},{1,9},{5,13},{9,1},{13,5},{2,10},{6,14},... | collective-permute-start | bytes 786440 | tf_op jit(solution)/shard_map/ppermute | solution.py:352
  8.5 14.5 %collective-permute-start = (bf16[64,2048]{1,0:T(8,128)(2,1)S(1)}, bf16[64,2048]{1,0:T(8,128)(2,1)}, u32[]{:S(2)}, u32[]{:S(2)}) collective-permute-start(bf16[64,2048]{1,0:T(8,128)(2,1)S(1)} %constant_dynamic-slice_fusion.1), channel_id=1, source_target_pairs={{0,4},{4,0},{8,12},{12,8},{1,5},{5,1},{9,13},{13,9},{2,6},{6,2},{1... | collective-permute-start | bytes 786440 | tf_op jit(solution)/shard_map/ppermute | solution.py:352
  10.1 33.9 %all-to-all-start = ((bf16[4,272,384]{2,1,0:T(8,128)(2,1)}), bf16[4,272,384]{2,1,0:T(8,128)(2,1)S(1)}, u32[]{:S(2)}, u32[]{:S(2)}) async-start(bf16[4,272,384]{2,1,0:T(8,128)(2,1)} %shard_map.203), calls=%async_computation | async-start | bytes 1671168 | tf_op jit(solution)/shard_map/all_to_all | solution.py:881
  23.0 21.0 %collective-permute-start.4 = (bf16[64,2048]{1,0:T(8,128)(2,1)S(1)}, bf16[64,2048]{1,0:T(8,128)(2,1)S(1)}, u32[]{:S(2)}, u32[]{:S(2)}) collective-permute-start(bf16[64,2048]{1,0:T(8,128)(2,1)S(1)} %collective-permute-done.1.refs_1_), channel_id=1, source_target_pairs={{0,2},{2,0},{1,3},{3,1},{4,6},{6,4},{5,7},{7,5},{8,10},{10,8},{9,1... | collective-permute-start | bytes 786440 | tf_op jit(solution)/shard_map/ppermute | solution.py:352
  26.7 13.1 %collective-permute-start.2 = (bf16[64,2048]{1,0:T(8,128)(2,1)S(1)}, bf16[64,2048]{1,0:T(8,128)(2,1)}, u32[]{:S(2)}, u32[]{:S(2)}) collective-permute-start(bf16[64,2048]{1,0:T(8,128)(2,1)S(1)} %collective-permute-done.1.refs_1_), channel_id=1, source_target_pairs={{0,4},{4,0},{8,12},{12,8},{1,5},{5,1},{9,13},{13,9},{2,6},{6,2},{1... | collective-permute-start | bytes 786440 | tf_op jit(solution)/shard_map/ppermute | solution.py:352
  26.9 17.1 %collective-permute-start.3 = (bf16[64,2048]{1,0:T(8,128)(2,1)}, bf16[64,2048]{1,0:T(8,128)(2,1)}, u32[]{:S(2)}, u32[]{:S(2)}) collective-permute-start(bf16[64,2048]{1,0:T(8,128)(2,1)} %collective-permute-done.refs_0_), channel_id=1, source_target_pairs={{0,2},{2,0},{1,3},{3,1},{4,6},{6,4},{5,7},{7,5},{8,10},{10,8},{9,1... | collective-permute-start | bytes 786440 | tf_op jit(solution)/shard_map/ppermute | solution.py:352
  44.1 22.6 %collective-permute-start.11 = (bf16[4,272,384]{2,1,0:T(8,128)(2,1)S(1)}, bf16[4,272,384]{2,1,0:T(8,128)(2,1)S(1)}, u32[]{:S(2)}, u32[]{:S(2)}) collective-permute-start(bf16[4,272,384]{2,1,0:T(8,128)(2,1)S(1)} %all-to-all-done.refs_13_), channel_id=1, source_target_pairs={{0,16},{16,0},{1,17},{17,1},{2,18},{18,2},{3,19},{19,3},{4,20},{20... | collective-permute-start | bytes 2506760 | tf_op jit(solution)/shard_map/ppermute | solution.py:352
  45.6 13.0 %all-to-all-start.1 = ((bf16[4,128,256]{2,1,0:T(8,128)(2,1)}), bf16[4,128,256]{2,1,0:T(8,128)(2,1)S(1)}, u32[]{:S(2)}, u32[]{:S(2)}) async-start(bf16[4,128,256]{2,1,0:T(8,128)(2,1)} %bitcast), calls=%async_computation.1 | async-start | bytes 524288 | tf_op jit(solution)/shard_map/all_to_all | solution.py:881
  58.7 21.5 %collective-permute-start.14 = (bf16[64,2048]{1,0:T(8,128)(2,1)}, bf16[64,2048]{1,0:T(8,128)(2,1)}, u32[]{:S(2)}, u32[]{:S(2)}) collective-permute-start(bf16[64,2048]{1,0:T(8,128)(2,1)} %constant_dynamic-slice_fusion), channel_id=1, source_target_pairs={{0,8},{4,12},{8,0},{12,4},{1,9},{5,13},{9,1},{13,5},{2,10},{6,14},... | collective-permute-start | bytes 786440 | tf_op jit(solution)/shard_map/ppermute | solution.py:352
  58.7 21.5 %collective-permute-start.13 = (bf16[64,2048]{1,0:T(8,128)(2,1)}, bf16[64,2048]{1,0:T(8,128)(2,1)}, u32[]{:S(2)}, u32[]{:S(2)}) collective-permute-start(bf16[64,2048]{1,0:T(8,128)(2,1)} %constant_dynamic-slice_fusion), channel_id=1, source_target_pairs={{0,4},{4,0},{8,12},{12,8},{1,5},{5,1},{9,13},{13,9},{2,6},{6,2},{1... | collective-permute-start | bytes 786440 | tf_op jit(solution)/shard_map/ppermute | solution.py:352
  63.0 31.1 %all-to-all-start.2 = ((bf16[4,256,512]{2,1,0:T(8,128)(2,1)}), bf16[4,256,512]{2,1,0:T(8,128)(2,1)S(1)}, u32[]{:S(2)}, u32[]{:S(2)}) async-start(bf16[4,256,512]{2,1,0:T(8,128)(2,1)} %pad_maximum_fusion.5), calls=%async_computation.2 | async-start | bytes 2097152 | tf_op jit(solution)/shard_map/all_to_all | solution.py:881
  66.8 13.3 %collective-permute-start.15 = (bf16[4,128,256]{2,1,0:T(8,128)(2,1)S(1)}, bf16[4,128,256]{2,1,0:T(8,128)(2,1)S(1)}, u32[]{:S(2)}, u32[]{:S(2)}) collective-permute-start(bf16[4,128,256]{2,1,0:T(8,128)(2,1)S(1)} %all-to-all-done.1.own_ref), channel_id=1, source_target_pairs={{0,16},{16,0},{1,17},{17,1},{2,18},{18,2},{3,19},{19,3},{4,20},{20... | collective-permute-start | bytes 786440 | tf_op jit(solution)/shard_map/ppermute | solution.py:352
  94.1 20.6 %collective-permute-start.20 = (bf16[256,2048]{1,0:T(8,128)(2,1)}, bf16[256,2048]{1,0:T(8,128)(2,1)}, u32[]{:S(2)}, u32[]{:S(2)}) collective-permute-start(bf16[256,2048]{1,0:T(8,128)(2,1)} %get-tuple-element.982), channel_id=1, source_target_pairs={{0,1},{1,0},{2,3},{3,2},{4,5},{5,4},{6,7},{7,6},{8,9},{9,8},{10,11... | collective-permute-start | bytes 3145736 | tf_op jit(solution)/shard_map/ppermute | solution.py:352
  94.7 14.5 %collective-permute-start.18 = (bf16[64,2048]{1,0:T(8,128)(2,1)}, bf16[64,2048]{1,0:T(8,128)(2,1)}, u32[]{:S(2)}, u32[]{:S(2)}) collective-permute-start(bf16[64,2048]{1,0:T(8,128)(2,1)} %collective-permute-done.14.refs_2_), channel_id=1, source_target_pairs={{0,2},{2,0},{1,3},{3,1},{4,6},{6,4},{5,7},{7,5},{8,10},{10,8},{9,1... | collective-permute-start | bytes 786440 | tf_op jit(solution)/shard_map/ppermute | solution.py:352
  96.2 39.0 %all-to-all-start.3 = ((bf16[4,256,512]{2,1,0:T(8,128)(2,1)}), bf16[4,256,512]{2,1,0:T(8,128)(2,1)S(1)}, u32[]{:S(2)}, u32[]{:S(2)}) async-start(bf16[4,256,512]{2,1,0:T(8,128)(2,1)} %pad_maximum_fusion.4), calls=%async_computation.3 | async-start | bytes 2097152 | tf_op jit(solution)/shard_map/all_to_all | solution.py:881
  99.7 11.2 %collective-permute-start.21 = (bf16[64,2048]{1,0:T(8,128)(2,1)}, bf16[64,2048]{1,0:T(8,128)(2,1)S(1)}, u32[]{:S(2)}, u32[]{:S(2)}) collective-permute-start(bf16[64,2048]{1,0:T(8,128)(2,1)} %collective-permute-done.13.refs_1_), channel_id=1, source_target_pairs={{0,1},{1,0},{2,3},{3,2},{4,5},{5,4},{6,7},{7,6},{8,9},{9,8},{10,11... | collective-permute-start | bytes 786440 | tf_op jit(solution)/shard_map/ppermute | solution.py:352
  99.8 11.2 %collective-permute-start.22 = (bf16[64,2048]{1,0:T(8,128)(2,1)}, bf16[64,2048]{1,0:T(8,128)(2,1)S(1)}, u32[]{:S(2)}, u32[]{:S(2)}) collective-permute-start(bf16[64,2048]{1,0:T(8,128)(2,1)} %collective-permute-done.14.refs_2_), channel_id=1, source_target_pairs={{0,1},{1,0},{2,3},{3,2},{4,5},{5,4},{6,7},{7,6},{8,9},{9,8},{10,11... | collective-permute-start | bytes 786440 | tf_op jit(solution)/shard_map/ppermute | solution.py:352
  103.5 11.2 %collective-permute-start.19 = (bf16[64,2048]{1,0:T(8,128)(2,1)S(1)}, bf16[64,2048]{1,0:T(8,128)(2,1)S(1)}, u32[]{:S(2)}, u32[]{:S(2)}) collective-permute-start(bf16[64,2048]{1,0:T(8,128)(2,1)S(1)} %get-tuple-element.1694), channel_id=1, source_target_pairs={{0,2},{2,0},{1,3},{3,1},{4,6},{6,4},{5,7},{7,5},{8,10},{10,8},{9,1... | collective-permute-start | bytes 786440 | tf_op jit(solution)/shard_map/ppermute | solution.py:352
  109.2 24.3 %collective-permute-start.23 = (bf16[4,256,512]{2,1,0:T(8,128)(2,1)S(1)}, bf16[4,256,512]{2,1,0:T(8,128)(2,1)S(1)}, u32[]{:S(2)}, u32[]{:S(2)}) collective-permute-start(bf16[4,256,512]{2,1,0:T(8,128)(2,1)S(1)} %all-to-all-done.2), channel_id=1, source_target_pairs={{0,16},{16,0},{1,17},{17,1},{2,18},{18,2},{3,19},{19,3},{4,20},{20... | collective-permute-start | bytes 3145736 | tf_op jit(solution)/shard_map/ppermute | solution.py:352
  111.0 12.6 %collective-permute-start.25 = (bf16[64,2048]{1,0:T(8,128)(2,1)}, bf16[64,2048]{1,0:T(8,128)(2,1)S(1)}, u32[]{:S(2)}, u32[]{:S(2)}) collective-permute-start(bf16[64,2048]{1,0:T(8,128)(2,1)} %collective-permute-done.14.refs_2_), channel_id=1, source_target_pairs={{0,4},{4,0},{8,12},{12,8},{1,5},{5,1},{9,13},{13,9},{2,6},{6,2},{1... | collective-permute-start | bytes 786440 | tf_op jit(solution)/shard_map/ppermute | solution.py:352
  111.1 14.9 %collective-permute-start.24 = (bf16[128,2048]{1,0:T(8,128)(2,1)S(1)}, bf16[128,2048]{1,0:T(8,128)(2,1)S(1)}, u32[]{:S(2)}, u32[]{:S(2)}) collective-permute-start(bf16[128,2048]{1,0:T(8,128)(2,1)S(1)} %add_convert_fusion.7), channel_id=1, source_target_pairs={{0,2},{2,0},{1,3},{3,1},{4,6},{6,4},{5,7},{7,5},{8,10},{10,8},{9,1... | collective-permute-start | bytes 1572872 | tf_op jit(solution)/shard_map/ppermute | solution.py:352
  115.9 18.6 %collective-permute-start.26 = (bf16[64,2048]{1,0:T(8,128)(2,1)S(1)}, bf16[64,2048]{1,0:T(8,128)(2,1)S(1)}, u32[]{:S(2)}, u32[]{:S(2)}) collective-permute-start(bf16[64,2048]{1,0:T(8,128)(2,1)S(1)} %add_convert_fusion.27), channel_id=1, source_target_pairs={{0,4},{4,0},{8,12},{12,8},{1,5},{5,1},{9,13},{13,9},{2,6},{6,2},{1... | collective-permute-start | bytes 786440 | tf_op jit(solution)/shard_map/ppermute | solution.py:352
  116.0 23.5 %collective-permute-start.27 = (bf16[64,2048]{1,0:T(8,128)(2,1)}, bf16[64,2048]{1,0:T(8,128)(2,1)}, u32[]{:S(2)}, u32[]{:S(2)}) collective-permute-start(bf16[64,2048]{1,0:T(8,128)(2,1)} %get-tuple-element.1047), channel_id=1, source_target_pairs={{0,2},{2,0},{1,3},{3,1},{4,6},{6,4},{5,7},{7,5},{8,10},{10,8},{9,1... | collective-permute-start | bytes 786440 | tf_op jit(solution)/shard_map/ppermute | solution.py:352
  136.7 13.8 %collective-permute-start.29 = (bf16[64,2048]{1,0:T(8,128)(2,1)S(1)}, bf16[64,2048]{1,0:T(8,128)(2,1)S(1)}, u32[]{:S(2)}, u32[]{:S(2)}) collective-permute-start(bf16[64,2048]{1,0:T(8,128)(2,1)S(1)} %get-tuple-element.1679), channel_id=1, source_target_pairs={{0,4},{4,0},{8,12},{12,8},{1,5},{5,1},{9,13},{13,9},{2,6},{6,2},{1... | collective-permute-start | bytes 786440 | tf_op jit(solution)/shard_map/ppermute | solution.py:352
  136.8 15.5 %collective-permute-start.28 = (bf16[64,2048]{1,0:T(8,128)(2,1)S(1)}, bf16[64,2048]{1,0:T(8,128)(2,1)}, u32[]{:S(2)}, u32[]{:S(2)}) collective-permute-start(bf16[64,2048]{1,0:T(8,128)(2,1)S(1)} %get-tuple-element.1680), channel_id=1, source_target_pairs={{0,8},{4,12},{8,0},{12,4},{1,9},{5,13},{9,1},{13,5},{2,10},{6,14},... | collective-permute-start | bytes 786440 | tf_op jit(solution)/shard_map/ppermute | solution.py:352
  152.3 52.6 %all-to-all-start.4 = ((bf16[4,256,512]{2,1,0:T(8,128)(2,1)}), bf16[4,256,512]{2,1,0:T(8,128)(2,1)S(1)}, u32[]{:S(2)}, u32[]{:S(2)}) async-start(bf16[4,256,512]{2,1,0:T(8,128)(2,1)} %shard_map.204), calls=%async_computation.4 | async-start | bytes 2097152 | tf_op jit(solution)/shard_map/all_to_all | solution.py:881
  167.9 45.3 %collective-permute-start.38 = (bf16[4,256,512]{2,1,0:T(8,128)(2,1)S(1)}, bf16[4,256,512]{2,1,0:T(8,128)(2,1)}, u32[]{:S(2)}, u32[]{:S(2)}) collective-permute-start(bf16[4,256,512]{2,1,0:T(8,128)(2,1)S(1)} %all-to-all-done.3), channel_id=1, source_target_pairs={{0,16},{16,0},{1,17},{17,1},{2,18},{18,2},{3,19},{19,3},{4,20},{20... | collective-permute-start | bytes 3145736 | tf_op jit(solution)/shard_map/ppermute | solution.py:352
  168.5 12.4 %collective-permute-start.36 = (bf16[64,2048]{1,0:T(8,128)(2,1)}, bf16[64,2048]{1,0:T(8,128)(2,1)S(1)}, u32[]{:S(2)}, u32[]{:S(2)}) collective-permute-start(bf16[64,2048]{1,0:T(8,128)(2,1)} %collective-permute-done.18.refs_5_), channel_id=1, source_target_pairs={{0,1},{1,0},{2,3},{3,2},{4,5},{5,4},{6,7},{7,6},{8,9},{9,8},{10,11... | collective-permute-start | bytes 786440 | tf_op jit(solution)/shard_map/ppermute | solution.py:352
  177.1 27.1 %collective-permute-start.33 = (bf16[64,2048]{1,0:T(8,128)(2,1)}, bf16[64,2048]{1,0:T(8,128)(2,1)S(1)}, u32[]{:S(2)}, u32[]{:S(2)}) collective-permute-start(bf16[64,2048]{1,0:T(8,128)(2,1)} %multiply_convert_fusion.refs_0_), channel_id=1, source_target_pairs={{0,8},{4,12},{8,0},{12,4},{1,9},{5,13},{9,1},{13,5},{2,10},{6,14},... | collective-permute-start | bytes 786440 | tf_op jit(solution)/shard_map/ppermute | solution.py:352
  179.4 25.5 %collective-permute-start.32 = (bf16[64,2048]{1,0:T(8,128)(2,1)}, bf16[64,2048]{1,0:T(8,128)(2,1)S(1)}, u32[]{:S(2)}, u32[]{:S(2)}) collective-permute-start(bf16[64,2048]{1,0:T(8,128)(2,1)} %multiply_convert_fusion.refs_0_), channel_id=1, source_target_pairs={{0,4},{4,0},{8,12},{12,8},{1,5},{5,1},{9,13},{13,9},{2,6},{6,2},{1... | collective-permute-start | bytes 786440 | tf_op jit(solution)/shard_map/ppermute | solution.py:352
  180.9 31.7 %collective-permute-start.39 = (bf16[64,2048]{1,0:T(8,128)(2,1)}, bf16[64,2048]{1,0:T(8,128)(2,1)}, u32[]{:S(2)}, u32[]{:S(2)}) collective-permute-start(bf16[64,2048]{1,0:T(8,128)(2,1)} %multiply_convert_fusion.refs_0_), channel_id=1, source_target_pairs={{0,2},{2,0},{1,3},{3,1},{4,6},{6,4},{5,7},{7,5},{8,10},{10,8},{9,1... | collective-permute-start | bytes 786440 | tf_op jit(solution)/shard_map/ppermute | solution.py:352
  205.6 13.8 %collective-permute-start.42 = (bf16[64,2048]{1,0:T(8,128)(2,1)}, bf16[64,2048]{1,0:T(8,128)(2,1)}, u32[]{:S(2)}, u32[]{:S(2)}) collective-permute-start(bf16[64,2048]{1,0:T(8,128)(2,1)} %copy-done.84), channel_id=1, source_target_pairs={{0,2},{2,0},{1,3},{3,1},{4,6},{6,4},{5,7},{7,5},{8,10},{10,8},{9,1... | collective-permute-start | bytes 786440 | tf_op jit(solution)/shard_map/ppermute | solution.py:352
  206.1 12.7 %collective-permute-start.41 = (bf16[64,2048]{1,0:T(8,128)(2,1)}, bf16[64,2048]{1,0:T(8,128)(2,1)}, u32[]{:S(2)}, u32[]{:S(2)}) collective-permute-start(bf16[64,2048]{1,0:T(8,128)(2,1)} %copy-done.86), channel_id=1, source_target_pairs={{0,2},{2,0},{1,3},{3,1},{4,6},{6,4},{5,7},{7,5},{8,10},{10,8},{9,1... | collective-permute-start | bytes 786440 | tf_op jit(solution)/shard_map/ppermute | solution.py:352
  212.6 23.7 %collective-permute-start.48 = (bf16[4,256,512]{2,1,0:T(8,128)(2,1)S(1)}, bf16[4,256,512]{2,1,0:T(8,128)(2,1)S(1)}, u32[]{:S(2)}, u32[]{:S(2)}) collective-permute-start(bf16[4,256,512]{2,1,0:T(8,128)(2,1)S(1)} %all-to-all-done.4), channel_id=1, source_target_pairs={{0,16},{16,0},{1,17},{17,1},{2,18},{18,2},{3,19},{19,3},{4,20},{20... | collective-permute-start | bytes 3145736 | tf_op jit(solution)/shard_map/ppermute | solution.py:352
  250.6 29.4 %collective-permute-start.57 = (bf16[1024,512]{1,0:T(8,128)(2,1)S(1)}, bf16[1024,512]{1,0:T(8,128)(2,1)S(1)}, u32[]{:S(2)}, u32[]{:S(2)}) collective-permute-start(bf16[1024,512]{1,0:T(8,128)(2,1)S(1)} %get-tuple-element.1362), channel_id=1, source_target_pairs={{0,16},{16,0},{1,17},{17,1},{2,18},{18,2},{3,19},{19,3},{4,20},{20... | collective-permute-start | bytes 3145736 | tf_op jit(solution)/shard_map/ppermute | solution.py:352
  255.6 19.9 %collective-permute-start.55 = (bf16[128,2048]{1,0:T(8,128)(2,1)S(1)}, bf16[128,2048]{1,0:T(8,128)(2,1)S(1)}, u32[]{:S(2)}, u32[]{:S(2)}) collective-permute-start(bf16[128,2048]{1,0:T(8,128)(2,1)S(1)} %add_convert_fusion.6), channel_id=1, source_target_pairs={{0,2},{2,0},{1,3},{3,1},{4,6},{6,4},{5,7},{7,5},{8,10},{10,8},{9,1... | collective-permute-start | bytes 1572872 | tf_op jit(solution)/shard_map/ppermute | solution.py:352
  266.2 14.1 %collective-permute-start.58 = (bf16[64,2048]{1,0:T(8,128)(2,1)S(1)}, bf16[64,2048]{1,0:T(8,128)(2,1)S(1)}, u32[]{:S(2)}, u32[]{:S(2)}) collective-permute-start(bf16[64,2048]{1,0:T(8,128)(2,1)S(1)} %get-tuple-element.1366), channel_id=1, source_target_pairs={{0,2},{2,0},{1,3},{3,1},{4,6},{6,4},{5,7},{7,5},{8,10},{10,8},{9,1... | collective-permute-start | bytes 786440 | tf_op jit(solution)/shard_map/ppermute | solution.py:352
  277.6 12.9 %collective-permute-start.59 = (bf16[64,2048]{1,0:T(8,128)(2,1)S(1)}, bf16[64,2048]{1,0:T(8,128)(2,1)S(1)}, u32[]{:S(2)}, u32[]{:S(2)}) collective-permute-start(bf16[64,2048]{1,0:T(8,128)(2,1)S(1)} %get-tuple-element.1678), channel_id=1, source_target_pairs={{0,8},{4,12},{8,0},{12,4},{1,9},{5,13},{9,1},{13,5},{2,10},{6,14},... | collective-permute-start | bytes 786440 | tf_op jit(solution)/shard_map/ppermute | solution.py:352
  277.6 30.3 %collective-permute-start.64 = (bf16[1024,512]{1,0:T(8,128)(2,1)S(1)}, bf16[1024,512]{1,0:T(8,128)(2,1)S(1)}, u32[]{:S(2)}, u32[]{:S(2)}) collective-permute-start(bf16[1024,512]{1,0:T(8,128)(2,1)S(1)} %get-tuple-element.1422), channel_id=1, source_target_pairs={{0,16},{16,0},{1,17},{17,1},{2,18},{18,2},{3,19},{19,3},{4,20},{20... | collective-permute-start | bytes 3145736 | tf_op jit(solution)/shard_map/ppermute | solution.py:352
  293.2 14.0 %collective-permute-start.62 = (bf16[64,2048]{1,0:T(8,128)(2,1)S(1)}, bf16[64,2048]{1,0:T(8,128)(2,1)S(1)}, u32[]{:S(2)}, u32[]{:S(2)}) collective-permute-start(bf16[64,2048]{1,0:T(8,128)(2,1)S(1)} %get-tuple-element.1507.refs_0_), channel_id=1, source_target_pairs={{0,8},{4,12},{8,0},{12,4},{1,9},{5,13},{9,1},{13,5},{2,10},{6,14},... | collective-permute-start | bytes 786440 | tf_op jit(solution)/shard_map/ppermute | solution.py:352
  293.5 14.1 %collective-permute-start.61 = (bf16[64,2048]{1,0:T(8,128)(2,1)S(1)}, bf16[64,2048]{1,0:T(8,128)(2,1)S(1)}, u32[]{:S(2)}, u32[]{:S(2)}) collective-permute-start(bf16[64,2048]{1,0:T(8,128)(2,1)S(1)} %get-tuple-element.1507.refs_0_), channel_id=1, source_target_pairs={{0,4},{4,0},{8,12},{12,8},{1,5},{5,1},{9,13},{13,9},{2,6},{6,2},{1... | collective-permute-start | bytes 786440 | tf_op jit(solution)/shard_map/ppermute | solution.py:352
  293.5 14.4 %collective-permute-start.65 = (bf16[64,2048]{1,0:T(8,128)(2,1)S(1)}, bf16[64,2048]{1,0:T(8,128)(2,1)S(1)}, u32[]{:S(2)}, u32[]{:S(2)}) collective-permute-start(bf16[64,2048]{1,0:T(8,128)(2,1)S(1)} %get-tuple-element.1507.refs_0_), channel_id=1, source_target_pairs={{0,2},{2,0},{1,3},{3,1},{4,6},{6,4},{5,7},{7,5},{8,10},{10,8},{9,1... | collective-permute-start | bytes 786440 | tf_op jit(solution)/shard_map/ppermute | solution.py:352
  316.7 29.4 %all-to-all-start.5 = ((bf16[4,256,512]{2,1,0:T(8,128)(2,1)}), bf16[4,256,512]{2,1,0:T(8,128)(2,1)S(1)}, u32[]{:S(2)}, u32[]{:S(2)}) async-start(bf16[4,256,512]{2,1,0:T(8,128)(2,1)} %bitcast.179), calls=%async_computation.5 | async-start | bytes 2097152 | tf_op jit(solution)/shard_map/all_to_all | solution.py:881
  320.2 24.1 %collective-permute-start.74 = (bf16[1024,512]{1,0:T(8,128)(2,1)}, bf16[1024,512]{1,0:T(8,128)(2,1)S(1)}, u32[]{:S(2)}, u32[]{:S(2)}) collective-permute-start(bf16[1024,512]{1,0:T(8,128)(2,1)} %get-tuple-element.1476), channel_id=1, source_target_pairs={{0,16},{16,0},{1,17},{17,1},{2,18},{18,2},{3,19},{19,3},{4,20},{20... | collective-permute-start | bytes 3145736 | tf_op jit(solution)/shard_map/ppermute | solution.py:352
  321.9 14.3 %collective-permute-start.68 = (bf16[64,2048]{1,0:T(8,128)(2,1)S(1)}, bf16[64,2048]{1,0:T(8,128)(2,1)S(1)}, u32[]{:S(2)}, u32[]{:S(2)}) collective-permute-start(bf16[64,2048]{1,0:T(8,128)(2,1)S(1)} %collective-permute-done.62.refs_2_), channel_id=1, source_target_pairs={{0,2},{2,0},{1,3},{3,1},{4,6},{6,4},{5,7},{7,5},{8,10},{10,8},{9,1... | collective-permute-start | bytes 786440 | tf_op jit(solution)/shard_map/ppermute | solution.py:352
  323.3 12.8 %collective-permute-start.70 = (bf16[64,2048]{1,0:T(8,128)(2,1)S(1)}, bf16[64,2048]{1,0:T(8,128)(2,1)S(1)}, u32[]{:S(2)}, u32[]{:S(2)}) collective-permute-start(bf16[64,2048]{1,0:T(8,128)(2,1)S(1)} %collective-permute-done.61.refs_1_), channel_id=1, source_target_pairs={{0,1},{1,0},{2,3},{3,2},{4,5},{5,4},{6,7},{7,6},{8,9},{9,8},{10,11... | collective-permute-start | bytes 786440 | tf_op jit(solution)/shard_map/ppermute | solution.py:352
  323.3 16.9 %collective-permute-start.72 = (bf16[64,2048]{1,0:T(8,128)(2,1)}, bf16[64,2048]{1,0:T(8,128)(2,1)S(1)}, u32[]{:S(2)}, u32[]{:S(2)}) collective-permute-start(bf16[64,2048]{1,0:T(8,128)(2,1)} %copy-done.92), channel_id=1, source_target_pairs={{0,1},{1,0},{2,3},{3,2},{4,5},{5,4},{6,7},{7,6},{8,9},{9,8},{10,11... | collective-permute-start | bytes 786440 | tf_op jit(solution)/shard_map/ppermute | solution.py:352
  347.1 28.6 %all-to-all-start.6 = ((bf16[4,256,512]{2,1,0:T(8,128)(2,1)}), bf16[4,256,512]{2,1,0:T(8,128)(2,1)}, u32[]{:S(2)}, u32[]{:S(2)}) async-start(bf16[4,256,512]{2,1,0:T(8,128)(2,1)} %bitcast.178), calls=%async_computation.6 | async-start | bytes 2097152 | tf_op jit(solution)/shard_map/all_to_all | solution.py:881
  365.1 37.6 %collective-permute-start.82 = (bf16[1024,128]{1,0:T(8,128)(2,1)S(1)}, bf16[1024,128]{1,0:T(8,128)(2,1)S(1)}, u32[]{:S(2)}, u32[]{:S(2)}) collective-permute-start(bf16[1024,128]{1,0:T(8,128)(2,1)S(1)} %get-tuple-element.1576), channel_id=1, source_target_pairs={{0,16},{16,0},{1,17},{17,1},{2,18},{18,2},{3,19},{19,3},{4,20},{20... | collective-permute-start | bytes 786440 | tf_op jit(solution)/shard_map/ppermute | solution.py:352
  383.1 21.0 %collective-permute-start.83 = (bf16[128,2048]{1,0:T(8,128)(2,1)S(1)}, bf16[128,2048]{1,0:T(8,128)(2,1)}, u32[]{:S(2)}, u32[]{:S(2)}) collective-permute-start(bf16[128,2048]{1,0:T(8,128)(2,1)S(1)} %add_convert_fusion.5), channel_id=1, source_target_pairs={{0,2},{2,0},{1,3},{3,1},{4,6},{6,4},{5,7},{7,5},{8,10},{10,8},{9,1... | collective-permute-start | bytes 1572872 | tf_op jit(solution)/shard_map/ppermute | solution.py:352
  388.9 15.8 %collective-permute-start.84 = (bf16[64,2048]{1,0:T(8,128)(2,1)}, bf16[64,2048]{1,0:T(8,128)(2,1)}, u32[]{:S(2)}, u32[]{:S(2)}) collective-permute-start(bf16[64,2048]{1,0:T(8,128)(2,1)} %add_convert_fusion.17), channel_id=1, source_target_pairs={{0,4},{4,0},{8,12},{12,8},{1,5},{5,1},{9,13},{13,9},{2,6},{6,2},{1... | collective-permute-start | bytes 786440 | tf_op jit(solution)/shard_map/ppermute | solution.py:352
  388.9 15.8 %collective-permute-start.85 = (bf16[64,2048]{1,0:T(8,128)(2,1)}, bf16[64,2048]{1,0:T(8,128)(2,1)}, u32[]{:S(2)}, u32[]{:S(2)}) collective-permute-start(bf16[64,2048]{1,0:T(8,128)(2,1)} %get-tuple-element.1682), channel_id=1, source_target_pairs={{0,2},{2,0},{1,3},{3,1},{4,6},{6,4},{5,7},{7,5},{8,10},{10,8},{9,1... | collective-permute-start | bytes 786440 | tf_op jit(solution)/shard_map/ppermute | solution.py:352
  390.9 40.8 %all-to-all-start.7 = ((bf16[4,256,512]{2,1,0:T(8,128)(2,1)}), bf16[4,256,512]{2,1,0:T(8,128)(2,1)}, u32[]{:S(2)}, u32[]{:S(2)}) async-start(bf16[4,256,512]{2,1,0:T(8,128)(2,1)} %bitcast.177), calls=%async_computation.7 | async-start | bytes 2097152 | tf_op jit(solution)/shard_map/all_to_all | solution.py:881
  402.6 13.4 %collective-permute-start.87 = (bf16[64,2048]{1,0:T(8,128)(2,1)}, bf16[64,2048]{1,0:T(8,128)(2,1)S(1)}, u32[]{:S(2)}, u32[]{:S(2)}) collective-permute-start(bf16[64,2048]{1,0:T(8,128)(2,1)} %get-tuple-element.1593), channel_id=1, source_target_pairs={{0,2},{2,0},{1,3},{3,1},{4,6},{6,4},{5,7},{7,5},{8,10},{10,8},{9,1... | collective-permute-start | bytes 786440 | tf_op jit(solution)/shard_map/ppermute | solution.py:352
  404.1 19.2 %collective-permute-start.88 = (bf16[128,2048]{1,0:T(8,128)(2,1)}, bf16[128,2048]{1,0:T(8,128)(2,1)}, u32[]{:S(2)}, u32[]{:S(2)}) collective-permute-start(bf16[128,2048]{1,0:T(8,128)(2,1)} %add_convert_fusion.4), channel_id=1, source_target_pairs={{0,2},{2,0},{1,3},{3,1},{4,6},{6,4},{5,7},{7,5},{8,10},{10,8},{9,1... | collective-permute-start | bytes 1572872 | tf_op jit(solution)/shard_map/ppermute | solution.py:352
  406.7 17.6 %collective-permute-start.91 = (bf16[64,2048]{1,0:T(8,128)(2,1)}, bf16[64,2048]{1,0:T(8,128)(2,1)}, u32[]{:S(2)}, u32[]{:S(2)}) collective-permute-start(bf16[64,2048]{1,0:T(8,128)(2,1)} %add_convert_fusion.12), channel_id=1, source_target_pairs={{0,4},{4,0},{8,12},{12,8},{1,5},{5,1},{9,13},{13,9},{2,6},{6,2},{1... | collective-permute-start | bytes 786440 | tf_op jit(solution)/shard_map/ppermute | solution.py:352
  410.9 20.8 %collective-permute-start.90 = (bf16[64,2048]{1,0:T(8,128)(2,1)}, bf16[64,2048]{1,0:T(8,128)(2,1)S(1)}, u32[]{:S(2)}, u32[]{:S(2)}) collective-permute-start(bf16[64,2048]{1,0:T(8,128)(2,1)} %get-tuple-element.1675), channel_id=1, source_target_pairs={{0,4},{4,0},{8,12},{12,8},{1,5},{5,1},{9,13},{13,9},{2,6},{6,2},{1... | collective-permute-start | bytes 786440 | tf_op jit(solution)/shard_map/ppermute | solution.py:352
  411.0 20.8 %collective-permute-start.89 = (bf16[64,2048]{1,0:T(8,128)(2,1)}, bf16[64,2048]{1,0:T(8,128)(2,1)}, u32[]{:S(2)}, u32[]{:S(2)}) collective-permute-start(bf16[64,2048]{1,0:T(8,128)(2,1)} %get-tuple-element.1676), channel_id=1, source_target_pairs={{0,8},{4,12},{8,0},{12,4},{1,9},{5,13},{9,1},{13,5},{2,10},{6,14},... | collective-permute-start | bytes 786440 | tf_op jit(solution)/shard_map/ppermute | solution.py:352
  416.0 28.7 %collective-permute-start.92 = (bf16[64,2048]{1,0:T(8,128)(2,1)}, bf16[64,2048]{1,0:T(8,128)(2,1)}, u32[]{:S(2)}, u32[]{:S(2)}) collective-permute-start(bf16[64,2048]{1,0:T(8,128)(2,1)} %get-tuple-element.1611), channel_id=1, source_target_pairs={{0,2},{2,0},{1,3},{3,1},{4,6},{6,4},{5,7},{7,5},{8,10},{10,8},{9,1... | collective-permute-start | bytes 786440 | tf_op jit(solution)/shard_map/ppermute | solution.py:352
  423.3 18.9 %collective-permute-start.95 = (bf16[1024,384]{1,0:T(8,128)(2,1)}, bf16[1024,384]{1,0:T(8,128)(2,1)}, u32[]{:S(2)}, u32[]{:S(2)}) collective-permute-start(bf16[1024,384]{1,0:T(8,128)(2,1)} %get-tuple-element.1616), channel_id=1, source_target_pairs={{0,16},{16,0},{1,17},{17,1},{2,18},{18,2},{3,19},{19,3},{4,20},{20... | collective-permute-start | bytes 2359304 | tf_op jit(solution)/shard_map/ppermute | solution.py:352
  436.4 12.5 %collective-permute-start.94 = (bf16[64,2048]{1,0:T(8,128)(2,1)S(1)}, bf16[64,2048]{1,0:T(8,128)(2,1)S(1)}, u32[]{:S(2)}, u32[]{:S(2)}) collective-permute-start(bf16[64,2048]{1,0:T(8,128)(2,1)S(1)} %get-tuple-element.1673), channel_id=1, source_target_pairs={{0,4},{4,0},{8,12},{12,8},{1,5},{5,1},{9,13},{13,9},{2,6},{6,2},{1... | collective-permute-start | bytes 786440 | tf_op jit(solution)/shard_map/ppermute | solution.py:352
  438.7 13.2 %collective-permute-start.93 = (bf16[64,2048]{1,0:T(8,128)(2,1)S(1)}, bf16[64,2048]{1,0:T(8,128)(2,1)S(1)}, u32[]{:S(2)}, u32[]{:S(2)}) collective-permute-start(bf16[64,2048]{1,0:T(8,128)(2,1)S(1)} %get-tuple-element.1674), channel_id=1, source_target_pairs={{0,8},{4,12},{8,0},{12,4},{1,9},{5,13},{9,1},{13,5},{2,10},{6,14},... | collective-permute-start | bytes 786440 | tf_op jit(solution)/shard_map/ppermute | solution.py:352
  452.6 27.8 %all-to-all-start.8 = ((bf16[4,256,512]{2,1,0:T(8,128)(2,1)}), bf16[4,256,512]{2,1,0:T(8,128)(2,1)}, u32[]{:S(2)}, u32[]{:S(2)}) async-start(bf16[4,256,512]{2,1,0:T(8,128)(2,1)} %bitcast.44), calls=%async_computation.8 | async-start | bytes 2097152 | tf_op jit(solution)/shard_map/all_to_all | solution.py:881
  460.1 12.6 %collective-permute-start.96 = (bf16[64,2048]{1,0:T(8,128)(2,1)S(1)}, bf16[64,2048]{1,0:T(8,128)(2,1)S(1)}, u32[]{:S(2)}, u32[]{:S(2)}) collective-permute-start(bf16[64,2048]{1,0:T(8,128)(2,1)S(1)} %maximum_select_fusion.2.refs_0_), channel_id=1, source_target_pairs={{0,2},{2,0},{1,3},{3,1},{4,6},{6,4},{5,7},{7,5},{8,10},{10,8},{9,1... | collective-permute-start | bytes 786440 | tf_op jit(solution)/shard_map/ppermute | solution.py:352
  (160 other events, 1495.6 us)

commit v3 on v2

--- a/solution.py
+++ b/solution.py
@@ -428,18 +428,16 @@
     )(query, key, value, gain_one, gain_two)
 
 
-def feed_forward(pieces, cotangent, gates, ups, downs):
-    rows, features = cotangent.shape
-    unit, count, steps = gates[0].shape[1], pieces[0].shape[0], 4
-    part = features // 2
+def feed_forward(pieces, gates, ups):
+    features, count, steps = pieces[0].shape[1], pieces[0].shape[0], 4
+    rows, unit, part = count * len(pieces), gates[0].shape[1], features // 2
     block, group = rows // steps, len(pieces) // steps
     f32 = jnp.float32
 
     def kernel(*refs):
         ins, refs = refs[: len(pieces)], refs[len(pieces) :]
-        cot_ref, *weights = refs[:7]
-        gate_refs, up_refs, down_refs = weights[:2], weights[2:4], weights[4:]
-        rows_ref, hidden_ref, gate_grad_ref, up_grad_ref, held, sems = refs[7:]
+        gate_refs, up_refs = refs[:2], refs[2:4]
+        rows_ref, hidden_ref, gate_slope_ref, up_slope_ref, held, sems = refs[4:]
         step = pl.program_id(0)
 
         def copy(i):
@@ -461,27 +459,21 @@
             product(values[:, :part], first[...]) + product(values[:, part:], second[...])
             for first, second in (gate_refs, up_refs)
         )
-        cot = cot_ref[...]
-        hidden_grad = product(cot[:, :part], down_refs[0][...])
-        hidden_grad += product(cot[:, part:], down_refs[1][...])
         sigmoid = 1.0 / (1.0 + jnp.exp(-gate))
         silu = gate * sigmoid
         hidden_ref[...] = (silu * up).astype(LOW)
-        slope = sigmoid * (1.0 + gate * (1.0 - sigmoid))
-        gate_grad_ref[...] = (hidden_grad * up * slope).astype(LOW)
-        up_grad_ref[...] = (hidden_grad * silu).astype(LOW)
+        gate_slope_ref[...] = (up * (sigmoid * (1.0 + gate * (1.0 - sigmoid)))).astype(LOW)
+        up_slope_ref[...] = silu.astype(LOW)
 
     wide = pl.BlockSpec((block, features), lambda i: (i, 0))
     narrow = pl.BlockSpec((block, unit), lambda i: (i, 0))
-    once = pl.Buffered(1)
-    half = pl.BlockSpec((part, unit), lambda i: (0, 0), pipeline_mode=once)
+    half = pl.BlockSpec((part, unit), lambda i: (0, 0), pipeline_mode=pl.Buffered(1))
     return pl.pallas_call(
         kernel,
         grid=(steps,),
-        out_shape=[jax.ShapeDtypeStruct((rows, features), LOW)]
-        + [jax.ShapeDtypeStruct((rows, unit), LOW)] * 3,
-        in_specs=[pl.BlockSpec(memory_space=pltpu.HBM)] * len(pieces)
-        + [wide, half, half, half, half, half, half],
+        out_shape=[pltpu.HBM((rows, features), LOW), jax.ShapeDtypeStruct((rows, unit), LOW)]
+        + [pltpu.HBM((rows, unit), LOW)] * 2,
+        in_specs=[pl.BlockSpec(memory_space=pltpu.HBM)] * len(pieces) + [half] * 4,
         out_specs=[wide, narrow, narrow, narrow],
         scratch_shapes=[
             pltpu.VMEM((rows, features), LOW),
@@ -491,11 +483,43 @@
             dimension_semantics=("arbitrary",), vmem_limit_bytes=32 << 20
         ),
         cost_estimate=pl.CostEstimate(
-            flops=6 * rows * features * unit,
+            flops=4 * rows * features * unit,
             transcendentals=rows * unit,
-            bytes_accessed=6 * rows * features + 6 * features * unit + 6 * rows * unit,
+            bytes_accessed=4 * rows * features + 4 * features * unit + 10 * rows * unit,
         ),
-    )(*(in_main(piece) for piece in pieces), cotangent, *gates, *ups, *downs)
+    )(*(in_main(piece) for piece in pieces), *gates, *ups)
+
+
+def feed_back(cotangent, downs, gate_slope, up_slope):
+    rows, features = cotangent.shape
+    unit, steps, part = gate_slope.shape[1], 4, features // 2
+    block = rows // steps
+
+    def kernel(cot_ref, *refs):
+        gate_slope_ref, up_slope_ref, gate_ref, up_ref = refs[4:]
+        for i in range(2):
+            at = slice(i * unit // 2, (i + 1) * unit // 2)
+            hidden_grad = product(cot_ref[:, :part], refs[2 * i][...])
+            hidden_grad += product(cot_ref[:, part:], refs[2 * i + 1][...])
+            gate_ref[:, at] = (hidden_grad * gate_slope_ref[:, at].astype(jnp.float32)).astype(LOW)
+            up_ref[:, at] = (hidden_grad * up_slope_ref[:, at].astype(jnp.float32)).astype(LOW)
+
+    wide = pl.BlockSpec((block, features), lambda i: (i, 0))
+    narrow = pl.BlockSpec((block, unit), lambda i: (i, 0))
+    half = pl.BlockSpec((part, unit // 2), lambda i: (0, 0), pipeline_mode=pl.Buffered(1))
+    return pl.pallas_call(
+        kernel,
+        grid=(steps,),
+        out_shape=[jax.ShapeDtypeStruct((rows, unit), LOW)] * 2,
+        in_specs=[wide, half, half, half, half, narrow, narrow],
+        out_specs=[narrow, narrow],
+        compiler_params=pltpu.CompilerParams(dimension_semantics=("arbitrary",)),
+        cost_estimate=pl.CostEstimate(
+            flops=2 * rows * features * unit,
+            transcendentals=0,
+            bytes_accessed=2 * rows * features + 2 * features * unit + 12 * rows * unit,
+        ),
+    )(in_main(cotangent), *downs, gate_slope, up_slope)
 
 
 def swapped(values):
@@ -657,18 +681,20 @@
     )(mixed, *outs)
 
 
-def attention_back(pieces, output, queries, keys, values, mixed, numerator, total, *places):
+def attention_back(pieces, outs, queries, keys, values, mixed, numerator, total, *places):
     rows, width = queries.shape
-    features, count, steps = output.shape[1], pieces[0].shape[0], 4
+    depth, count, steps = outs[0].shape[2], pieces[0].shape[0], 4
+    features = 8 * depth
     block, group = rows // steps, len(pieces) // steps
     cosine, sine, column, line = places
     f32 = jnp.float32
 
     def kernel(*refs):
         ins, refs = refs[: len(pieces)], refs[len(pieces) :]
-        w_ref, q_ref, k_ref, v_ref, mixed_ref, num_ref, total_ref, *refs = refs
+        out_refs, refs = refs[:2], refs[2:]
+        q_ref, k_ref, v_ref, mixed_ref, num_ref, total_ref, *refs = refs
         cos_ref, sin_ref, col_ref, line_ref, grad_ref, keep_ref, give_ref, *refs = refs
-        held, key_sum, value_sum, output_sum, sems = refs
+        held, w_ref, key_sum, value_sum, output_sum, sems = refs
         step = pl.program_id(0)
 
         def copy(i):
@@ -681,6 +707,8 @@
                 if at == 0:
                     for i in range(len(pieces)):
                         copy(i).start()
+                    for i in range(8):
+                        w_ref[:, i * depth : (i + 1) * depth] = out_refs[i // 4][i % 4]
                     key_sum[...] = jnp.zeros_like(key_sum)
                     value_sum[...] = jnp.zeros_like(value_sum)
                     output_sum[...] = jnp.zeros_like(output_sum)
@@ -739,12 +767,13 @@
             jax.ShapeDtypeStruct(half, LOW),
         ],
         in_specs=[pl.BlockSpec(memory_space=pltpu.HBM)] * len(pieces)
-        + [still(output.shape), moving, still((rows, width)), still((rows, width))]
+        + [still(outs[0].shape), still(outs[1].shape), moving, still((rows, width)), still((rows, width))]
         + [moving, moving, moving, still((rows, width)), still((rows, width))]
         + [pl.BlockSpec((block, 1), lambda i: (i, 0)), still((1, rows))],
         out_specs=[whole((rows, 3 * width)), whole(half), whole(half)],
         scratch_shapes=[
             pltpu.VMEM((rows, features), LOW),
+            pltpu.VMEM((width, features), LOW),
             pltpu.VMEM((width, rows), f32),
             pltpu.VMEM((width, rows), f32),
             pltpu.VMEM((width, features), f32),
@@ -758,22 +787,24 @@
             transcendentals=2 * rows * rows,
             bytes_accessed=2 * rows * features + 24 * rows * width,
         ),
-    )(*(in_main(a) for a in (*pieces, output, queries, keys, values, mixed, numerator, total, *places)))
+    )(*(in_main(a) for a in (*pieces, *outs, queries, keys, values, mixed, numerator, total, *places)))
 
 
 def turned_pieces(value):
     total, rows, columns = value.shape
-
-    def kernel(value_ref, out_ref):
-        out_ref[0] = value_ref[0].T
+    half = rows // 2
+
+    def kernel(value_ref, first_ref, second_ref):
+        first_ref[0] = value_ref[0, :half].T
+        second_ref[0] = value_ref[0, half:].T
 
     size = value.size * value.dtype.itemsize
     return pl.pallas_call(
         kernel,
         grid=(total,),
-        out_shape=jax.ShapeDtypeStruct((total, columns, rows), value.dtype),
+        out_shape=[jax.ShapeDtypeStruct((total, columns, half), value.dtype)] * 2,
         in_specs=[pl.BlockSpec((1, rows, columns), lambda i: (i, 0, 0))],
-        out_specs=pl.BlockSpec((1, columns, rows), lambda i: (i, 0, 0)),
+        out_specs=[pl.BlockSpec((1, columns, half), lambda i: (i, 0, 0))] * 2,
         cost_estimate=pl.CostEstimate(flops=0, transcendentals=0, bytes_accessed=2 * size),
     )(value)
 
@@ -983,7 +1014,7 @@
 
     v.qkv_o = swap(v.qkv_own, SEQ)
     v.output = spread(v.output)
-    v.down = turned_pieces(v.down.reshape(4, unit, depth))
+    v.down, v.down_late = turned_pieces(v.down.reshape(4, unit, depth))
     v.c1, v.c2, v.c3 = (swap(g, CORE) for g in (v.g1, v.g2, v.g3))
     v.c4, v.c5 = swap(v.x1, CORE), swap(v.x2, CORE)
     v.step("qkv_o")
@@ -1036,43 +1067,52 @@
     v.f1, v.f2 = swap(v.d1, CORE), swap(v.d2, CORE)
     v.step("up", "gate_o", "d3", "s_middle")
     v.scatter_2("s_")
-    v.step("s_first")
+    v.step("s_first", "gate_o")
     v.scatter_3("s_")
     v.up_o = swap(v.up, SEQ)
     v.e3, v.f3 = swap(v.d3, X), swap(v.d3, CORE)
     v.step("up_o", "e3")
-    v.down = spread(v.down)
     v.middle = local(v.tokens, 0, 0).astype(f32) + v.scatter_4("s_")
     v.scale_second = lax.rsqrt(jnp.mean(v.middle * v.middle, axis=1, keepdims=True) + EPS)
     v.gather_0((v.middle * v.scale_second * v.gain_second).astype(LOW))
     v.f4, v.f5, v.f6 = (swap(e, CORE) for e in (v.e1, v.e2, v.e3))
     v.step("x0", "up_o")
     v.gather_1()
-    v.down_o = swap(v.down, SEQ)
     d1, d2, d3, e1, e2, e3 = v.take("d1", "d2", "d3", "e1", "e2", "e3")
     f1, f2, f3, f4, f5, f6 = v.take("f1", "f2", "f3", "f4", "f5", "f6")
     v.every_cotangent = whole(v.cotangent, [d1, d2, d3], [e1, e2, e3], [f1, f2, f3], [f4, f5, f6])
-    v.step("x1", "x2", "down_o")
+    v.step("x1", "x2")
     v.gather_2()
-    v.output_full = side_by_side(jnp.concatenate(v.take("output", "output_other")))
-    v.gate_full = jnp.concatenate([v.gate, v.gate_o]).reshape(8 * depth, unit)
-    v.up_full = jnp.concatenate([v.up, v.up_o]).reshape(8 * depth, unit)
-    v.step("down_o")
+    v.down = spread(v.down)
+    v.step("down")
     pieces = v.gather_3()
     for i, piece in enumerate(pieces):
         setattr(v, "piece%d" % i, piece)
     v.step()
 
-    v.normed_two, v.hidden, v.gate_grad, v.up_grad = feed_forward(
+    v.down_late = spread(v.down_late)
+    v.down_o = swap(v.down, SEQ)
+    v.normed_two, v.hidden, v.gate_slope, v.up_slope = feed_forward(
         v.take(*("piece%d" % i for i in range(16))),
-        v.every_cotangent,
-        [own.reshape(4 * depth, unit) for own in v.take("gate", "gate_o")],
-        [own.reshape(4 * depth, unit) for own in v.take("up", "up_o")],
-        [own.reshape(4 * depth, unit) for own in (v.down, v.down_o)],
-    )
+        [own.reshape(4 * depth, unit) for own in (v.gate, v.gate_o)],
+        [own.reshape(4 * depth, unit) for own in (v.up, v.up_o)],
+    )
+    v.step("down_o")
+    v.late_other = swap(v.down_late, SEQ)
     v.down_k, v.down_g = halves(v.every_cotangent, v.hidden)
-    del v.every_cotangent
+    v.gate_full = jnp.concatenate(v.take("gate", "gate_o")).reshape(8 * depth, unit)
+    v.up_full = jnp.concatenate(v.take("up", "up_o")).reshape(8 * depth, unit)
     v.step()
+    v.gate_grad, v.up_grad = feed_back(
+        v.take("every_cotangent")[0],
+        [
+            own.reshape(4 * depth, unit // 2)
+            for own in (v.down, v.down_o, v.down_late, v.late_other)
+        ],
+        *v.take("gate_slope", "up_slope"),
+    )
+    v.down_g = swap(v.down_g, SEQ)
+    v.step("down_g")
 
     def quarter(values, index):
         size = rows // 4
@@ -1082,7 +1122,6 @@
         gate, up = quarter(v.gate_grad, index), quarter(v.up_grad, index)
         return (contract_cols(gate, v.gate_full) + contract_cols(up, v.up_full)).astype(LOW)
 
-    v.down_g = swap(v.down_g, SEQ)
     v.scatter_0("s_", rows, normed_grads)
     v.step("down_g")
     v.scatter_1("s_", rows, normed_grads)
@@ -1096,7 +1135,13 @@
     del v.normed_two, v.gate_grad, v.up_grad
     v.scatter_3("s_")
     v.up_g = swap(v.up_g, SEQ)
-    v.down_full = jnp.concatenate(v.take("down", "down_o")).reshape(8 * depth, unit)
+    v.down_full = jnp.concatenate(
+        [
+            jnp.concatenate(v.take("down", "down_o")),
+            jnp.concatenate(v.take("down_late", "late_other")),
+        ],
+        axis=2,
+    ).reshape(8 * depth, unit)
     v.step("gate_g", "up_g")
     normed_two_grad = v.scatter_4("s_")
     middle, scale_second = v.middle, v.scale_second
@@ -1123,7 +1168,7 @@
     v.gather_2()
     v.down = spread(added(*v.take("down_k", "down_g")).reshape(4, depth, unit))
     v.gate_sum = added(*v.take("gate_k", "gate_g")).reshape(4, depth, unit)
-    v.step("down", "up_g")
+    v.step("down")
     pieces = v.gather_3()
     for i, piece in enumerate(pieces):
         setattr(v, "piece%d" % i, piece)
@@ -1132,7 +1177,8 @@
     v.gate = spread(v.take("gate_sum")[0])
     v.projected_grad, v.out_k, v.out_g = attention_back(
         v.take(*("piece%d" % i for i in range(16))),
-        *v.take("output_full", "queries", "keys", "values", "mixed", "numerator", "total"),
+        v.take("output", "output_other"),
+        *v.take("queries", "keys", "values", "mixed", "numerator", "total"),
         *v.take("cosine", "sine", "column", "line"),
     )
     v.step("gate")
@@ -1166,14 +1212,23 @@
         + scale_own * scaled
         - own_input * scale_own**3 * jnp.mean(scaled * own_input, axis=1, keepdims=True)
     )
-    v.input_grad = turned(input_grad.astype(LOW))
+    v.input_grad = input_grad.astype(LOW)
     v.step()
     v.qkv = spread(v.take("qkv_sum")[0])
     v.produced = turned((v.take("middle")[0] + v.scatter_4("p_")).astype(LOW))
+    v.input_grad = turned(v.input_grad)
     v.input_x, v.input_core = swap(v.input_grad, X), swap(v.input_grad, CORE)
     v.produced_x, v.produced_core = swap(v.produced, X), swap(v.produced, CORE)
     v.gate_wgrad = side_by_side(v.take("gate")[0]).astype(f32)
     v.up_wgrad = side_by_side(v.take("up")[0]).astype(f32)
+
+    def gain_grad(gain, *pairs):
+        part = sum(jnp.sum(w.astype(f32) * g, axis=1) for w, g in pairs)
+        return part / gain.astype(f32)
+
+    v.second_gain = gain_grad(
+        feedforward_gain, (gate_weight, v.gate_wgrad), (up_weight, v.up_wgrad)
+    )
     v.step("qkv")
     v.input_far = swap(v.input_x, CORE)
     v.produced_far = swap(v.produced_x, CORE)
@@ -1192,10 +1247,6 @@
     )
     gate_wgrad, up_wgrad = v.gate_wgrad, v.up_wgrad
 
-    def gain_grad(gain, *pairs):
-        part = sum(jnp.sum(w.astype(f32) * g, axis=1) for w, g in pairs)
-        return part / gain.astype(f32)
-
     gain_grads = jnp.stack(
         [
             gain_grad(
@@ -1204,7 +1255,7 @@
                 (key_weight, key_wgrad),
                 (value_weight, value_wgrad),
             ),
-            gain_grad(feedforward_gain, (gate_weight, gate_wgrad), (up_weight, up_wgrad)),
+            v.second_gain,
         ]
     )
     gain_grads = gain_grads + swap(gain_grads, CORE)

time: 496 us -> 492 us (level)
  waiting for transfers between devices: 207 us -> 190 us
  local copies, waits for them, and re-layouts: 28.7 us -> 21.5 us
  Pallas kernels: 54.5 us -> 60.6 us
  starting transfers between devices: 119 us -> 125 us
    ppermute x104 -> x105, waiting for transfers between devices: 185 us -> 144 us  [swap(): return lax.ppermute(value, axis, pairs)]
    all_to_all x9 -> x10, waiting for transfers between devices: 21.8 us -> 46 us  [spread(): return lax.all_to_all(pieces, CTX, 0, 0, tiled=True)]
    pallas_call x2 -> x3, Pallas kernels: 13.8 us -> 19.7 us  [the longest x1 9.26 us: feed_forward(): pl.pallas_call(kernel, grid=(steps,), out_shape=[pltpu.HBM((rows, feature...]
    unnamed x235 -> x186, local copies, waits for them, and re-layouts: 14.3 us -> 8.54 us
    all_to_all x9 -> x10, starting transfers between devices: 46.5 us -> 51 us  [spread(): return lax.all_to_all(pieces, CTX, 0, 0, tiled=True)]
    ppermute x104 -> x105, starting transfers between devices: 72.2 us -> 73.8 us  [swap(): return lax.ppermute(value, axis, pairs)]
  transfers between devices with their start and end apart: 113 -> 115, of which waited for: 48 -> 53; matrix products, arithmetic and copies ran while one was open for 17% -> 19% of each run, Pallas kernels for 9% -> 11%
where the time goes in v3:
time: 492 us; the launch traced here: 487 us
  waiting for transfers between devices  190 us (39%)
  starting transfers between devices  125 us (25%)
  Pallas kernels  60.6 us (12%)
  other arithmetic  58.8 us (12%)
  matrix products  29.1 us (6%)
  local copies, waits for them, and re-layouts  21.5 us (4%)
    ppermute x105, waiting for transfers between devices, swap(): return lax.ppermute(value, axis, pairs)  144 us
    ppermute x105, starting transfers between devices, swap(): return lax.ppermute(value, axis, pairs)  73.8 us
    all_to_all x10, starting transfers between devices, spread(): return lax.all_to_all(pieces, CTX, 0, 0, tiled=True)  51 us
    all_to_all x10, waiting for transfers between devices, spread(): return lax.all_to_all(pieces, CTX, 0, 0, tiled=True)  46 us
    dot_general x16, matrix products, contract_cols(): lax.dot_general(left, right, (((1,), (1,)), ((), ())), preferred_element_...  17.1 us
    pallas_call x1, Pallas kernels, attention(): pl.pallas_call(kernel, grid=(2 * steps,), out_shape=[pltpu.HBM((rows, fea...  12.7 us
    pallas_call x1, Pallas kernels, attention_back(): pl.pallas_call(kernel, grid=(steps,), out_shape=[jax.ShapeDtypeStruct((ro...  12.5 us
    dot_general x4, matrix products, contract_rows(): lax.dot_general(left, right, (((0,), (0,)), ((), ())), preferred_element_...  12 us
  transfers between devices with their start and end apart: 115, of which 53 were waited for; matrix products, arithmetic and copies ran while one was open for 19% of the time, Pallas kernels for 11%

profile of v3, /device:TPU:0, one launch (start us, length us, event | category | flops | bytes accessed | tf_op | source)
XLA Modules:
  0.0 487.3 jit_solution(2473226042707766548)
XLA Ops:
  0.7 2.2 shard_map.203
  4.4 4.1 collective-permute-start.1
  10.1 3.5 all-to-all-start
  14.3 7.9 %collective-permute-done.1.refs_1_ = bf16[64,2048]{1,0:T(8,128)(2,1)} collective-permute-done((bf16[64,2048]{1,0:T(8,128)(2,1)S(1)}, bf16[64,2048]{1,0:T(8,128)(2,1)}, u32[]{:S(2)}, u32[]{:S(2)}) %collective-permute-start.1) | collective-permute-done | bytes 262176 | tf_op jit(solution)/shard_map/ppermute | solution.py:352
  23.0 3.7 collective-permute-start.4
  27.8 3.0 fusion.4
  31.8 8.0 %collective-permute-done.2.refs_2_ = bf16[64,2048]{1,0:T(8,128)(2,1)} collective-permute-done((bf16[64,2048]{1,0:T(8,128)(2,1)}, bf16[64,2048]{1,0:T(8,128)(2,1)}, u32[]{:S(2)}, u32[]{:S(2)}) %collective-permute-start.2) | collective-permute-done | bytes 262176 | tf_op jit(solution)/shard_map/ppermute | solution.py:352
  44.9 3.8 all-to-all-start.1
  49.8 3.5 shard_map.204
  53.3 4.6 all-to-all-done.1.own_ref.refs_16_
  61.9 3.7 all-to-all-start.2
  66.3 12.7 %shard_map.205 = (bf16[1024,2048]{1,0:T(8,128)(2,1)}, bf16[1024,128]{1,0:T(8,128)(2,1)}, bf16[1024,128]{1,0:T(8,128)(2,1)}, bf16[1024,128]{1,0:T(8,128)(2,1)}, b...) custom-call(s32[4]{0:T(128)S(1)} %pad_add_fusion.at_ref.refs_0_, ...), custom_call_target="tpu_custom_call" | custom-call | flops 2684354560 | bytes 14155776 | tf_op jit(solution)/shard_map/pallas_call | solution.py:625
  79.0 3.6 shard_map.206
  82.7 11.2 %all-to-all-done.2 = bf16[4,256,512]{2,1,0:T(8,128)(2,1)S(1)} async-done(((bf16[4,256,512]{2,1,0:T(8,128)(2,1)}), bf16[4,256,512]{2,1,0:T(8,128)(2,1)S(1)}, u32[]{:S(2)}, u32[]{:S(2)}) %all-to-all-start.2) | async-done | bytes 1048608 | tf_op jit(solution)/shard_map/all_to_all | solution.py:912
  96.0 3.5 all-to-all-start.3
  104.9 3.8 collective-permute-done.18.refs_5_
  109.9 4.4 collective-permute-done.19
  116.1 9.6 %collective-permute-done.24.refs_3_ = bf16[64,2048]{1,0:T(8,128)(2,1)S(1)} collective-permute-done((bf16[64,2048]{1,0:T(8,128)(2,1)}, bf16[64,2048]{1,0:T(8,128)(2,1)S(1)}, u32[]{:S(2)}, u32[]{:S(2)}) %collective-permute-start.24) | collective-permute-done | bytes 262176 | tf_op jit(solution)/shard_map/ppermute | solution.py:352
  126.4 3.9 collective-permute-done.25
  132.4 2.6 collective-permute-start.28
  136.1 10.3 %collective-permute-done.29 = bf16[64,2048]{1,0:T(8,128)(2,1)S(1)} collective-permute-done((bf16[64,2048]{1,0:T(8,128)(2,1)S(1)}, bf16[64,2048]{1,0:T(8,128)(2,1)S(1)}, u32[]{:S(2)}, u32[]{:S(2)}) %collective-permute-start.29) | collective-permute-done | bytes 262176 | tf_op jit(solution)/shard_map/ppermute | solution.py:352
  151.4 3.9 collective-permute-start.32
  156.0 9.3 %collective-permute-done.33.refs_2_ = bf16[64,2048]{1,0:T(8,128)(2,1)} collective-permute-done((bf16[64,2048]{1,0:T(8,128)(2,1)}, bf16[64,2048]{1,0:T(8,128)(2,1)}, u32[]{:S(2)}, u32[]{:S(2)}) %collective-permute-start.33) | collective-permute-done | bytes 262176 | tf_op jit(solution)/shard_map/ppermute | solution.py:352
  167.7 5.0 %shard_map.207.cot_ref = bf16[1024,2048]{1,0:T(8,128)(2,1)} custom-call(s32[4]{0:T(128)} %copy-done.4, bf16[64,2048]{1,0:T(8,128)(2,1)} %copy-done.46, bf16[64,2048]{1,0:T(8,128)(2,1)} %collective-permute-done.14.refs_2_, bf16[64,2048]{1,0:T(8,128)(2,1)} %copy-done.51, bf16[64,2048]{1,0:T(8,128)(2,1)} %copy-done.47, ...), custom_call_target="tpu_custom_call" | custom-call | bytes 8388608 | tf_op jit(solution)/shard_map/pallas_call | solution.py:393
  173.1 16.4 %all-to-all-start.4 = ((bf16[4,256,256]{2,1,0:T(8,128)(2,1)}), bf16[4,256,256]{2,1,0:T(8,128)(2,1)}, u32[]{:S(2)}, u32[]{:S(2)}) async-start(bf16[4,256,256]{2,1,0:T(8,128)(2,1)} %get-tuple-element.1270), calls=%async_computation.4 | async-start | bytes 1048576 | tf_op jit(solution)/shard_map/all_to_all | solution.py:912
  192.6 6.5 %collective-permute-done.43.refs_7_ = bf16[64,2048]{1,0:T(8,128)(2,1)S(1)} collective-permute-done((bf16[64,2048]{1,0:T(8,128)(2,1)}, bf16[64,2048]{1,0:T(8,128)(2,1)S(1)}, u32[]{:S(2)}, u32[]{:S(2)}) %collective-permute-start.43) | collective-permute-done | bytes 262176 | tf_op jit(solution)/shard_map/ppermute | solution.py:352
  203.6 4.2 all-to-all-start.5
  208.3 9.3 %shard_map.208 = (bf16[1024,2048]{1,0:T(8,128)(2,1)}, bf16[1024,512]{1,0:T(8,128)(2,1)S(1)}, bf16[1024,512]{1,0:T(8,128)(2,1)}, bf16[1024,512]{1,0:T(8,128)(2,1)}) custom-call(bf16[64,2048]{1,0:T(8,128)(2,1)} %multiply_convert_fusion.refs_0_, bf16[64,2048]{1,0:T(8,128)(2,1)} %collective-permute-done.32.refs_1_, ...), custom_call_target="tpu_custom_call" | custom-call | flops 4294967296 | bytes 17825792 | tf_op jit(solution)/shard_map/pallas_call | solution.py:471
  218.6 3.1 all-to-all-done.5
  222.2 4.9 convolution_convert_fusion.2
  227.1 2.7 pad_maximum_fusion
  229.8 2.7 pad_maximum_fusion.1
  235.6 7.0 %shard_map.209 = (bf16[1024,512]{1,0:T(8,128)(2,1)}, bf16[1024,512]{1,0:T(8,128)(2,1)}) custom-call(bf16[1024,2048]{1,0:T(8,128)(2,1)} %shard_map.207.cot_ref, bf16[1024,256]{1,0:T(8,128)(2,1)} %bitcast.24.refs_0_, bf16[1024,256]{1,0:T(8,128)(2,1)} %bitcast.25.refs_1_, bf16[1024,256]{1,0:T(8,128)(2,1)} %bitcast.26.refs_2_, bf16[1024,256]{1,0:T(8,128)(2,1)} %bitcast.164, ...), custom_call_target="tpu_custom_call" | custom-call | flops 2147483648 | bytes 12582912 | tf_op jit(solution)/shard_map/pallas_call | solution.py:510
  254.7 2.4 convolution_convert_fusion.1
  259.7 2.4 convolution_convert_fusion
  263.7 6.5 %collective-permute-done.56 = bf16[128,2048]{1,0:T(8,128)(2,1)S(1)} collective-permute-done((bf16[128,2048]{1,0:T(8,128)(2,1)S(1)}, bf16[128,2048]{1,0:T(8,128)(2,1)S(1)}, u32[]{:S(2)}, u32[]{:S(2)}) %collective-permute-start.56) | collective-permute-done | bytes 524320 | tf_op jit(solution)/shard_map/ppermute | solution.py:352
  273.3 2.9 maximum_maximum_fusion
  276.1 5.1 %collective-permute-done.61 = bf16[64,2048]{1,0:T(8,128)(2,1)S(1)} collective-permute-done((bf16[64,2048]{1,0:T(8,128)(2,1)S(1)}, bf16[64,2048]{1,0:T(8,128)(2,1)S(1)}, u32[]{:S(2)}, u32[]{:S(2)}) %collective-permute-start.61) | collective-permute-done | bytes 262176 | tf_op jit(solution)/shard_map/ppermute | solution.py:352
  281.3 2.6 collective-permute-done.60
  289.1 11.3 %collective-permute-done.63.refs_2_ = bf16[64,2048]{1,0:T(8,128)(2,1)S(1)} collective-permute-done((bf16[64,2048]{1,0:T(8,128)(2,1)S(1)}, bf16[64,2048]{1,0:T(8,128)(2,1)S(1)}, u32[]{:S(2)}, u32[]{:S(2)}) %collective-permute-start.63) | collective-permute-done | bytes 262176 | tf_op jit(solution)/shard_map/ppermute | solution.py:352
  302.0 6.6 %collective-permute-done.67.refs_3_ = bf16[64,2048]{1,0:T(8,128)(2,1)S(1)} collective-permute-done((bf16[64,2048]{1,0:T(8,128)(2,1)S(1)}, bf16[64,2048]{1,0:T(8,128)(2,1)S(1)}, u32[]{:S(2)}, u32[]{:S(2)}) %collective-permute-start.67) | collective-permute-done | bytes 262176 | tf_op jit(solution)/shard_map/ppermute | solution.py:352
  310.0 3.9 all-to-all-start.6
  316.4 6.7 %collective-permute-done.69.refs_5_ = bf16[64,2048]{1,0:T(8,128)(2,1)S(1)} collective-permute-done((bf16[64,2048]{1,0:T(8,128)(2,1)S(1)}, bf16[64,2048]{1,0:T(8,128)(2,1)S(1)}, u32[]{:S(2)}, u32[]{:S(2)}) %collective-permute-start.69) | collective-permute-done | bytes 262176 | tf_op jit(solution)/shard_map/ppermute | solution.py:352
  323.1 5.6 %collective-permute-done.70.refs_6_ = bf16[64,2048]{1,0:T(8,128)(2,1)S(1)} collective-permute-done((bf16[64,2048]{1,0:T(8,128)(2,1)S(1)}, bf16[64,2048]{1,0:T(8,128)(2,1)S(1)}, u32[]{:S(2)}, u32[]{:S(2)}) %collective-permute-start.70) | collective-permute-done | bytes 262176 | tf_op jit(solution)/shard_map/ppermute | solution.py:352
  329.2 2.8 add_convert_fusion.2
  334.5 4.4 all-to-all-done.6
  339.9 4.3 all-to-all-start.7
  344.1 12.5 %shard_map.210 = (bf16[1024,384]{1,0:T(8,128)(2,1)S(1)}, bf16[1024,128]{1,0:T(8,128)(2,1)S(1)}, bf16[1024,128]{1,0:T(8,128)(2,1)S(1)}) custom-call(bf16[64,2048]{1,0:T(8,128)(2,1)} %copy-done.53, bf16[64,2048]{1,0:T(8,128)(2,1)} %copy-done.73, bf16[64,2048]{1,0:T(8,128)(2,1)} %copy-done.71, bf16[64,2048]{1,0:T(8,128)(2,1)} %copy-done.76, ...), custom_call_target="tpu_custom_call" | custom-call | flops 3758096384 | bytes 7340032 | tf_op jit(solution)/shard_map/pallas_call | solution.py:761
  360.2 9.2 %all-to-all-done.7 = bf16[4,256,512]{2,1,0:T(8,128)(2,1)} async-done(((bf16[4,256,512]{2,1,0:T(8,128)(2,1)}), bf16[4,256,512]{2,1,0:T(8,128)(2,1)}, u32[]{:S(2)}, u32[]{:S(2)}) %all-to-all-start.7) | async-done | bytes 1048608 | tf_op jit(solution)/shard_map/all_to_all | solution.py:912
  369.4 2.2 add_convert_fusion.18
  383.3 2.5 add_convert_fusion
  385.8 4.4 all-to-all-start.8
  390.2 2.5 convolution_convert_fusion.5
  393.7 2.4 convolution_convert_fusion.3
  405.7 2.9 collective-permute-start.90
  412.1 6.0 %collective-permute-done.89 = bf16[128,2048]{1,0:T(8,128)(2,1)} collective-permute-done((bf16[128,2048]{1,0:T(8,128)(2,1)}, bf16[128,2048]{1,0:T(8,128)(2,1)}, u32[]{:S(2)}, u32[]{:S(2)}) %collective-permute-start.89) | collective-permute-done | bytes 524320 | tf_op jit(solution)/shard_map/ppermute | solution.py:352
  419.0 7.6 %collective-permute-done.91 = bf16[64,2048]{1,0:T(8,128)(2,1)S(1)} collective-permute-done((bf16[64,2048]{1,0:T(8,128)(2,1)}, bf16[64,2048]{1,0:T(8,128)(2,1)S(1)}, u32[]{:S(2)}, u32[]{:S(2)}) %collective-permute-start.91) | collective-permute-done | bytes 262176 | tf_op jit(solution)/shard_map/ppermute | solution.py:352
  429.8 2.2 collective-permute-start.95
  438.3 3.8 collective-permute-done.95
  442.1 3.2 collective-permute-done.94
  449.1 3.5 all-to-all-start.9
  462.4 2.2 shard_map.212
  464.6 2.7 shard_map.211
  467.4 11.5 %all-to-all-done.9 = bf16[4,256,512]{2,1,0:T(8,128)(2,1)S(1)} async-done(((bf16[4,256,512]{2,1,0:T(8,128)(2,1)}), bf16[4,256,512]{2,1,0:T(8,128)(2,1)S(1)}, u32[]{:S(2)}, u32[]{:S(2)}) %all-to-all-start.9) | async-done | bytes 1048608 | tf_op jit(solution)/shard_map/all_to_all | solution.py:912
  (476 shorter events, 147.7 us)
Async XLA Ops:
  4.4 17.9 %collective-permute-start.1 = (bf16[64,2048]{1,0:T(8,128)(2,1)S(1)}, bf16[64,2048]{1,0:T(8,128)(2,1)}, u32[]{:S(2)}, u32[]{:S(2)}) collective-permute-start(bf16[64,2048]{1,0:T(8,128)(2,1)S(1)} %constant_dynamic-slice_fusion.1), channel_id=1, source_target_pairs={{0,8},{4,12},{8,0},{12,4},{1,9},{5,13},{9,1},{13,5},{2,10},{6,14},... | collective-permute-start | bytes 786440 | tf_op jit(solution)/shard_map/ppermute | solution.py:352
  8.5 14.5 %collective-permute-start = (bf16[64,2048]{1,0:T(8,128)(2,1)S(1)}, bf16[64,2048]{1,0:T(8,128)(2,1)}, u32[]{:S(2)}, u32[]{:S(2)}) collective-permute-start(bf16[64,2048]{1,0:T(8,128)(2,1)S(1)} %constant_dynamic-slice_fusion.1), channel_id=1, source_target_pairs={{0,4},{4,0},{8,12},{12,8},{1,5},{5,1},{9,13},{13,9},{2,6},{6,2},{1... | collective-permute-start | bytes 786440 | tf_op jit(solution)/shard_map/ppermute | solution.py:352
  10.1 33.2 %all-to-all-start = ((bf16[4,272,384]{2,1,0:T(8,128)(2,1)}), bf16[4,272,384]{2,1,0:T(8,128)(2,1)S(1)}, u32[]{:S(2)}, u32[]{:S(2)}) async-start(bf16[4,272,384]{2,1,0:T(8,128)(2,1)} %shard_map.203), calls=%async_computation | async-start | bytes 1671168 | tf_op jit(solution)/shard_map/all_to_all | solution.py:912
  23.0 20.3 %collective-permute-start.4 = (bf16[64,2048]{1,0:T(8,128)(2,1)}, bf16[64,2048]{1,0:T(8,128)(2,1)}, u32[]{:S(2)}, u32[]{:S(2)}) collective-permute-start(bf16[64,2048]{1,0:T(8,128)(2,1)} %collective-permute-done.1.refs_1_), channel_id=1, source_target_pairs={{0,2},{2,0},{1,3},{3,1},{4,6},{6,4},{5,7},{7,5},{8,10},{10,8},{9,1... | collective-permute-start | bytes 786440 | tf_op jit(solution)/shard_map/ppermute | solution.py:352
  26.7 13.1 %collective-permute-start.2 = (bf16[64,2048]{1,0:T(8,128)(2,1)}, bf16[64,2048]{1,0:T(8,128)(2,1)}, u32[]{:S(2)}, u32[]{:S(2)}) collective-permute-start(bf16[64,2048]{1,0:T(8,128)(2,1)} %collective-permute-done.1.refs_1_), channel_id=1, source_target_pairs={{0,4},{4,0},{8,12},{12,8},{1,5},{5,1},{9,13},{13,9},{2,6},{6,2},{1... | collective-permute-start | bytes 786440 | tf_op jit(solution)/shard_map/ppermute | solution.py:352
  26.9 16.3 %collective-permute-start.3 = (bf16[64,2048]{1,0:T(8,128)(2,1)}, bf16[64,2048]{1,0:T(8,128)(2,1)}, u32[]{:S(2)}, u32[]{:S(2)}) collective-permute-start(bf16[64,2048]{1,0:T(8,128)(2,1)} %collective-permute-done.refs_0_), channel_id=1, source_target_pairs={{0,2},{2,0},{1,3},{3,1},{4,6},{6,4},{5,7},{7,5},{8,10},{10,8},{9,1... | collective-permute-start | bytes 786440 | tf_op jit(solution)/shard_map/ppermute | solution.py:352
  43.3 22.3 %collective-permute-start.11 = (bf16[4,272,384]{2,1,0:T(8,128)(2,1)S(1)}, bf16[4,272,384]{2,1,0:T(8,128)(2,1)S(1)}, u32[]{:S(2)}, u32[]{:S(2)}) collective-permute-start(bf16[4,272,384]{2,1,0:T(8,128)(2,1)S(1)} %all-to-all-done.refs_13_), channel_id=1, source_target_pairs={{0,16},{16,0},{1,17},{17,1},{2,18},{18,2},{3,19},{19,3},{4,20},{20... | collective-permute-start | bytes 2506760 | tf_op jit(solution)/shard_map/ppermute | solution.py:352
  44.9 13.0 %all-to-all-start.1 = ((bf16[4,128,256]{2,1,0:T(8,128)(2,1)}), bf16[4,128,256]{2,1,0:T(8,128)(2,1)S(1)}, u32[]{:S(2)}, u32[]{:S(2)}) async-start(bf16[4,128,256]{2,1,0:T(8,128)(2,1)} %bitcast), calls=%async_computation.1 | async-start | bytes 524288 | tf_op jit(solution)/shard_map/all_to_all | solution.py:912
  58.6 20.4 %collective-permute-start.14 = (bf16[64,2048]{1,0:T(8,128)(2,1)S(1)}, bf16[64,2048]{1,0:T(8,128)(2,1)}, u32[]{:S(2)}, u32[]{:S(2)}) collective-permute-start(bf16[64,2048]{1,0:T(8,128)(2,1)S(1)} %constant_dynamic-slice_fusion), channel_id=1, source_target_pairs={{0,8},{4,12},{8,0},{12,4},{1,9},{5,13},{9,1},{13,5},{2,10},{6,14},... | collective-permute-start | bytes 786440 | tf_op jit(solution)/shard_map/ppermute | solution.py:352
  58.6 20.4 %collective-permute-start.13 = (bf16[64,2048]{1,0:T(8,128)(2,1)S(1)}, bf16[64,2048]{1,0:T(8,128)(2,1)S(1)}, u32[]{:S(2)}, u32[]{:S(2)}) collective-permute-start(bf16[64,2048]{1,0:T(8,128)(2,1)S(1)} %constant_dynamic-slice_fusion), channel_id=1, source_target_pairs={{0,4},{4,0},{8,12},{12,8},{1,5},{5,1},{9,13},{13,9},{2,6},{6,2},{1... | collective-permute-start | bytes 786440 | tf_op jit(solution)/shard_map/ppermute | solution.py:352
  61.9 32.0 %all-to-all-start.2 = ((bf16[4,256,512]{2,1,0:T(8,128)(2,1)}), bf16[4,256,512]{2,1,0:T(8,128)(2,1)S(1)}, u32[]{:S(2)}, u32[]{:S(2)}) async-start(bf16[4,256,512]{2,1,0:T(8,128)(2,1)} %pad_maximum_fusion.4), calls=%async_computation.2 | async-start | bytes 2097152 | tf_op jit(solution)/shard_map/all_to_all | solution.py:912
  65.7 13.4 %collective-permute-start.15 = (bf16[4,128,256]{2,1,0:T(8,128)(2,1)}, bf16[4,128,256]{2,1,0:T(8,128)(2,1)}, u32[]{:S(2)}, u32[]{:S(2)}) collective-permute-start(bf16[4,128,256]{2,1,0:T(8,128)(2,1)} %copy-done.62), channel_id=1, source_target_pairs={{0,16},{16,0},{1,17},{17,1},{2,18},{18,2},{3,19},{19,3},{4,20},{20... | collective-permute-start | bytes 786440 | tf_op jit(solution)/shard_map/ppermute | solution.py:352
  93.9 20.4 %collective-permute-start.20 = (bf16[256,2048]{1,0:T(8,128)(2,1)}, bf16[256,2048]{1,0:T(8,128)(2,1)}, u32[]{:S(2)}, u32[]{:S(2)}) collective-permute-start(bf16[256,2048]{1,0:T(8,128)(2,1)} %get-tuple-element.1084), channel_id=1, source_target_pairs={{0,1},{1,0},{2,3},{3,2},{4,5},{5,4},{6,7},{7,6},{8,9},{9,8},{10,11... | collective-permute-start | bytes 3145736 | tf_op jit(solution)/shard_map/ppermute | solution.py:352
  94.5 14.3 %collective-permute-start.18 = (bf16[64,2048]{1,0:T(8,128)(2,1)}, bf16[64,2048]{1,0:T(8,128)(2,1)}, u32[]{:S(2)}, u32[]{:S(2)}) collective-permute-start(bf16[64,2048]{1,0:T(8,128)(2,1)} %collective-permute-done.14.refs_2_), channel_id=1, source_target_pairs={{0,2},{2,0},{1,3},{3,1},{4,6},{6,4},{5,7},{7,5},{8,10},{10,8},{9,1... | collective-permute-start | bytes 786440 | tf_op jit(solution)/shard_map/ppermute | solution.py:352
  96.0 34.4 %all-to-all-start.3 = ((bf16[4,256,512]{2,1,0:T(8,128)(2,1)}), bf16[4,256,512]{2,1,0:T(8,128)(2,1)S(1)}, u32[]{:S(2)}, u32[]{:S(2)}) async-start(bf16[4,256,512]{2,1,0:T(8,128)(2,1)} %pad_maximum_fusion.3), calls=%async_computation.3 | async-start | bytes 2097152 | tf_op jit(solution)/shard_map/all_to_all | solution.py:912
  108.8 16.9 %collective-permute-start.24 = (bf16[64,2048]{1,0:T(8,128)(2,1)}, bf16[64,2048]{1,0:T(8,128)(2,1)S(1)}, u32[]{:S(2)}, u32[]{:S(2)}) collective-permute-start(bf16[64,2048]{1,0:T(8,128)(2,1)} %collective-permute-done.14.refs_2_), channel_id=1, source_target_pairs={{0,4},{4,0},{8,12},{12,8},{1,5},{5,1},{9,13},{13,9},{2,6},{6,2},{1... | collective-permute-start | bytes 786440 | tf_op jit(solution)/shard_map/ppermute | solution.py:352
  108.8 16.9 %collective-permute-start.23 = (bf16[128,2048]{1,0:T(8,128)(2,1)S(1)}, bf16[128,2048]{1,0:T(8,128)(2,1)S(1)}, u32[]{:S(2)}, u32[]{:S(2)}) collective-permute-start(bf16[128,2048]{1,0:T(8,128)(2,1)S(1)} %add_convert_fusion.7), channel_id=1, source_target_pairs={{0,2},{2,0},{1,3},{3,1},{4,6},{6,4},{5,7},{7,5},{8,10},{10,8},{9,1... | collective-permute-start | bytes 1572872 | tf_op jit(solution)/shard_map/ppermute | solution.py:352
  109.4 25.6 %collective-permute-start.26 = (bf16[4,256,512]{2,1,0:T(8,128)(2,1)S(1)}, bf16[4,256,512]{2,1,0:T(8,128)(2,1)}, u32[]{:S(2)}, u32[]{:S(2)}) collective-permute-start(bf16[4,256,512]{2,1,0:T(8,128)(2,1)S(1)} %all-to-all-done.2), channel_id=1, source_target_pairs={{0,16},{16,0},{1,17},{17,1},{2,18},{18,2},{3,19},{19,3},{4,20},{20... | collective-permute-start | bytes 3145736 | tf_op jit(solution)/shard_map/ppermute | solution.py:352
  115.4 14.9 %collective-permute-start.25 = (bf16[64,2048]{1,0:T(8,128)(2,1)S(1)}, bf16[64,2048]{1,0:T(8,128)(2,1)}, u32[]{:S(2)}, u32[]{:S(2)}) collective-permute-start(bf16[64,2048]{1,0:T(8,128)(2,1)S(1)} %add_convert_fusion.27), channel_id=1, source_target_pairs={{0,4},{4,0},{8,12},{12,8},{1,5},{5,1},{9,13},{13,9},{2,6},{6,2},{1... | collective-permute-start | bytes 786440 | tf_op jit(solution)/shard_map/ppermute | solution.py:352
  115.5 20.1 %collective-permute-start.27 = (bf16[64,2048]{1,0:T(8,128)(2,1)}, bf16[64,2048]{1,0:T(8,128)(2,1)}, u32[]{:S(2)}, u32[]{:S(2)}) collective-permute-start(bf16[64,2048]{1,0:T(8,128)(2,1)} %get-tuple-element.1150), channel_id=1, source_target_pairs={{0,2},{2,0},{1,3},{3,1},{4,6},{6,4},{5,7},{7,5},{8,10},{10,8},{9,1... | collective-permute-start | bytes 786440 | tf_op jit(solution)/shard_map/ppermute | solution.py:352
  132.0 14.3 %collective-permute-start.29 = (bf16[64,2048]{1,0:T(8,128)(2,1)S(1)}, bf16[64,2048]{1,0:T(8,128)(2,1)S(1)}, u32[]{:S(2)}, u32[]{:S(2)}) collective-permute-start(bf16[64,2048]{1,0:T(8,128)(2,1)S(1)} %get-tuple-element.1871), channel_id=1, source_target_pairs={{0,4},{4,0},{8,12},{12,8},{1,5},{5,1},{9,13},{13,9},{2,6},{6,2},{1... | collective-permute-start | bytes 786440 | tf_op jit(solution)/shard_map/ppermute | solution.py:352
  132.4 13.9 %collective-permute-start.28 = (bf16[64,2048]{1,0:T(8,128)(2,1)S(1)}, bf16[64,2048]{1,0:T(8,128)(2,1)S(1)}, u32[]{:S(2)}, u32[]{:S(2)}) collective-permute-start(bf16[64,2048]{1,0:T(8,128)(2,1)S(1)} %get-tuple-element.1872), channel_id=1, source_target_pairs={{0,8},{4,12},{8,0},{12,4},{1,9},{5,13},{9,1},{13,5},{2,10},{6,14},... | collective-permute-start | bytes 786440 | tf_op jit(solution)/shard_map/ppermute | solution.py:352
  135.0 13.4 %collective-permute-start.31 = (bf16[64,2048]{1,0:T(8,128)(2,1)S(1)}, bf16[64,2048]{1,0:T(8,128)(2,1)S(1)}, u32[]{:S(2)}, u32[]{:S(2)}) collective-permute-start(bf16[64,2048]{1,0:T(8,128)(2,1)S(1)} %copy-done.52), channel_id=1, source_target_pairs={{0,2},{2,0},{1,3},{3,1},{4,6},{6,4},{5,7},{7,5},{8,10},{10,8},{9,1... | collective-permute-start | bytes 786440 | tf_op jit(solution)/shard_map/ppermute | solution.py:352
  135.6 37.5 %collective-permute-start.38 = (bf16[4,256,512]{2,1,0:T(8,128)(2,1)S(1)}, bf16[4,256,512]{2,1,0:T(8,128)(2,1)}, u32[]{:S(2)}, u32[]{:S(2)}) collective-permute-start(bf16[4,256,512]{2,1,0:T(8,128)(2,1)S(1)} %all-to-all-done.3), channel_id=1, source_target_pairs={{0,16},{16,0},{1,17},{17,1},{2,18},{18,2},{3,19},{19,3},{4,20},{20... | collective-permute-start | bytes 3145736 | tf_op jit(solution)/shard_map/ppermute | solution.py:352
  150.0 15.3 %collective-permute-start.33 = (bf16[64,2048]{1,0:T(8,128)(2,1)}, bf16[64,2048]{1,0:T(8,128)(2,1)}, u32[]{:S(2)}, u32[]{:S(2)}) collective-permute-start(bf16[64,2048]{1,0:T(8,128)(2,1)} %multiply_convert_fusion.refs_0_), channel_id=1, source_target_pairs={{0,8},{4,12},{8,0},{12,4},{1,9},{5,13},{9,1},{13,5},{2,10},{6,14},... | collective-permute-start | bytes 786440 | tf_op jit(solution)/shard_map/ppermute | solution.py:352
  151.4 14.1 %collective-permute-start.32 = (bf16[64,2048]{1,0:T(8,128)(2,1)}, bf16[64,2048]{1,0:T(8,128)(2,1)}, u32[]{:S(2)}, u32[]{:S(2)}) collective-permute-start(bf16[64,2048]{1,0:T(8,128)(2,1)} %multiply_convert_fusion.refs_0_), channel_id=1, source_target_pairs={{0,4},{4,0},{8,12},{12,8},{1,5},{5,1},{9,13},{13,9},{2,6},{6,2},{1... | collective-permute-start | bytes 786440 | tf_op jit(solution)/shard_map/ppermute | solution.py:352
  155.3 17.4 %collective-permute-start.39 = (bf16[64,2048]{1,0:T(8,128)(2,1)}, bf16[64,2048]{1,0:T(8,128)(2,1)}, u32[]{:S(2)}, u32[]{:S(2)}) collective-permute-start(bf16[64,2048]{1,0:T(8,128)(2,1)} %multiply_convert_fusion.refs_0_), channel_id=1, source_target_pairs={{0,2},{2,0},{1,3},{3,1},{4,6},{6,4},{5,7},{7,5},{8,10},{10,8},{9,1... | collective-permute-start | bytes 786440 | tf_op jit(solution)/shard_map/ppermute | solution.py:352
  165.7 24.9 %collective-permute-start.42 = (bf16[64,2048]{1,0:T(8,128)(2,1)}, bf16[64,2048]{1,0:T(8,128)(2,1)}, u32[]{:S(2)}, u32[]{:S(2)}) collective-permute-start(bf16[64,2048]{1,0:T(8,128)(2,1)} %collective-permute-done.33.refs_2_), channel_id=1, source_target_pairs={{0,2},{2,0},{1,3},{3,1},{4,6},{6,4},{5,7},{7,5},{8,10},{10,8},{9,1... | collective-permute-start | bytes 786440 | tf_op jit(solution)/shard_map/ppermute | solution.py:352
  166.3 23.9 %collective-permute-start.41 = (bf16[64,2048]{1,0:T(8,128)(2,1)}, bf16[64,2048]{1,0:T(8,128)(2,1)}, u32[]{:S(2)}, u32[]{:S(2)}) collective-permute-start(bf16[64,2048]{1,0:T(8,128)(2,1)} %collective-permute-done.32.refs_1_), channel_id=1, source_target_pairs={{0,2},{2,0},{1,3},{3,1},{4,6},{6,4},{5,7},{7,5},{8,10},{10,8},{9,1... | collective-permute-start | bytes 786440 | tf_op jit(solution)/shard_map/ppermute | solution.py:352
  173.1 30.5 %all-to-all-start.4 = ((bf16[4,256,256]{2,1,0:T(8,128)(2,1)}), bf16[4,256,256]{2,1,0:T(8,128)(2,1)}, u32[]{:S(2)}, u32[]{:S(2)}) async-start(bf16[4,256,256]{2,1,0:T(8,128)(2,1)} %get-tuple-element.1270), calls=%async_computation.4 | async-start | bytes 1048576 | tf_op jit(solution)/shard_map/all_to_all | solution.py:912
  203.6 18.1 %all-to-all-start.5 = ((bf16[4,256,256]{2,1,0:T(8,128)(2,1)}), bf16[4,256,256]{2,1,0:T(8,128)(2,1)}, u32[]{:S(2)}, u32[]{:S(2)}) async-start(bf16[4,256,256]{2,1,0:T(8,128)(2,1)} %get-tuple-element.1318), calls=%async_computation.5 | async-start | bytes 1048576 | tf_op jit(solution)/shard_map/all_to_all | solution.py:912
  207.7 26.2 %collective-permute-start.51 = (bf16[4,256,256]{2,1,0:T(8,128)(2,1)}, bf16[4,256,256]{2,1,0:T(8,128)(2,1)}, u32[]{:S(2)}, u32[]{:S(2)}) collective-permute-start(bf16[4,256,256]{2,1,0:T(8,128)(2,1)} %all-to-all-done.4), channel_id=1, source_target_pairs={{0,16},{16,0},{1,17},{17,1},{2,18},{18,2},{3,19},{19,3},{4,20},{20... | collective-permute-start | bytes 1572872 | tf_op jit(solution)/shard_map/ppermute | solution.py:352
  221.7 13.1 %collective-permute-start.52 = (bf16[4,256,256]{2,1,0:T(8,128)(2,1)}, bf16[4,256,256]{2,1,0:T(8,128)(2,1)S(1)}, u32[]{:S(2)}, u32[]{:S(2)}) collective-permute-start(bf16[4,256,256]{2,1,0:T(8,128)(2,1)} %all-to-all-done.5), channel_id=1, source_target_pairs={{0,16},{16,0},{1,17},{17,1},{2,18},{18,2},{3,19},{19,3},{4,20},{20... | collective-permute-start | bytes 1572872 | tf_op jit(solution)/shard_map/ppermute | solution.py:352
  245.7 30.4 %collective-permute-start.58 = (bf16[1024,512]{1,0:T(8,128)(2,1)S(1)}, bf16[1024,512]{1,0:T(8,128)(2,1)S(1)}, u32[]{:S(2)}, u32[]{:S(2)}) collective-permute-start(bf16[1024,512]{1,0:T(8,128)(2,1)S(1)} %copy-done.41), channel_id=1, source_target_pairs={{0,16},{16,0},{1,17},{17,1},{2,18},{18,2},{3,19},{19,3},{4,20},{20... | collective-permute-start | bytes 3145736 | tf_op jit(solution)/shard_map/ppermute | solution.py:352
  250.3 19.8 %collective-permute-start.56 = (bf16[128,2048]{1,0:T(8,128)(2,1)S(1)}, bf16[128,2048]{1,0:T(8,128)(2,1)S(1)}, u32[]{:S(2)}, u32[]{:S(2)}) collective-permute-start(bf16[128,2048]{1,0:T(8,128)(2,1)S(1)} %add_convert_fusion.6), channel_id=1, source_target_pairs={{0,2},{2,0},{1,3},{3,1},{4,6},{6,4},{5,7},{7,5},{8,10},{10,8},{9,1... | collective-permute-start | bytes 1572872 | tf_op jit(solution)/shard_map/ppermute | solution.py:352
  259.1 17.0 %collective-permute-start.59 = (bf16[64,2048]{1,0:T(8,128)(2,1)S(1)}, bf16[64,2048]{1,0:T(8,128)(2,1)S(1)}, u32[]{:S(2)}, u32[]{:S(2)}) collective-permute-start(bf16[64,2048]{1,0:T(8,128)(2,1)S(1)} %get-tuple-element.1547), channel_id=1, source_target_pairs={{0,2},{2,0},{1,3},{3,1},{4,6},{6,4},{5,7},{7,5},{8,10},{10,8},{9,1... | collective-permute-start | bytes 786440 | tf_op jit(solution)/shard_map/ppermute | solution.py:352
  270.5 13.3 %collective-permute-start.60 = (bf16[64,2048]{1,0:T(8,128)(2,1)S(1)}, bf16[64,2048]{1,0:T(8,128)(2,1)S(1)}, u32[]{:S(2)}, u32[]{:S(2)}) collective-permute-start(bf16[64,2048]{1,0:T(8,128)(2,1)S(1)} %get-tuple-element.1870), channel_id=1, source_target_pairs={{0,8},{4,12},{8,0},{12,4},{1,9},{5,13},{9,1},{13,5},{2,10},{6,14},... | collective-permute-start | bytes 786440 | tf_op jit(solution)/shard_map/ppermute | solution.py:352
  272.6 29.5 %collective-permute-start.65 = (bf16[1024,512]{1,0:T(8,128)(2,1)S(1)}, bf16[1024,512]{1,0:T(8,128)(2,1)S(1)}, u32[]{:S(2)}, u32[]{:S(2)}) collective-permute-start(bf16[1024,512]{1,0:T(8,128)(2,1)S(1)} %get-tuple-element.1607), channel_id=1, source_target_pairs={{0,16},{16,0},{1,17},{17,1},{2,18},{18,2},{3,19},{19,3},{4,20},{20... | collective-permute-start | bytes 3145736 | tf_op jit(solution)/shard_map/ppermute | solution.py:352
  286.3 14.1 %collective-permute-start.63 = (bf16[64,2048]{1,0:T(8,128)(2,1)S(1)}, bf16[64,2048]{1,0:T(8,128)(2,1)S(1)}, u32[]{:S(2)}, u32[]{:S(2)}) collective-permute-start(bf16[64,2048]{1,0:T(8,128)(2,1)S(1)} %get-tuple-element.1695.refs_0_), channel_id=1, source_target_pairs={{0,8},{4,12},{8,0},{12,4},{1,9},{5,13},{9,1},{13,5},{2,10},{6,14},... | collective-permute-start | bytes 786440 | tf_op jit(solution)/shard_map/ppermute | solution.py:352
  286.6 14.0 %collective-permute-start.62 = (bf16[64,2048]{1,0:T(8,128)(2,1)S(1)}, bf16[64,2048]{1,0:T(8,128)(2,1)S(1)}, u32[]{:S(2)}, u32[]{:S(2)}) collective-permute-start(bf16[64,2048]{1,0:T(8,128)(2,1)S(1)} %get-tuple-element.1695.refs_0_), channel_id=1, source_target_pairs={{0,4},{4,0},{8,12},{12,8},{1,5},{5,1},{9,13},{13,9},{2,6},{6,2},{1... | collective-permute-start | bytes 786440 | tf_op jit(solution)/shard_map/ppermute | solution.py:352
  288.3 13.7 %collective-permute-start.66 = (bf16[64,2048]{1,0:T(8,128)(2,1)S(1)}, bf16[64,2048]{1,0:T(8,128)(2,1)S(1)}, u32[]{:S(2)}, u32[]{:S(2)}) collective-permute-start(bf16[64,2048]{1,0:T(8,128)(2,1)S(1)} %get-tuple-element.1695.refs_0_), channel_id=1, source_target_pairs={{0,2},{2,0},{1,3},{3,1},{4,6},{6,4},{5,7},{7,5},{8,10},{10,8},{9,1... | collective-permute-start | bytes 786440 | tf_op jit(solution)/shard_map/ppermute | solution.py:352
  301.0 27.8 %collective-permute-start.68 = (bf16[1024,512]{1,0:T(8,128)(2,1)}, bf16[1024,512]{1,0:T(8,128)(2,1)}, u32[]{:S(2)}, u32[]{:S(2)}) collective-permute-start(bf16[1024,512]{1,0:T(8,128)(2,1)} %get-tuple-element.1634), channel_id=1, source_target_pairs={{0,16},{16,0},{1,17},{17,1},{2,18},{18,2},{3,19},{19,3},{4,20},{20... | collective-permute-start | bytes 3145736 | tf_op jit(solution)/shard_map/ppermute | solution.py:352
  310.0 28.9 %all-to-all-start.6 = ((bf16[4,256,512]{2,1,0:T(8,128)(2,1)}), bf16[4,256,512]{2,1,0:T(8,128)(2,1)S(1)}, u32[]{:S(2)}, u32[]{:S(2)}) async-start(bf16[4,256,512]{2,1,0:T(8,128)(2,1)} %bitcast.162), calls=%async_computation.6 | async-start | bytes 2097152 | tf_op jit(solution)/shard_map/all_to_all | solution.py:912
  314.4 14.3 %collective-permute-start.70 = (bf16[64,2048]{1,0:T(8,128)(2,1)S(1)}, bf16[64,2048]{1,0:T(8,128)(2,1)S(1)}, u32[]{:S(2)}, u32[]{:S(2)}) collective-permute-start(bf16[64,2048]{1,0:T(8,128)(2,1)S(1)} %copy-done.72), channel_id=1, source_target_pairs={{0,2},{2,0},{1,3},{3,1},{4,6},{6,4},{5,7},{7,5},{8,10},{10,8},{9,1... | collective-permute-start | bytes 786440 | tf_op jit(solution)/shard_map/ppermute | solution.py:352
  315.9 16.2 %collective-permute-start.74 = (bf16[64,2048]{1,0:T(8,128)(2,1)S(1)}, bf16[64,2048]{1,0:T(8,128)(2,1)S(1)}, u32[]{:S(2)}, u32[]{:S(2)}) collective-permute-start(bf16[64,2048]{1,0:T(8,128)(2,1)S(1)} %collective-permute-done.67.refs_3_), channel_id=1, source_target_pairs={{0,1},{1,0},{2,3},{3,2},{4,5},{5,4},{6,7},{7,6},{8,9},{9,8},{10,11... | collective-permute-start | bytes 786440 | tf_op jit(solution)/shard_map/ppermute | solution.py:352
  315.9 16.3 %collective-permute-start.71 = (bf16[64,2048]{1,0:T(8,128)(2,1)S(1)}, bf16[64,2048]{1,0:T(8,128)(2,1)S(1)}, u32[]{:S(2)}, u32[]{:S(2)}) collective-permute-start(bf16[64,2048]{1,0:T(8,128)(2,1)S(1)} %collective-permute-done.67.refs_3_), channel_id=1, source_target_pairs={{0,2},{2,0},{1,3},{3,1},{4,6},{6,4},{5,7},{7,5},{8,10},{10,8},{9,1... | collective-permute-start | bytes 786440 | tf_op jit(solution)/shard_map/ppermute | solution.py:352
  339.9 29.5 %all-to-all-start.7 = ((bf16[4,256,512]{2,1,0:T(8,128)(2,1)}), bf16[4,256,512]{2,1,0:T(8,128)(2,1)}, u32[]{:S(2)}, u32[]{:S(2)}) async-start(bf16[4,256,512]{2,1,0:T(8,128)(2,1)} %bitcast.161), calls=%async_computation.7 | async-start | bytes 2097152 | tf_op jit(solution)/shard_map/all_to_all | solution.py:912
  357.4 40.0 %collective-permute-start.83 = (bf16[1024,128]{1,0:T(8,128)(2,1)S(1)}, bf16[1024,128]{1,0:T(8,128)(2,1)S(1)}, u32[]{:S(2)}, u32[]{:S(2)}) collective-permute-start(bf16[1024,128]{1,0:T(8,128)(2,1)S(1)} %get-tuple-element.1765), channel_id=1, source_target_pairs={{0,16},{16,0},{1,17},{17,1},{2,18},{18,2},{3,19},{19,3},{4,20},{20... | collective-permute-start | bytes 786440 | tf_op jit(solution)/shard_map/ppermute | solution.py:352
  376.9 22.1 %collective-permute-start.84 = (bf16[128,2048]{1,0:T(8,128)(2,1)S(1)}, bf16[128,2048]{1,0:T(8,128)(2,1)}, u32[]{:S(2)}, u32[]{:S(2)}) collective-permute-start(bf16[128,2048]{1,0:T(8,128)(2,1)S(1)} %add_convert_fusion.5), channel_id=1, source_target_pairs={{0,2},{2,0},{1,3},{3,1},{4,6},{6,4},{5,7},{7,5},{8,10},{10,8},{9,1... | collective-permute-start | bytes 1572872 | tf_op jit(solution)/shard_map/ppermute | solution.py:352
  382.6 16.9 %collective-permute-start.85 = (bf16[64,2048]{1,0:T(8,128)(2,1)}, bf16[64,2048]{1,0:T(8,128)(2,1)S(1)}, u32[]{:S(2)}, u32[]{:S(2)}) collective-permute-start(bf16[64,2048]{1,0:T(8,128)(2,1)} %add_convert_fusion.17), channel_id=1, source_target_pairs={{0,4},{4,0},{8,12},{12,8},{1,5},{5,1},{9,13},{13,9},{2,6},{6,2},{1... | collective-permute-start | bytes 786440 | tf_op jit(solution)/shard_map/ppermute | solution.py:352
  382.6 16.9 %collective-permute-start.86 = (bf16[64,2048]{1,0:T(8,128)(2,1)}, bf16[64,2048]{1,0:T(8,128)(2,1)}, u32[]{:S(2)}, u32[]{:S(2)}) collective-permute-start(bf16[64,2048]{1,0:T(8,128)(2,1)} %get-tuple-element.1874), channel_id=1, source_target_pairs={{0,2},{2,0},{1,3},{3,1},{4,6},{6,4},{5,7},{7,5},{8,10},{10,8},{9,1... | collective-permute-start | bytes 786440 | tf_op jit(solution)/shard_map/ppermute | solution.py:352
  385.8 40.8 %all-to-all-start.8 = ((bf16[4,256,512]{2,1,0:T(8,128)(2,1)}), bf16[4,256,512]{2,1,0:T(8,128)(2,1)}, u32[]{:S(2)}, u32[]{:S(2)}) async-start(bf16[4,256,512]{2,1,0:T(8,128)(2,1)} %bitcast.160), calls=%async_computation.8 | async-start | bytes 2097152 | tf_op jit(solution)/shard_map/all_to_all | solution.py:912
  397.5 13.2 %collective-permute-start.88 = (bf16[64,2048]{1,0:T(8,128)(2,1)}, bf16[64,2048]{1,0:T(8,128)(2,1)S(1)}, u32[]{:S(2)}, u32[]{:S(2)}) collective-permute-start(bf16[64,2048]{1,0:T(8,128)(2,1)} %get-tuple-element.1782), channel_id=1, source_target_pairs={{0,2},{2,0},{1,3},{3,1},{4,6},{6,4},{5,7},{7,5},{8,10},{10,8},{9,1... | collective-permute-start | bytes 786440 | tf_op jit(solution)/shard_map/ppermute | solution.py:352
  399.0 19.1 %collective-permute-start.89 = (bf16[128,2048]{1,0:T(8,128)(2,1)}, bf16[128,2048]{1,0:T(8,128)(2,1)}, u32[]{:S(2)}, u32[]{:S(2)}) collective-permute-start(bf16[128,2048]{1,0:T(8,128)(2,1)} %add_convert_fusion.4), channel_id=1, source_target_pairs={{0,2},{2,0},{1,3},{3,1},{4,6},{6,4},{5,7},{7,5},{8,10},{10,8},{9,1... | collective-permute-start | bytes 1572872 | tf_op jit(solution)/shard_map/ppermute | solution.py:352
  401.5 17.5 %collective-permute-start.92 = (bf16[64,2048]{1,0:T(8,128)(2,1)}, bf16[64,2048]{1,0:T(8,128)(2,1)}, u32[]{:S(2)}, u32[]{:S(2)}) collective-permute-start(bf16[64,2048]{1,0:T(8,128)(2,1)} %add_convert_fusion.12), channel_id=1, source_target_pairs={{0,4},{4,0},{8,12},{12,8},{1,5},{5,1},{9,13},{13,9},{2,6},{6,2},{1... | collective-permute-start | bytes 786440 | tf_op jit(solution)/shard_map/ppermute | solution.py:352
  405.6 20.9 %collective-permute-start.91 = (bf16[64,2048]{1,0:T(8,128)(2,1)}, bf16[64,2048]{1,0:T(8,128)(2,1)S(1)}, u32[]{:S(2)}, u32[]{:S(2)}) collective-permute-start(bf16[64,2048]{1,0:T(8,128)(2,1)} %get-tuple-element.1867), channel_id=1, source_target_pairs={{0,4},{4,0},{8,12},{12,8},{1,5},{5,1},{9,13},{13,9},{2,6},{6,2},{1... | collective-permute-start | bytes 786440 | tf_op jit(solution)/shard_map/ppermute | solution.py:352
  405.7 20.9 %collective-permute-start.90 = (bf16[64,2048]{1,0:T(8,128)(2,1)}, bf16[64,2048]{1,0:T(8,128)(2,1)S(1)}, u32[]{:S(2)}, u32[]{:S(2)}) collective-permute-start(bf16[64,2048]{1,0:T(8,128)(2,1)} %get-tuple-element.1868), channel_id=1, source_target_pairs={{0,8},{4,12},{8,0},{12,4},{1,9},{5,13},{9,1},{13,5},{2,10},{6,14},... | collective-permute-start | bytes 786440 | tf_op jit(solution)/shard_map/ppermute | solution.py:352
  410.7 27.6 %collective-permute-start.93 = (bf16[64,2048]{1,0:T(8,128)(2,1)}, bf16[64,2048]{1,0:T(8,128)(2,1)S(1)}, u32[]{:S(2)}, u32[]{:S(2)}) collective-permute-start(bf16[64,2048]{1,0:T(8,128)(2,1)} %get-tuple-element.1800), channel_id=1, source_target_pairs={{0,2},{2,0},{1,3},{3,1},{4,6},{6,4},{5,7},{7,5},{8,10},{10,8},{9,1... | collective-permute-start | bytes 786440 | tf_op jit(solution)/shard_map/ppermute | solution.py:352
  418.1 18.8 %collective-permute-start.96 = (bf16[1024,384]{1,0:T(8,128)(2,1)}, bf16[1024,384]{1,0:T(8,128)(2,1)S(1)}, u32[]{:S(2)}, u32[]{:S(2)}) collective-permute-start(bf16[1024,384]{1,0:T(8,128)(2,1)} %get-tuple-element.1805), channel_id=1, source_target_pairs={{0,16},{16,0},{1,17},{17,1},{2,18},{18,2},{3,19},{19,3},{4,20},{20... | collective-permute-start | bytes 2359304 | tf_op jit(solution)/shard_map/ppermute | solution.py:352
  429.8 12.2 %collective-permute-start.95 = (bf16[64,2048]{1,0:T(8,128)(2,1)S(1)}, bf16[64,2048]{1,0:T(8,128)(2,1)S(1)}, u32[]{:S(2)}, u32[]{:S(2)}) collective-permute-start(bf16[64,2048]{1,0:T(8,128)(2,1)S(1)} %get-tuple-element.1865), channel_id=1, source_target_pairs={{0,4},{4,0},{8,12},{12,8},{1,5},{5,1},{9,13},{13,9},{2,6},{6,2},{1... | collective-permute-start | bytes 786440 | tf_op jit(solution)/shard_map/ppermute | solution.py:352
  432.0 13.2 %collective-permute-start.94 = (bf16[64,2048]{1,0:T(8,128)(2,1)S(1)}, bf16[64,2048]{1,0:T(8,128)(2,1)S(1)}, u32[]{:S(2)}, u32[]{:S(2)}) collective-permute-start(bf16[64,2048]{1,0:T(8,128)(2,1)S(1)} %get-tuple-element.1866), channel_id=1, source_target_pairs={{0,8},{4,12},{8,0},{12,4},{1,9},{5,13},{9,1},{13,5},{2,10},{6,14},... | collective-permute-start | bytes 786440 | tf_op jit(solution)/shard_map/ppermute | solution.py:352
  445.3 13.9 %collective-permute-start.98 = (bf16[64,2048]{1,0:T(8,128)(2,1)S(1)}, bf16[64,2048]{1,0:T(8,128)(2,1)S(1)}, u32[]{:S(2)}, u32[]{:S(2)}) collective-permute-start(bf16[64,2048]{1,0:T(8,128)(2,1)S(1)} %maximum_select_fusion.2.refs_0_), channel_id=1, source_target_pairs={{0,1},{1,0},{2,3},{3,2},{4,5},{5,4},{6,7},{7,6},{8,9},{9,8},{10,11... | collective-permute-start | bytes 786440 | tf_op jit(solution)/shard_map/ppermute | solution.py:352
  445.4 13.8 %collective-permute-start.97 = (bf16[64,2048]{1,0:T(8,128)(2,1)S(1)}, bf16[64,2048]{1,0:T(8,128)(2,1)S(1)}, u32[]{:S(2)}, u32[]{:S(2)}) collective-permute-start(bf16[64,2048]{1,0:T(8,128)(2,1)S(1)} %maximum_select_fusion.2.refs_0_), channel_id=1, source_target_pairs={{0,2},{2,0},{1,3},{3,1},{4,6},{6,4},{5,7},{7,5},{8,10},{10,8},{9,1... | collective-permute-start | bytes 786440 | tf_op jit(solution)/shard_map/ppermute | solution.py:352
  449.1 29.7 %all-to-all-start.9 = ((bf16[4,256,512]{2,1,0:T(8,128)(2,1)}), bf16[4,256,512]{2,1,0:T(8,128)(2,1)S(1)}, u32[]{:S(2)}, u32[]{:S(2)}) async-start(bf16[4,256,512]{2,1,0:T(8,128)(2,1)} %bitcast.38), calls=%async_computation.9 | async-start | bytes 2097152 | tf_op jit(solution)/shard_map/all_to_all | solution.py:912
  (141 other events, 1121.7 us)

commit v4 on v3

--- a/solution.py
+++ b/solution.py
@@ -1084,7 +1084,6 @@
     v.step("x1", "x2")
     v.gather_2()
     v.down = spread(v.down)
-    v.step("down")
     pieces = v.gather_3()
     for i, piece in enumerate(pieces):
         setattr(v, "piece%d" % i, piece)
@@ -1155,8 +1154,10 @@
     v.gather_0(v.middle_grad.astype(LOW))
     v.qkv_full = jnp.concatenate([v.qkv_own, v.qkv_o])[:, :depth].reshape(8 * depth, 3 * width)
     del v.qkv_own, v.qkv_o
-    v.step("gate_g", "up_g", "x0")
+    v.step("up_g", "x0")
     v.gather_1()
+    v.down_sum = added(*v.take("down_k", "down_g")).reshape(4, depth, unit)
+    v.gate_sum = added(*v.take("gate_k", "gate_g")).reshape(4, depth, unit)
     v.step("up_g", "x1", "x2")
 
     def fed(index):
@@ -1166,8 +1167,7 @@
         return contract_cols(quarter(v.projected_grad, index), v.qkv_full).astype(LOW)
 
     v.gather_2()
-    v.down = spread(added(*v.take("down_k", "down_g")).reshape(4, depth, unit))
-    v.gate_sum = added(*v.take("gate_k", "gate_g")).reshape(4, depth, unit)
+    v.down = spread(v.take("down_sum")[0])
     v.step("down")
     pieces = v.gather_3()
     for i, piece in enumerate(pieces):
@@ -1258,8 +1258,8 @@
             v.second_gain,
         ]
     )
-    gain_grads = gain_grads + swap(gain_grads, CORE)
-    gain_grads = gain_grads + swap(gain_grads, X)
+    across = lax.ppermute(gain_grads, (X, CORE), [(i, i ^ 3) for i in range(4)])
+    gain_grads = gain_grads + swap(gain_grads, CORE) + swap(gain_grads, X) + across
     return (
         block_output,
         input_grad,

time: 492 us -> 491 us (level)
  transfers between devices with their start and end apart: 115 -> 116, of which waited for: 53 -> 51; matrix products, arithmetic and copies ran while one was open for 19% -> 19% of each run, Pallas kernels for 11% -> 11%
where the time goes in v4:
time: 491 us; the launch traced here: 487 us
  waiting for transfers between devices  190 us (39%)
  starting transfers between devices  125 us (25%)
  Pallas kernels  60.6 us (12%)
  other arithmetic  57.3 us (12%)
  matrix products  29.1 us (6%)
  local copies, waits for them, and re-layouts  21.7 us (4%)
    ppermute x105, waiting for transfers between devices, swap(): return lax.ppermute(value, axis, pairs)  144 us
    ppermute x105, starting transfers between devices, swap(): return lax.ppermute(value, axis, pairs)  74.3 us
    all_to_all x10, starting transfers between devices, spread(): return lax.all_to_all(pieces, CTX, 0, 0, tiled=True)  50.9 us
    all_to_all x10, waiting for transfers between devices, spread(): return lax.all_to_all(pieces, CTX, 0, 0, tiled=True)  45.4 us
    dot_general x16, matrix products, contract_cols(): lax.dot_general(left, right, (((1,), (1,)), ((), ())), preferred_element_...  17.1 us
    pallas_call x1, Pallas kernels, attention(): pl.pallas_call(kernel, grid=(2 * steps,), out_shape=[pltpu.HBM((rows, fea...  12.7 us
    pallas_call x1, Pallas kernels, attention_back(): pl.pallas_call(kernel, grid=(steps,), out_shape=[jax.ShapeDtypeStruct((ro...  12.5 us
    dot_general x4, matrix products, contract_rows(): lax.dot_general(left, right, (((0,), (0,)), ((), ())), preferred_element_...  12.1 us
  transfers between devices with their start and end apart: 116, of which 51 were waited for; matrix products, arithmetic and copies ran while one was open for 19% of the time, Pallas kernels for 11%

profile of v4, /device:TPU:0, one launch (start us, length us, event | category | flops | bytes accessed | tf_op | source)
XLA Modules:
  0.0 486.6 jit_solution(7697672333941452544)
XLA Ops:
  0.7 2.2 shard_map.203
  4.4 4.1 collective-permute-start.1
  10.1 3.5 all-to-all-start
  14.3 7.9 %collective-permute-done.1.refs_1_ = bf16[64,2048]{1,0:T(8,128)(2,1)} collective-permute-done((bf16[64,2048]{1,0:T(8,128)(2,1)S(1)}, bf16[64,2048]{1,0:T(8,128)(2,1)}, u32[]{:S(2)}, u32[]{:S(2)}) %collective-permute-start.1) | collective-permute-done | bytes 262176 | tf_op jit(solution)/shard_map/ppermute | solution.py:352
  23.0 3.7 collective-permute-start.4
  27.8 3.0 fusion.4
  31.8 8.0 %collective-permute-done.2.refs_2_ = bf16[64,2048]{1,0:T(8,128)(2,1)} collective-permute-done((bf16[64,2048]{1,0:T(8,128)(2,1)}, bf16[64,2048]{1,0:T(8,128)(2,1)}, u32[]{:S(2)}, u32[]{:S(2)}) %collective-permute-start.2) | collective-permute-done | bytes 262176 | tf_op jit(solution)/shard_map/ppermute | solution.py:352
  44.9 3.8 all-to-all-start.1
  49.8 3.5 shard_map.204
  53.3 4.6 all-to-all-done.1.own_ref.refs_16_
  61.9 3.7 all-to-all-start.2
  66.3 12.7 %shard_map.205 = (bf16[1024,2048]{1,0:T(8,128)(2,1)}, bf16[1024,128]{1,0:T(8,128)(2,1)}, bf16[1024,128]{1,0:T(8,128)(2,1)}, bf16[1024,128]{1,0:T(8,128)(2,1)}, b...) custom-call(s32[4]{0:T(128)S(1)} %pad_add_fusion.at_ref.refs_0_, ...), custom_call_target="tpu_custom_call" | custom-call | flops 2684354560 | bytes 14155776 | tf_op jit(solution)/shard_map/pallas_call | solution.py:625
  79.0 3.6 shard_map.206
  82.7 11.2 %all-to-all-done.2 = bf16[4,256,512]{2,1,0:T(8,128)(2,1)S(1)} async-done(((bf16[4,256,512]{2,1,0:T(8,128)(2,1)}), bf16[4,256,512]{2,1,0:T(8,128)(2,1)S(1)}, u32[]{:S(2)}, u32[]{:S(2)}) %all-to-all-start.2) | async-done | bytes 1048608 | tf_op jit(solution)/shard_map/all_to_all | solution.py:912
  96.0 3.5 all-to-all-start.3
  105.0 3.8 collective-permute-done.18.refs_5_
  109.9 4.4 collective-permute-done.19
  116.1 9.6 %collective-permute-done.24.refs_3_ = bf16[64,2048]{1,0:T(8,128)(2,1)S(1)} collective-permute-done((bf16[64,2048]{1,0:T(8,128)(2,1)}, bf16[64,2048]{1,0:T(8,128)(2,1)S(1)}, u32[]{:S(2)}, u32[]{:S(2)}) %collective-permute-start.24) | collective-permute-done | bytes 262176 | tf_op jit(solution)/shard_map/ppermute | solution.py:352
  126.4 3.9 collective-permute-done.25
  132.4 2.6 collective-permute-start.28
  136.1 10.3 %collective-permute-done.29 = bf16[64,2048]{1,0:T(8,128)(2,1)S(1)} collective-permute-done((bf16[64,2048]{1,0:T(8,128)(2,1)S(1)}, bf16[64,2048]{1,0:T(8,128)(2,1)S(1)}, u32[]{:S(2)}, u32[]{:S(2)}) %collective-permute-start.29) | collective-permute-done | bytes 262176 | tf_op jit(solution)/shard_map/ppermute | solution.py:352
  151.4 3.9 collective-permute-start.32
  156.0 9.3 %collective-permute-done.33.refs_2_ = bf16[64,2048]{1,0:T(8,128)(2,1)} collective-permute-done((bf16[64,2048]{1,0:T(8,128)(2,1)}, bf16[64,2048]{1,0:T(8,128)(2,1)}, u32[]{:S(2)}, u32[]{:S(2)}) %collective-permute-start.33) | collective-permute-done | bytes 262176 | tf_op jit(solution)/shard_map/ppermute | solution.py:352
  167.7 5.0 %shard_map.207.cot_ref = bf16[1024,2048]{1,0:T(8,128)(2,1)} custom-call(s32[4]{0:T(128)} %copy-done.4, bf16[64,2048]{1,0:T(8,128)(2,1)} %copy-done.45, bf16[64,2048]{1,0:T(8,128)(2,1)} %collective-permute-done.14.refs_2_, bf16[64,2048]{1,0:T(8,128)(2,1)} %copy-done.50, bf16[64,2048]{1,0:T(8,128)(2,1)} %copy-done.46, ...), custom_call_target="tpu_custom_call" | custom-call | bytes 8388608 | tf_op jit(solution)/shard_map/pallas_call | solution.py:393
  173.1 16.4 %all-to-all-start.4 = ((bf16[4,256,256]{2,1,0:T(8,128)(2,1)}), bf16[4,256,256]{2,1,0:T(8,128)(2,1)}, u32[]{:S(2)}, u32[]{:S(2)}) async-start(bf16[4,256,256]{2,1,0:T(8,128)(2,1)} %get-tuple-element.1196), calls=%async_computation.4 | async-start | bytes 1048576 | tf_op jit(solution)/shard_map/all_to_all | solution.py:912
  192.0 6.6 %collective-permute-done.43.refs_7_ = bf16[64,2048]{1,0:T(8,128)(2,1)S(1)} collective-permute-done((bf16[64,2048]{1,0:T(8,128)(2,1)}, bf16[64,2048]{1,0:T(8,128)(2,1)S(1)}, u32[]{:S(2)}, u32[]{:S(2)}) %collective-permute-start.43) | collective-permute-done | bytes 262176 | tf_op jit(solution)/shard_map/ppermute | solution.py:352
  201.0 2.6 all-to-all-done.4
  203.6 4.2 all-to-all-start.5
  208.3 9.3 %shard_map.208 = (bf16[1024,2048]{1,0:T(8,128)(2,1)}, bf16[1024,512]{1,0:T(8,128)(2,1)S(1)}, bf16[1024,512]{1,0:T(8,128)(2,1)}, bf16[1024,512]{1,0:T(8,128)(2,1)}) custom-call(bf16[64,2048]{1,0:T(8,128)(2,1)} %multiply_convert_fusion.refs_0_, bf16[64,2048]{1,0:T(8,128)(2,1)} %collective-permute-done.32.refs_1_, ...), custom_call_target="tpu_custom_call" | custom-call | flops 4294967296 | bytes 17825792 | tf_op jit(solution)/shard_map/pallas_call | solution.py:471
  218.5 3.1 all-to-all-done.5
  222.2 4.9 convolution_convert_fusion.2
  227.1 2.7 pad_maximum_fusion
  229.8 2.7 pad_maximum_fusion.1
  235.6 6.9 %shard_map.209 = (bf16[1024,512]{1,0:T(8,128)(2,1)}, bf16[1024,512]{1,0:T(8,128)(2,1)}) custom-call(bf16[1024,2048]{1,0:T(8,128)(2,1)} %shard_map.207.cot_ref, bf16[1024,256]{1,0:T(8,128)(2,1)} %bitcast.24.refs_0_, bf16[1024,256]{1,0:T(8,128)(2,1)} %bitcast.25.refs_1_, bf16[1024,256]{1,0:T(8,128)(2,1)} %bitcast.26.refs_2_, bf16[1024,256]{1,0:T(8,128)(2,1)} %bitcast.164, ...), custom_call_target="tpu_custom_call" | custom-call | flops 2147483648 | bytes 12582912 | tf_op jit(solution)/shard_map/pallas_call | solution.py:510
  254.7 2.4 convolution_convert_fusion.1
  259.7 2.4 convolution_convert_fusion
  263.7 6.5 %collective-permute-done.56 = bf16[128,2048]{1,0:T(8,128)(2,1)S(1)} collective-permute-done((bf16[128,2048]{1,0:T(8,128)(2,1)S(1)}, bf16[128,2048]{1,0:T(8,128)(2,1)S(1)}, u32[]{:S(2)}, u32[]{:S(2)}) %collective-permute-start.56) | collective-permute-done | bytes 524320 | tf_op jit(solution)/shard_map/ppermute | solution.py:352
  273.2 2.9 maximum_maximum_fusion
  276.1 5.1 %collective-permute-done.61 = bf16[64,2048]{1,0:T(8,128)(2,1)S(1)} collective-permute-done((bf16[64,2048]{1,0:T(8,128)(2,1)S(1)}, bf16[64,2048]{1,0:T(8,128)(2,1)S(1)}, u32[]{:S(2)}, u32[]{:S(2)}) %collective-permute-start.61) | collective-permute-done | bytes 262176 | tf_op jit(solution)/shard_map/ppermute | solution.py:352
  281.2 2.6 collective-permute-done.60
  289.9 10.5 %collective-permute-done.64.refs_2_ = bf16[64,2048]{1,0:T(8,128)(2,1)S(1)} collective-permute-done((bf16[64,2048]{1,0:T(8,128)(2,1)S(1)}, bf16[64,2048]{1,0:T(8,128)(2,1)S(1)}, u32[]{:S(2)}, u32[]{:S(2)}) %collective-permute-start.64) | collective-permute-done | bytes 262176 | tf_op jit(solution)/shard_map/ppermute | solution.py:352
  304.0 5.1 %collective-permute-done.67.refs_3_ = bf16[64,2048]{1,0:T(8,128)(2,1)S(1)} collective-permute-done((bf16[64,2048]{1,0:T(8,128)(2,1)S(1)}, bf16[64,2048]{1,0:T(8,128)(2,1)S(1)}, u32[]{:S(2)}, u32[]{:S(2)}) %collective-permute-start.67) | collective-permute-done | bytes 262176 | tf_op jit(solution)/shard_map/ppermute | solution.py:352
  309.8 3.7 all-to-all-start.6
  317.4 5.3 %collective-permute-done.69.refs_5_ = bf16[64,2048]{1,0:T(8,128)(2,1)S(1)} collective-permute-done((bf16[64,2048]{1,0:T(8,128)(2,1)S(1)}, bf16[64,2048]{1,0:T(8,128)(2,1)S(1)}, u32[]{:S(2)}, u32[]{:S(2)}) %collective-permute-start.69) | collective-permute-done | bytes 262176 | tf_op jit(solution)/shard_map/ppermute | solution.py:352
  322.8 3.5 collective-permute-done.70.refs_6_
  326.9 6.0 %collective-permute-done.71.refs_7_ = bf16[64,2048]{1,0:T(8,128)(2,1)S(1)} collective-permute-done((bf16[64,2048]{1,0:T(8,128)(2,1)}, bf16[64,2048]{1,0:T(8,128)(2,1)S(1)}, u32[]{:S(2)}, u32[]{:S(2)}) %collective-permute-start.71) | collective-permute-done | bytes 262176 | tf_op jit(solution)/shard_map/ppermute | solution.py:352
  335.3 3.3 all-to-all-done.6
  339.5 4.3 all-to-all-start.7
  343.8 12.5 %shard_map.210 = (bf16[1024,384]{1,0:T(8,128)(2,1)S(1)}, bf16[1024,128]{1,0:T(8,128)(2,1)S(1)}, bf16[1024,128]{1,0:T(8,128)(2,1)S(1)}) custom-call(bf16[64,2048]{1,0:T(8,128)(2,1)} %copy-done.52, bf16[64,2048]{1,0:T(8,128)(2,1)} %copy-done.72, bf16[64,2048]{1,0:T(8,128)(2,1)} %copy-done.70, bf16[64,2048]{1,0:T(8,128)(2,1)} %copy-done.75, ...), custom_call_target="tpu_custom_call" | custom-call | flops 3758096384 | bytes 7340032 | tf_op jit(solution)/shard_map/pallas_call | solution.py:761
  359.9 9.2 %all-to-all-done.7 = bf16[4,256,512]{2,1,0:T(8,128)(2,1)} async-done(((bf16[4,256,512]{2,1,0:T(8,128)(2,1)}), bf16[4,256,512]{2,1,0:T(8,128)(2,1)}, u32[]{:S(2)}, u32[]{:S(2)}) %all-to-all-start.7) | async-done | bytes 1048608 | tf_op jit(solution)/shard_map/all_to_all | solution.py:912
  382.9 2.5 add_convert_fusion
  385.4 4.4 all-to-all-start.8
  389.9 2.5 convolution_convert_fusion.5
  393.3 2.4 convolution_convert_fusion.3
  405.3 2.9 collective-permute-start.90
  411.8 6.0 %collective-permute-done.89 = bf16[128,2048]{1,0:T(8,128)(2,1)} collective-permute-done((bf16[128,2048]{1,0:T(8,128)(2,1)}, bf16[128,2048]{1,0:T(8,128)(2,1)}, u32[]{:S(2)}, u32[]{:S(2)}) %collective-permute-start.89) | collective-permute-done | bytes 524320 | tf_op jit(solution)/shard_map/ppermute | solution.py:352
  418.6 7.6 %collective-permute-done.91 = bf16[64,2048]{1,0:T(8,128)(2,1)S(1)} collective-permute-done((bf16[64,2048]{1,0:T(8,128)(2,1)}, bf16[64,2048]{1,0:T(8,128)(2,1)S(1)}, u32[]{:S(2)}, u32[]{:S(2)}) %collective-permute-start.91) | collective-permute-done | bytes 262176 | tf_op jit(solution)/shard_map/ppermute | solution.py:352
  429.5 2.2 collective-permute-start.95
  437.9 4.0 collective-permute-done.95
  441.8 3.0 collective-permute-done.94
  448.7 3.5 all-to-all-start.9
  462.0 2.2 shard_map.212
  464.3 2.7 shard_map.211
  467.0 11.5 %all-to-all-done.9 = bf16[4,256,512]{2,1,0:T(8,128)(2,1)S(1)} async-done(((bf16[4,256,512]{2,1,0:T(8,128)(2,1)}), bf16[4,256,512]{2,1,0:T(8,128)(2,1)S(1)}, u32[]{:S(2)}, u32[]{:S(2)}) %all-to-all-start.9) | async-done | bytes 1048608 | tf_op jit(solution)/shard_map/all_to_all | solution.py:912
  (473 shorter events, 150.5 us)
Async XLA Ops:
  4.4 17.9 %collective-permute-start.1 = (bf16[64,2048]{1,0:T(8,128)(2,1)S(1)}, bf16[64,2048]{1,0:T(8,128)(2,1)}, u32[]{:S(2)}, u32[]{:S(2)}) collective-permute-start(bf16[64,2048]{1,0:T(8,128)(2,1)S(1)} %constant_dynamic-slice_fusion.1), channel_id=1, source_target_pairs={{0,8},{4,12},{8,0},{12,4},{1,9},{5,13},{9,1},{13,5},{2,10},{6,14},... | collective-permute-start | bytes 786440 | tf_op jit(solution)/shard_map/ppermute | solution.py:352
  8.5 14.5 %collective-permute-start = (bf16[64,2048]{1,0:T(8,128)(2,1)S(1)}, bf16[64,2048]{1,0:T(8,128)(2,1)}, u32[]{:S(2)}, u32[]{:S(2)}) collective-permute-start(bf16[64,2048]{1,0:T(8,128)(2,1)S(1)} %constant_dynamic-slice_fusion.1), channel_id=1, source_target_pairs={{0,4},{4,0},{8,12},{12,8},{1,5},{5,1},{9,13},{13,9},{2,6},{6,2},{1... | collective-permute-start | bytes 786440 | tf_op jit(solution)/shard_map/ppermute | solution.py:352
  10.1 33.2 %all-to-all-start = ((bf16[4,272,384]{2,1,0:T(8,128)(2,1)}), bf16[4,272,384]{2,1,0:T(8,128)(2,1)S(1)}, u32[]{:S(2)}, u32[]{:S(2)}) async-start(bf16[4,272,384]{2,1,0:T(8,128)(2,1)} %shard_map.203), calls=%async_computation | async-start | bytes 1671168 | tf_op jit(solution)/shard_map/all_to_all | solution.py:912
  23.0 20.3 %collective-permute-start.4 = (bf16[64,2048]{1,0:T(8,128)(2,1)}, bf16[64,2048]{1,0:T(8,128)(2,1)}, u32[]{:S(2)}, u32[]{:S(2)}) collective-permute-start(bf16[64,2048]{1,0:T(8,128)(2,1)} %collective-permute-done.1.refs_1_), channel_id=1, source_target_pairs={{0,2},{2,0},{1,3},{3,1},{4,6},{6,4},{5,7},{7,5},{8,10},{10,8},{9,1... | collective-permute-start | bytes 786440 | tf_op jit(solution)/shard_map/ppermute | solution.py:352
  26.7 13.1 %collective-permute-start.2 = (bf16[64,2048]{1,0:T(8,128)(2,1)}, bf16[64,2048]{1,0:T(8,128)(2,1)}, u32[]{:S(2)}, u32[]{:S(2)}) collective-permute-start(bf16[64,2048]{1,0:T(8,128)(2,1)} %collective-permute-done.1.refs_1_), channel_id=1, source_target_pairs={{0,4},{4,0},{8,12},{12,8},{1,5},{5,1},{9,13},{13,9},{2,6},{6,2},{1... | collective-permute-start | bytes 786440 | tf_op jit(solution)/shard_map/ppermute | solution.py:352
  26.9 16.3 %collective-permute-start.3 = (bf16[64,2048]{1,0:T(8,128)(2,1)}, bf16[64,2048]{1,0:T(8,128)(2,1)}, u32[]{:S(2)}, u32[]{:S(2)}) collective-permute-start(bf16[64,2048]{1,0:T(8,128)(2,1)} %collective-permute-done.refs_0_), channel_id=1, source_target_pairs={{0,2},{2,0},{1,3},{3,1},{4,6},{6,4},{5,7},{7,5},{8,10},{10,8},{9,1... | collective-permute-start | bytes 786440 | tf_op jit(solution)/shard_map/ppermute | solution.py:352
  43.3 22.3 %collective-permute-start.11 = (bf16[4,272,384]{2,1,0:T(8,128)(2,1)S(1)}, bf16[4,272,384]{2,1,0:T(8,128)(2,1)S(1)}, u32[]{:S(2)}, u32[]{:S(2)}) collective-permute-start(bf16[4,272,384]{2,1,0:T(8,128)(2,1)S(1)} %all-to-all-done.refs_13_), channel_id=1, source_target_pairs={{0,16},{16,0},{1,17},{17,1},{2,18},{18,2},{3,19},{19,3},{4,20},{20... | collective-permute-start | bytes 2506760 | tf_op jit(solution)/shard_map/ppermute | solution.py:352
  44.9 13.0 %all-to-all-start.1 = ((bf16[4,128,256]{2,1,0:T(8,128)(2,1)}), bf16[4,128,256]{2,1,0:T(8,128)(2,1)S(1)}, u32[]{:S(2)}, u32[]{:S(2)}) async-start(bf16[4,128,256]{2,1,0:T(8,128)(2,1)} %bitcast), calls=%async_computation.1 | async-start | bytes 524288 | tf_op jit(solution)/shard_map/all_to_all | solution.py:912
  58.6 20.4 %collective-permute-start.14 = (bf16[64,2048]{1,0:T(8,128)(2,1)S(1)}, bf16[64,2048]{1,0:T(8,128)(2,1)}, u32[]{:S(2)}, u32[]{:S(2)}) collective-permute-start(bf16[64,2048]{1,0:T(8,128)(2,1)S(1)} %constant_dynamic-slice_fusion), channel_id=1, source_target_pairs={{0,8},{4,12},{8,0},{12,4},{1,9},{5,13},{9,1},{13,5},{2,10},{6,14},... | collective-permute-start | bytes 786440 | tf_op jit(solution)/shard_map/ppermute | solution.py:352
  58.6 20.4 %collective-permute-start.13 = (bf16[64,2048]{1,0:T(8,128)(2,1)S(1)}, bf16[64,2048]{1,0:T(8,128)(2,1)S(1)}, u32[]{:S(2)}, u32[]{:S(2)}) collective-permute-start(bf16[64,2048]{1,0:T(8,128)(2,1)S(1)} %constant_dynamic-slice_fusion), channel_id=1, source_target_pairs={{0,4},{4,0},{8,12},{12,8},{1,5},{5,1},{9,13},{13,9},{2,6},{6,2},{1... | collective-permute-start | bytes 786440 | tf_op jit(solution)/shard_map/ppermute | solution.py:352
  61.9 32.0 %all-to-all-start.2 = ((bf16[4,256,512]{2,1,0:T(8,128)(2,1)}), bf16[4,256,512]{2,1,0:T(8,128)(2,1)S(1)}, u32[]{:S(2)}, u32[]{:S(2)}) async-start(bf16[4,256,512]{2,1,0:T(8,128)(2,1)} %pad_maximum_fusion.4), calls=%async_computation.2 | async-start | bytes 2097152 | tf_op jit(solution)/shard_map/all_to_all | solution.py:912
  65.7 13.4 %collective-permute-start.15 = (bf16[4,128,256]{2,1,0:T(8,128)(2,1)}, bf16[4,128,256]{2,1,0:T(8,128)(2,1)}, u32[]{:S(2)}, u32[]{:S(2)}) collective-permute-start(bf16[4,128,256]{2,1,0:T(8,128)(2,1)} %copy-done.61), channel_id=1, source_target_pairs={{0,16},{16,0},{1,17},{17,1},{2,18},{18,2},{3,19},{19,3},{4,20},{20... | collective-permute-start | bytes 786440 | tf_op jit(solution)/shard_map/ppermute | solution.py:352
  93.9 20.4 %collective-permute-start.20 = (bf16[256,2048]{1,0:T(8,128)(2,1)}, bf16[256,2048]{1,0:T(8,128)(2,1)}, u32[]{:S(2)}, u32[]{:S(2)}) collective-permute-start(bf16[256,2048]{1,0:T(8,128)(2,1)} %get-tuple-element.1043), channel_id=1, source_target_pairs={{0,1},{1,0},{2,3},{3,2},{4,5},{5,4},{6,7},{7,6},{8,9},{9,8},{10,11... | collective-permute-start | bytes 3145736 | tf_op jit(solution)/shard_map/ppermute | solution.py:352
  94.5 14.3 %collective-permute-start.18 = (bf16[64,2048]{1,0:T(8,128)(2,1)}, bf16[64,2048]{1,0:T(8,128)(2,1)}, u32[]{:S(2)}, u32[]{:S(2)}) collective-permute-start(bf16[64,2048]{1,0:T(8,128)(2,1)} %collective-permute-done.14.refs_2_), channel_id=1, source_target_pairs={{0,2},{2,0},{1,3},{3,1},{4,6},{6,4},{5,7},{7,5},{8,10},{10,8},{9,1... | collective-permute-start | bytes 786440 | tf_op jit(solution)/shard_map/ppermute | solution.py:352
  96.0 34.4 %all-to-all-start.3 = ((bf16[4,256,512]{2,1,0:T(8,128)(2,1)}), bf16[4,256,512]{2,1,0:T(8,128)(2,1)S(1)}, u32[]{:S(2)}, u32[]{:S(2)}) async-start(bf16[4,256,512]{2,1,0:T(8,128)(2,1)} %pad_maximum_fusion.3), calls=%async_computation.3 | async-start | bytes 2097152 | tf_op jit(solution)/shard_map/all_to_all | solution.py:912
  108.8 16.9 %collective-permute-start.24 = (bf16[64,2048]{1,0:T(8,128)(2,1)}, bf16[64,2048]{1,0:T(8,128)(2,1)S(1)}, u32[]{:S(2)}, u32[]{:S(2)}) collective-permute-start(bf16[64,2048]{1,0:T(8,128)(2,1)} %collective-permute-done.14.refs_2_), channel_id=1, source_target_pairs={{0,4},{4,0},{8,12},{12,8},{1,5},{5,1},{9,13},{13,9},{2,6},{6,2},{1... | collective-permute-start | bytes 786440 | tf_op jit(solution)/shard_map/ppermute | solution.py:352
  108.8 16.9 %collective-permute-start.23 = (bf16[128,2048]{1,0:T(8,128)(2,1)S(1)}, bf16[128,2048]{1,0:T(8,128)(2,1)S(1)}, u32[]{:S(2)}, u32[]{:S(2)}) collective-permute-start(bf16[128,2048]{1,0:T(8,128)(2,1)S(1)} %add_convert_fusion.7), channel_id=1, source_target_pairs={{0,2},{2,0},{1,3},{3,1},{4,6},{6,4},{5,7},{7,5},{8,10},{10,8},{9,1... | collective-permute-start | bytes 1572872 | tf_op jit(solution)/shard_map/ppermute | solution.py:352
  109.4 25.6 %collective-permute-start.26 = (bf16[4,256,512]{2,1,0:T(8,128)(2,1)S(1)}, bf16[4,256,512]{2,1,0:T(8,128)(2,1)}, u32[]{:S(2)}, u32[]{:S(2)}) collective-permute-start(bf16[4,256,512]{2,1,0:T(8,128)(2,1)S(1)} %all-to-all-done.2), channel_id=1, source_target_pairs={{0,16},{16,0},{1,17},{17,1},{2,18},{18,2},{3,19},{19,3},{4,20},{20... | collective-permute-start | bytes 3145736 | tf_op jit(solution)/shard_map/ppermute | solution.py:352
  115.4 14.9 %collective-permute-start.25 = (bf16[64,2048]{1,0:T(8,128)(2,1)S(1)}, bf16[64,2048]{1,0:T(8,128)(2,1)}, u32[]{:S(2)}, u32[]{:S(2)}) collective-permute-start(bf16[64,2048]{1,0:T(8,128)(2,1)S(1)} %add_convert_fusion.27), channel_id=1, source_target_pairs={{0,4},{4,0},{8,12},{12,8},{1,5},{5,1},{9,13},{13,9},{2,6},{6,2},{1... | collective-permute-start | bytes 786440 | tf_op jit(solution)/shard_map/ppermute | solution.py:352
  115.5 20.1 %collective-permute-start.27 = (bf16[64,2048]{1,0:T(8,128)(2,1)}, bf16[64,2048]{1,0:T(8,128)(2,1)}, u32[]{:S(2)}, u32[]{:S(2)}) collective-permute-start(bf16[64,2048]{1,0:T(8,128)(2,1)} %get-tuple-element.1109), channel_id=1, source_target_pairs={{0,2},{2,0},{1,3},{3,1},{4,6},{6,4},{5,7},{7,5},{8,10},{10,8},{9,1... | collective-permute-start | bytes 786440 | tf_op jit(solution)/shard_map/ppermute | solution.py:352
  132.0 14.3 %collective-permute-start.29 = (bf16[64,2048]{1,0:T(8,128)(2,1)S(1)}, bf16[64,2048]{1,0:T(8,128)(2,1)S(1)}, u32[]{:S(2)}, u32[]{:S(2)}) collective-permute-start(bf16[64,2048]{1,0:T(8,128)(2,1)S(1)} %get-tuple-element.1789), channel_id=1, source_target_pairs={{0,4},{4,0},{8,12},{12,8},{1,5},{5,1},{9,13},{13,9},{2,6},{6,2},{1... | collective-permute-start | bytes 786440 | tf_op jit(solution)/shard_map/ppermute | solution.py:352
  132.4 13.9 %collective-permute-start.28 = (bf16[64,2048]{1,0:T(8,128)(2,1)S(1)}, bf16[64,2048]{1,0:T(8,128)(2,1)S(1)}, u32[]{:S(2)}, u32[]{:S(2)}) collective-permute-start(bf16[64,2048]{1,0:T(8,128)(2,1)S(1)} %get-tuple-element.1790), channel_id=1, source_target_pairs={{0,8},{4,12},{8,0},{12,4},{1,9},{5,13},{9,1},{13,5},{2,10},{6,14},... | collective-permute-start | bytes 786440 | tf_op jit(solution)/shard_map/ppermute | solution.py:352
  135.0 13.4 %collective-permute-start.31 = (bf16[64,2048]{1,0:T(8,128)(2,1)S(1)}, bf16[64,2048]{1,0:T(8,128)(2,1)S(1)}, u32[]{:S(2)}, u32[]{:S(2)}) collective-permute-start(bf16[64,2048]{1,0:T(8,128)(2,1)S(1)} %copy-done.51), channel_id=1, source_target_pairs={{0,2},{2,0},{1,3},{3,1},{4,6},{6,4},{5,7},{7,5},{8,10},{10,8},{9,1... | collective-permute-start | bytes 786440 | tf_op jit(solution)/shard_map/ppermute | solution.py:352
  135.6 37.5 %collective-permute-start.38 = (bf16[4,256,512]{2,1,0:T(8,128)(2,1)S(1)}, bf16[4,256,512]{2,1,0:T(8,128)(2,1)}, u32[]{:S(2)}, u32[]{:S(2)}) collective-permute-start(bf16[4,256,512]{2,1,0:T(8,128)(2,1)S(1)} %all-to-all-done.3), channel_id=1, source_target_pairs={{0,16},{16,0},{1,17},{17,1},{2,18},{18,2},{3,19},{19,3},{4,20},{20... | collective-permute-start | bytes 3145736 | tf_op jit(solution)/shard_map/ppermute | solution.py:352
  150.1 15.3 %collective-permute-start.33 = (bf16[64,2048]{1,0:T(8,128)(2,1)}, bf16[64,2048]{1,0:T(8,128)(2,1)}, u32[]{:S(2)}, u32[]{:S(2)}) collective-permute-start(bf16[64,2048]{1,0:T(8,128)(2,1)} %multiply_convert_fusion.refs_0_), channel_id=1, source_target_pairs={{0,8},{4,12},{8,0},{12,4},{1,9},{5,13},{9,1},{13,5},{2,10},{6,14},... | collective-permute-start | bytes 786440 | tf_op jit(solution)/shard_map/ppermute | solution.py:352
  151.4 14.1 %collective-permute-start.32 = (bf16[64,2048]{1,0:T(8,128)(2,1)}, bf16[64,2048]{1,0:T(8,128)(2,1)}, u32[]{:S(2)}, u32[]{:S(2)}) collective-permute-start(bf16[64,2048]{1,0:T(8,128)(2,1)} %multiply_convert_fusion.refs_0_), channel_id=1, source_target_pairs={{0,4},{4,0},{8,12},{12,8},{1,5},{5,1},{9,13},{13,9},{2,6},{6,2},{1... | collective-permute-start | bytes 786440 | tf_op jit(solution)/shard_map/ppermute | solution.py:352
  155.3 17.4 %collective-permute-start.39 = (bf16[64,2048]{1,0:T(8,128)(2,1)}, bf16[64,2048]{1,0:T(8,128)(2,1)}, u32[]{:S(2)}, u32[]{:S(2)}) collective-permute-start(bf16[64,2048]{1,0:T(8,128)(2,1)} %multiply_convert_fusion.refs_0_), channel_id=1, source_target_pairs={{0,2},{2,0},{1,3},{3,1},{4,6},{6,4},{5,7},{7,5},{8,10},{10,8},{9,1... | collective-permute-start | bytes 786440 | tf_op jit(solution)/shard_map/ppermute | solution.py:352
  165.7 23.9 %collective-permute-start.42 = (bf16[64,2048]{1,0:T(8,128)(2,1)}, bf16[64,2048]{1,0:T(8,128)(2,1)}, u32[]{:S(2)}, u32[]{:S(2)}) collective-permute-start(bf16[64,2048]{1,0:T(8,128)(2,1)} %collective-permute-done.33.refs_2_), channel_id=1, source_target_pairs={{0,2},{2,0},{1,3},{3,1},{4,6},{6,4},{5,7},{7,5},{8,10},{10,8},{9,1... | collective-permute-start | bytes 786440 | tf_op jit(solution)/shard_map/ppermute | solution.py:352
  166.3 23.2 %collective-permute-start.41 = (bf16[64,2048]{1,0:T(8,128)(2,1)}, bf16[64,2048]{1,0:T(8,128)(2,1)}, u32[]{:S(2)}, u32[]{:S(2)}) collective-permute-start(bf16[64,2048]{1,0:T(8,128)(2,1)} %collective-permute-done.32.refs_1_), channel_id=1, source_target_pairs={{0,2},{2,0},{1,3},{3,1},{4,6},{6,4},{5,7},{7,5},{8,10},{10,8},{9,1... | collective-permute-start | bytes 786440 | tf_op jit(solution)/shard_map/ppermute | solution.py:352
  173.1 30.4 %all-to-all-start.4 = ((bf16[4,256,256]{2,1,0:T(8,128)(2,1)}), bf16[4,256,256]{2,1,0:T(8,128)(2,1)}, u32[]{:S(2)}, u32[]{:S(2)}) async-start(bf16[4,256,256]{2,1,0:T(8,128)(2,1)} %get-tuple-element.1196), calls=%async_computation.4 | async-start | bytes 1048576 | tf_op jit(solution)/shard_map/all_to_all | solution.py:912
  203.6 18.1 %all-to-all-start.5 = ((bf16[4,256,256]{2,1,0:T(8,128)(2,1)}), bf16[4,256,256]{2,1,0:T(8,128)(2,1)}, u32[]{:S(2)}, u32[]{:S(2)}) async-start(bf16[4,256,256]{2,1,0:T(8,128)(2,1)} %get-tuple-element.1237), calls=%async_computation.5 | async-start | bytes 1048576 | tf_op jit(solution)/shard_map/all_to_all | solution.py:912
  207.7 26.2 %collective-permute-start.51 = (bf16[4,256,256]{2,1,0:T(8,128)(2,1)}, bf16[4,256,256]{2,1,0:T(8,128)(2,1)}, u32[]{:S(2)}, u32[]{:S(2)}) collective-permute-start(bf16[4,256,256]{2,1,0:T(8,128)(2,1)} %all-to-all-done.4), channel_id=1, source_target_pairs={{0,16},{16,0},{1,17},{17,1},{2,18},{18,2},{3,19},{19,3},{4,20},{20... | collective-permute-start | bytes 1572872 | tf_op jit(solution)/shard_map/ppermute | solution.py:352
  221.7 13.1 %collective-permute-start.52 = (bf16[4,256,256]{2,1,0:T(8,128)(2,1)}, bf16[4,256,256]{2,1,0:T(8,128)(2,1)S(1)}, u32[]{:S(2)}, u32[]{:S(2)}) collective-permute-start(bf16[4,256,256]{2,1,0:T(8,128)(2,1)} %all-to-all-done.5), channel_id=1, source_target_pairs={{0,16},{16,0},{1,17},{17,1},{2,18},{18,2},{3,19},{19,3},{4,20},{20... | collective-permute-start | bytes 1572872 | tf_op jit(solution)/shard_map/ppermute | solution.py:352
  245.7 30.4 %collective-permute-start.58 = (bf16[1024,512]{1,0:T(8,128)(2,1)S(1)}, bf16[1024,512]{1,0:T(8,128)(2,1)S(1)}, u32[]{:S(2)}, u32[]{:S(2)}) collective-permute-start(bf16[1024,512]{1,0:T(8,128)(2,1)S(1)} %copy-done.40), channel_id=1, source_target_pairs={{0,16},{16,0},{1,17},{17,1},{2,18},{18,2},{3,19},{19,3},{4,20},{20... | collective-permute-start | bytes 3145736 | tf_op jit(solution)/shard_map/ppermute | solution.py:352
  250.3 19.8 %collective-permute-start.56 = (bf16[128,2048]{1,0:T(8,128)(2,1)S(1)}, bf16[128,2048]{1,0:T(8,128)(2,1)S(1)}, u32[]{:S(2)}, u32[]{:S(2)}) collective-permute-start(bf16[128,2048]{1,0:T(8,128)(2,1)S(1)} %add_convert_fusion.6), channel_id=1, source_target_pairs={{0,2},{2,0},{1,3},{3,1},{4,6},{6,4},{5,7},{7,5},{8,10},{10,8},{9,1... | collective-permute-start | bytes 1572872 | tf_op jit(solution)/shard_map/ppermute | solution.py:352
  259.1 17.0 %collective-permute-start.59 = (bf16[64,2048]{1,0:T(8,128)(2,1)S(1)}, bf16[64,2048]{1,0:T(8,128)(2,1)S(1)}, u32[]{:S(2)}, u32[]{:S(2)}) collective-permute-start(bf16[64,2048]{1,0:T(8,128)(2,1)S(1)} %get-tuple-element.1466), channel_id=1, source_target_pairs={{0,2},{2,0},{1,3},{3,1},{4,6},{6,4},{5,7},{7,5},{8,10},{10,8},{9,1... | collective-permute-start | bytes 786440 | tf_op jit(solution)/shard_map/ppermute | solution.py:352
  270.5 13.3 %collective-permute-start.60 = (bf16[64,2048]{1,0:T(8,128)(2,1)S(1)}, bf16[64,2048]{1,0:T(8,128)(2,1)S(1)}, u32[]{:S(2)}, u32[]{:S(2)}) collective-permute-start(bf16[64,2048]{1,0:T(8,128)(2,1)S(1)} %get-tuple-element.1788), channel_id=1, source_target_pairs={{0,8},{4,12},{8,0},{12,4},{1,9},{5,13},{9,1},{13,5},{2,10},{6,14},... | collective-permute-start | bytes 786440 | tf_op jit(solution)/shard_map/ppermute | solution.py:352
  272.5 28.1 %collective-permute-start.62 = (bf16[1024,512]{1,0:T(8,128)(2,1)S(1)}, bf16[1024,512]{1,0:T(8,128)(2,1)S(1)}, u32[]{:S(2)}, u32[]{:S(2)}) collective-permute-start(bf16[1024,512]{1,0:T(8,128)(2,1)S(1)} %get-tuple-element.1494), channel_id=1, source_target_pairs={{0,16},{16,0},{1,17},{17,1},{2,18},{18,2},{3,19},{19,3},{4,20},{20... | collective-permute-start | bytes 3145736 | tf_op jit(solution)/shard_map/ppermute | solution.py:352
  286.3 14.1 %collective-permute-start.64 = (bf16[64,2048]{1,0:T(8,128)(2,1)S(1)}, bf16[64,2048]{1,0:T(8,128)(2,1)S(1)}, u32[]{:S(2)}, u32[]{:S(2)}) collective-permute-start(bf16[64,2048]{1,0:T(8,128)(2,1)S(1)} %get-tuple-element.1613.refs_0_), channel_id=1, source_target_pairs={{0,8},{4,12},{8,0},{12,4},{1,9},{5,13},{9,1},{13,5},{2,10},{6,14},... | collective-permute-start | bytes 786440 | tf_op jit(solution)/shard_map/ppermute | solution.py:352
  286.6 14.0 %collective-permute-start.63 = (bf16[64,2048]{1,0:T(8,128)(2,1)S(1)}, bf16[64,2048]{1,0:T(8,128)(2,1)S(1)}, u32[]{:S(2)}, u32[]{:S(2)}) collective-permute-start(bf16[64,2048]{1,0:T(8,128)(2,1)S(1)} %get-tuple-element.1613.refs_0_), channel_id=1, source_target_pairs={{0,4},{4,0},{8,12},{12,8},{1,5},{5,1},{9,13},{13,9},{2,6},{6,2},{1... | collective-permute-start | bytes 786440 | tf_op jit(solution)/shard_map/ppermute | solution.py:352
  288.3 29.1 %collective-permute-start.68 = (bf16[1024,512]{1,0:T(8,128)(2,1)}, bf16[1024,512]{1,0:T(8,128)(2,1)}, u32[]{:S(2)}, u32[]{:S(2)}) collective-permute-start(bf16[1024,512]{1,0:T(8,128)(2,1)} %get-tuple-element.1554), channel_id=1, source_target_pairs={{0,16},{16,0},{1,17},{17,1},{2,18},{18,2},{3,19},{19,3},{4,20},{20... | collective-permute-start | bytes 3145736 | tf_op jit(solution)/shard_map/ppermute | solution.py:352
  289.3 14.7 %collective-permute-start.66 = (bf16[64,2048]{1,0:T(8,128)(2,1)S(1)}, bf16[64,2048]{1,0:T(8,128)(2,1)S(1)}, u32[]{:S(2)}, u32[]{:S(2)}) collective-permute-start(bf16[64,2048]{1,0:T(8,128)(2,1)S(1)} %get-tuple-element.1613.refs_0_), channel_id=1, source_target_pairs={{0,2},{2,0},{1,3},{3,1},{4,6},{6,4},{5,7},{7,5},{8,10},{10,8},{9,1... | collective-permute-start | bytes 786440 | tf_op jit(solution)/shard_map/ppermute | solution.py:352
  309.8 28.7 %all-to-all-start.6 = ((bf16[4,256,512]{2,1,0:T(8,128)(2,1)}), bf16[4,256,512]{2,1,0:T(8,128)(2,1)S(1)}, u32[]{:S(2)}, u32[]{:S(2)}) async-start(bf16[4,256,512]{2,1,0:T(8,128)(2,1)} %bitcast.162), calls=%async_computation.6 | async-start | bytes 2097152 | tf_op jit(solution)/shard_map/all_to_all | solution.py:912
  314.1 12.2 %collective-permute-start.70 = (bf16[64,2048]{1,0:T(8,128)(2,1)S(1)}, bf16[64,2048]{1,0:T(8,128)(2,1)S(1)}, u32[]{:S(2)}, u32[]{:S(2)}) collective-permute-start(bf16[64,2048]{1,0:T(8,128)(2,1)S(1)} %copy-done.71), channel_id=1, source_target_pairs={{0,2},{2,0},{1,3},{3,1},{4,6},{6,4},{5,7},{7,5},{8,10},{10,8},{9,1... | collective-permute-start | bytes 786440 | tf_op jit(solution)/shard_map/ppermute | solution.py:352
  315.5 11.3 %collective-permute-start.72 = (bf16[64,2048]{1,0:T(8,128)(2,1)S(1)}, bf16[64,2048]{1,0:T(8,128)(2,1)S(1)}, u32[]{:S(2)}, u32[]{:S(2)}) collective-permute-start(bf16[64,2048]{1,0:T(8,128)(2,1)S(1)} %copy-done.73), channel_id=1, source_target_pairs={{0,1},{1,0},{2,3},{3,2},{4,5},{5,4},{6,7},{7,6},{8,9},{9,8},{10,11... | collective-permute-start | bytes 786440 | tf_op jit(solution)/shard_map/ppermute | solution.py:352
  315.5 11.3 %collective-permute-start.73 = (bf16[64,2048]{1,0:T(8,128)(2,1)S(1)}, bf16[64,2048]{1,0:T(8,128)(2,1)S(1)}, u32[]{:S(2)}, u32[]{:S(2)}) collective-permute-start(bf16[64,2048]{1,0:T(8,128)(2,1)S(1)} %copy-done.71), channel_id=1, source_target_pairs={{0,1},{1,0},{2,3},{3,2},{4,5},{5,4},{6,7},{7,6},{8,9},{9,8},{10,11... | collective-permute-start | bytes 786440 | tf_op jit(solution)/shard_map/ppermute | solution.py:352
  339.5 29.6 %all-to-all-start.7 = ((bf16[4,256,512]{2,1,0:T(8,128)(2,1)}), bf16[4,256,512]{2,1,0:T(8,128)(2,1)}, u32[]{:S(2)}, u32[]{:S(2)}) async-start(bf16[4,256,512]{2,1,0:T(8,128)(2,1)} %bitcast.160), calls=%async_computation.7 | async-start | bytes 2097152 | tf_op jit(solution)/shard_map/all_to_all | solution.py:912
  357.1 40.0 %collective-permute-start.83 = (bf16[1024,128]{1,0:T(8,128)(2,1)S(1)}, bf16[1024,128]{1,0:T(8,128)(2,1)S(1)}, u32[]{:S(2)}, u32[]{:S(2)}) collective-permute-start(bf16[1024,128]{1,0:T(8,128)(2,1)S(1)} %get-tuple-element.1683), channel_id=1, source_target_pairs={{0,16},{16,0},{1,17},{17,1},{2,18},{18,2},{3,19},{19,3},{4,20},{20... | collective-permute-start | bytes 786440 | tf_op jit(solution)/shard_map/ppermute | solution.py:352
  376.5 22.1 %collective-permute-start.84 = (bf16[128,2048]{1,0:T(8,128)(2,1)S(1)}, bf16[128,2048]{1,0:T(8,128)(2,1)}, u32[]{:S(2)}, u32[]{:S(2)}) collective-permute-start(bf16[128,2048]{1,0:T(8,128)(2,1)S(1)} %add_convert_fusion.5), channel_id=1, source_target_pairs={{0,2},{2,0},{1,3},{3,1},{4,6},{6,4},{5,7},{7,5},{8,10},{10,8},{9,1... | collective-permute-start | bytes 1572872 | tf_op jit(solution)/shard_map/ppermute | solution.py:352
  382.3 16.9 %collective-permute-start.85 = (bf16[64,2048]{1,0:T(8,128)(2,1)}, bf16[64,2048]{1,0:T(8,128)(2,1)S(1)}, u32[]{:S(2)}, u32[]{:S(2)}) collective-permute-start(bf16[64,2048]{1,0:T(8,128)(2,1)} %add_convert_fusion.17), channel_id=1, source_target_pairs={{0,4},{4,0},{8,12},{12,8},{1,5},{5,1},{9,13},{13,9},{2,6},{6,2},{1... | collective-permute-start | bytes 786440 | tf_op jit(solution)/shard_map/ppermute | solution.py:352
  382.3 16.8 %collective-permute-start.86 = (bf16[64,2048]{1,0:T(8,128)(2,1)}, bf16[64,2048]{1,0:T(8,128)(2,1)}, u32[]{:S(2)}, u32[]{:S(2)}) collective-permute-start(bf16[64,2048]{1,0:T(8,128)(2,1)} %get-tuple-element.1792), channel_id=1, source_target_pairs={{0,2},{2,0},{1,3},{3,1},{4,6},{6,4},{5,7},{7,5},{8,10},{10,8},{9,1... | collective-permute-start | bytes 786440 | tf_op jit(solution)/shard_map/ppermute | solution.py:352
  385.4 40.8 %all-to-all-start.8 = ((bf16[4,256,512]{2,1,0:T(8,128)(2,1)}), bf16[4,256,512]{2,1,0:T(8,128)(2,1)}, u32[]{:S(2)}, u32[]{:S(2)}) async-start(bf16[4,256,512]{2,1,0:T(8,128)(2,1)} %bitcast.161), calls=%async_computation.8 | async-start | bytes 2097152 | tf_op jit(solution)/shard_map/all_to_all | solution.py:912
  397.1 13.2 %collective-permute-start.88 = (bf16[64,2048]{1,0:T(8,128)(2,1)}, bf16[64,2048]{1,0:T(8,128)(2,1)S(1)}, u32[]{:S(2)}, u32[]{:S(2)}) collective-permute-start(bf16[64,2048]{1,0:T(8,128)(2,1)} %get-tuple-element.1700), channel_id=1, source_target_pairs={{0,2},{2,0},{1,3},{3,1},{4,6},{6,4},{5,7},{7,5},{8,10},{10,8},{9,1... | collective-permute-start | bytes 786440 | tf_op jit(solution)/shard_map/ppermute | solution.py:352
  398.6 19.2 %collective-permute-start.89 = (bf16[128,2048]{1,0:T(8,128)(2,1)}, bf16[128,2048]{1,0:T(8,128)(2,1)}, u32[]{:S(2)}, u32[]{:S(2)}) collective-permute-start(bf16[128,2048]{1,0:T(8,128)(2,1)} %add_convert_fusion.4), channel_id=1, source_target_pairs={{0,2},{2,0},{1,3},{3,1},{4,6},{6,4},{5,7},{7,5},{8,10},{10,8},{9,1... | collective-permute-start | bytes 1572872 | tf_op jit(solution)/shard_map/ppermute | solution.py:352
  401.1 17.5 %collective-permute-start.92 = (bf16[64,2048]{1,0:T(8,128)(2,1)}, bf16[64,2048]{1,0:T(8,128)(2,1)}, u32[]{:S(2)}, u32[]{:S(2)}) collective-permute-start(bf16[64,2048]{1,0:T(8,128)(2,1)} %add_convert_fusion.12), channel_id=1, source_target_pairs={{0,4},{4,0},{8,12},{12,8},{1,5},{5,1},{9,13},{13,9},{2,6},{6,2},{1... | collective-permute-start | bytes 786440 | tf_op jit(solution)/shard_map/ppermute | solution.py:352
  405.3 20.9 %collective-permute-start.91 = (bf16[64,2048]{1,0:T(8,128)(2,1)}, bf16[64,2048]{1,0:T(8,128)(2,1)S(1)}, u32[]{:S(2)}, u32[]{:S(2)}) collective-permute-start(bf16[64,2048]{1,0:T(8,128)(2,1)} %get-tuple-element.1785), channel_id=1, source_target_pairs={{0,4},{4,0},{8,12},{12,8},{1,5},{5,1},{9,13},{13,9},{2,6},{6,2},{1... | collective-permute-start | bytes 786440 | tf_op jit(solution)/shard_map/ppermute | solution.py:352
  405.3 20.9 %collective-permute-start.90 = (bf16[64,2048]{1,0:T(8,128)(2,1)}, bf16[64,2048]{1,0:T(8,128)(2,1)S(1)}, u32[]{:S(2)}, u32[]{:S(2)}) collective-permute-start(bf16[64,2048]{1,0:T(8,128)(2,1)} %get-tuple-element.1786), channel_id=1, source_target_pairs={{0,8},{4,12},{8,0},{12,4},{1,9},{5,13},{9,1},{13,5},{2,10},{6,14},... | collective-permute-start | bytes 786440 | tf_op jit(solution)/shard_map/ppermute | solution.py:352
  410.3 27.5 %collective-permute-start.93 = (bf16[64,2048]{1,0:T(8,128)(2,1)}, bf16[64,2048]{1,0:T(8,128)(2,1)S(1)}, u32[]{:S(2)}, u32[]{:S(2)}) collective-permute-start(bf16[64,2048]{1,0:T(8,128)(2,1)} %get-tuple-element.1718), channel_id=1, source_target_pairs={{0,2},{2,0},{1,3},{3,1},{4,6},{6,4},{5,7},{7,5},{8,10},{10,8},{9,1... | collective-permute-start | bytes 786440 | tf_op jit(solution)/shard_map/ppermute | solution.py:352
  417.8 18.8 %collective-permute-start.96 = (bf16[1024,384]{1,0:T(8,128)(2,1)}, bf16[1024,384]{1,0:T(8,128)(2,1)S(1)}, u32[]{:S(2)}, u32[]{:S(2)}) collective-permute-start(bf16[1024,384]{1,0:T(8,128)(2,1)} %get-tuple-element.1723), channel_id=1, source_target_pairs={{0,16},{16,0},{1,17},{17,1},{2,18},{18,2},{3,19},{19,3},{4,20},{20... | collective-permute-start | bytes 2359304 | tf_op jit(solution)/shard_map/ppermute | solution.py:352
  429.5 12.4 %collective-permute-start.95 = (bf16[64,2048]{1,0:T(8,128)(2,1)S(1)}, bf16[64,2048]{1,0:T(8,128)(2,1)S(1)}, u32[]{:S(2)}, u32[]{:S(2)}) collective-permute-start(bf16[64,2048]{1,0:T(8,128)(2,1)S(1)} %get-tuple-element.1783), channel_id=1, source_target_pairs={{0,4},{4,0},{8,12},{12,8},{1,5},{5,1},{9,13},{13,9},{2,6},{6,2},{1... | collective-permute-start | bytes 786440 | tf_op jit(solution)/shard_map/ppermute | solution.py:352
  431.7 13.2 %collective-permute-start.94 = (bf16[64,2048]{1,0:T(8,128)(2,1)S(1)}, bf16[64,2048]{1,0:T(8,128)(2,1)S(1)}, u32[]{:S(2)}, u32[]{:S(2)}) collective-permute-start(bf16[64,2048]{1,0:T(8,128)(2,1)S(1)} %get-tuple-element.1784), channel_id=1, source_target_pairs={{0,8},{4,12},{8,0},{12,4},{1,9},{5,13},{9,1},{13,5},{2,10},{6,14},... | collective-permute-start | bytes 786440 | tf_op jit(solution)/shard_map/ppermute | solution.py:352
  445.0 13.9 %collective-permute-start.98 = (bf16[64,2048]{1,0:T(8,128)(2,1)S(1)}, bf16[64,2048]{1,0:T(8,128)(2,1)S(1)}, u32[]{:S(2)}, u32[]{:S(2)}) collective-permute-start(bf16[64,2048]{1,0:T(8,128)(2,1)S(1)} %maximum_select_fusion.2.refs_0_), channel_id=1, source_target_pairs={{0,1},{1,0},{2,3},{3,2},{4,5},{5,4},{6,7},{7,6},{8,9},{9,8},{10,11... | collective-permute-start | bytes 786440 | tf_op jit(solution)/shard_map/ppermute | solution.py:352
  445.0 13.8 %collective-permute-start.97 = (bf16[64,2048]{1,0:T(8,128)(2,1)S(1)}, bf16[64,2048]{1,0:T(8,128)(2,1)S(1)}, u32[]{:S(2)}, u32[]{:S(2)}) collective-permute-start(bf16[64,2048]{1,0:T(8,128)(2,1)S(1)} %maximum_select_fusion.2.refs_0_), channel_id=1, source_target_pairs={{0,2},{2,0},{1,3},{3,1},{4,6},{6,4},{5,7},{7,5},{8,10},{10,8},{9,1... | collective-permute-start | bytes 786440 | tf_op jit(solution)/shard_map/ppermute | solution.py:352
  448.7 29.7 %all-to-all-start.9 = ((bf16[4,256,512]{2,1,0:T(8,128)(2,1)}), bf16[4,256,512]{2,1,0:T(8,128)(2,1)S(1)}, u32[]{:S(2)}, u32[]{:S(2)}) async-start(bf16[4,256,512]{2,1,0:T(8,128)(2,1)} %bitcast.38), calls=%async_computation.9 | async-start | bytes 2097152 | tf_op jit(solution)/shard_map/all_to_all | solution.py:912
  (140 other events, 1167.9 us)
